TPU v7x, 32 devices: a whole 2x2x4 slice. The times are simulated.
32 devices in a mesh: section: 2 (over core), dp: 16 (over z, y, x).
Axes of the slice: x: 2, y: 2, z: 4, core: 2. Of those that a mesh axis runs over, the one named last changes fastest.
Arguments:
- boundary_in: bfloat16 [2, 2, 16, 512, 1024], P('section', None, 'dp'), may hold values from -6 to 6
- segments: int32 [2, 16, 512], P(None, 'dp'), may hold values from 0 to 7, never falling along the last dimension, each value on 1 to 128 neighbouring positions
- routed: int32 [2, 16, 64], P(None, 'dp'), may hold values from 0 to 511, as said below
- gain_attn: float32 [2, 1024], P('section', 'dp'), may hold values from 0.5 to 1.5
- w_qkv: float32 [2, 1024, 3072], P('section', 'dp'), may hold values from -0.1875 to 0.1875
- w_out: float32 [2, 1024, 1024], P('section', 'dp'), may hold values from -0.75 to 0.75
- gain_mlp: float32 [2, 1024], P('section', 'dp'), may hold values from 0.5 to 1.5
- w_up: float32 [2, 1024, 4096], P('section', 'dp'), may hold values from -0.1875 to 0.1875
- b_up: float32 [2, 4096], P('section', 'dp'), may hold values from -1.8 to 1.8
- w_down: float32 [2, 4096, 1024], P('section', 'dp'), may hold values from -0.09375 to 0.09375
- b_down: float32 [2, 1024], P('section', 'dp'), may hold values from -1.8 to 1.8
- router: float32 [1024], P(('section', 'dp')), may hold values from -0.1875 to 0.1875
Outputs:
- boundary_out: bfloat16 [2, 2, 16, 512, 1024], P('section', None, 'dp')
- grad_gain_attn: float32 [2, 1024], P('section', 'dp')
- grad_w_qkv: float32 [2, 1024, 3072], P('section', 'dp')
- grad_w_out: float32 [2, 1024, 1024], P('section', 'dp')
- grad_gain_mlp: float32 [2, 1024], P('section', 'dp')
- grad_w_up: float32 [2, 1024, 4096], P('section', 'dp')
- grad_b_up: float32 [2, 4096], P('section', 'dp')
- grad_w_down: float32 [2, 4096, 1024], P('section', 'dp')
- grad_b_down: float32 [2, 1024], P('section', 'dp')
- grad_router: float32 [1024], P(('section', 'dp'))
Inputs may be any that keep to these rules, and one draw needn't show every extreme that they name: `routed`: each row holds 64 distinct positions of its sequence in increasing order.
All inputs are finite; a program needn't handle non-finite values.
Results may differ from a plain program's by a relative error of at most 0.013.
The roundings to bfloat16 on the way count: a program that leaves them out, or rounds other values in their place, can miss the bound.
Values may be sent and summed in bfloat16 or wider, within the bound.
No kernel may reach another device: no remote copies, remote signals or barrier semaphores. Data moves between devices by JAX's collectives and lax.ppermute only.
A program may use at most 576 MiB of HBM per device.

v0:
```python
import jax
import jax.numpy as jnp
from jax import lax
from jax.sharding import PartitionSpec as P

D = 1024
HEADS = 16
HEAD_DIM = 64
FF = 4096


epsilon = 1e-06
masked_score = -1e30
block_rows = 512
root_half = 0.7071067811865476
inverse_root_two_pi = 0.3989422804014327


def passed_along(array, axis, by):
    devices = lax.axis_size(axis)
    pairs = [(i, i + by) for i in range(devices) if 0 <= i + by < devices]
    return lax.ppermute(array, axis, pairs)


def shortened(array):
    return jax.tree.map(lambda a: a.astype(jnp.bfloat16) if a.dtype == jnp.float32 else a, array)


def over_rows(left_side, right_side):
    return lax.dot_general(
        left_side, right_side, (((0,), (0,)), ((), ())), preferred_element_type=jnp.float32
    )


def against(left_side, right_side):
    return lax.dot_general(
        left_side, right_side, (((1,), (1,)), ((), ())), preferred_element_type=jnp.float32
    )


def gelu_value(inputs):
    return 0.5 * inputs * (1.0 + lax.erf(inputs * root_half))


def gelu_slope(inputs):
    return (
        0.5 * (1.0 + lax.erf(inputs * root_half))
        + inputs * jnp.exp(-0.5 * inputs * inputs) * inverse_root_two_pi
    )


def split_heads(qkv):
    row_count = qkv.shape[0]
    width_all = HEADS * HEAD_DIM
    queries = qkv[:, :width_all].reshape(row_count, HEADS, HEAD_DIM)
    key_heads = qkv[:, width_all : 2 * width_all].reshape(row_count, HEADS, HEAD_DIM)
    value_heads = qkv[:, 2 * width_all :].reshape(row_count, HEADS, HEAD_DIM)
    return (queries, key_heads, value_heads)


def score_block(query_rows, key_heads, segment_ids, positions, row_start, row_count):
    scores = jnp.einsum(
        "qhd,khd->hqk", query_rows, key_heads, preferred_element_type=jnp.float32
    ) * HEAD_DIM ** (-0.5)
    same_doc = segment_ids[row_start : row_start + row_count, None] == segment_ids[None, :]
    earlier = positions[row_start : row_start + row_count, None] >= positions[None, :]
    return jnp.where((same_doc & earlier)[None], scores, masked_score)


def attend_forward(qkv, segment_ids, positions):
    queries, key_heads, value_heads = split_heads(qkv)
    row_count = qkv.shape[0]
    step_rows = min(row_count, block_rows)
    scores = score_block(queries, key_heads, segment_ids, positions, 0, step_rows)
    row_max = jnp.max(scores, axis=-1, keepdims=True)
    exponent = jnp.exp(scores - row_max)
    row_total = jnp.sum(exponent, axis=-1, keepdims=True)
    weights = (exponent / row_total).astype(jnp.bfloat16)
    outputs = [jnp.einsum("hqk,khd->qhd", weights, value_heads, preferred_element_type=jnp.float32)]
    totals = [row_max[..., 0] + jnp.log(row_total[..., 0])]
    attended = (
        jnp.concatenate(outputs, axis=0).reshape(row_count, HEADS * HEAD_DIM).astype(jnp.bfloat16)
    )
    return (attended, jnp.concatenate(totals, axis=1))


def attend_backward(qkv, segment_ids, positions, totals, grad_attended):
    queries, key_heads, value_heads = split_heads(qkv)
    row_count = qkv.shape[0]
    step_rows = min(row_count, block_rows)
    score_scale = HEAD_DIM ** (-0.5)
    grad_heads = grad_attended.reshape(row_count, HEADS, HEAD_DIM)
    grad_keys = jnp.zeros((row_count, HEADS, HEAD_DIM), jnp.float32)
    grad_values = jnp.zeros((row_count, HEADS, HEAD_DIM), jnp.float32)
    scores = score_block(queries, key_heads, segment_ids, positions, 0, step_rows)
    probs = jnp.exp(scores - totals[:, 0:step_rows, None])
    grad_probs = jnp.einsum(
        "qhd,khd->hqk", grad_heads, value_heads, preferred_element_type=jnp.float32
    )
    grad_values = grad_values + jnp.einsum(
        "hqk,qhd->khd", probs.astype(jnp.bfloat16), grad_heads, preferred_element_type=jnp.float32
    )
    row_inner = jnp.sum(grad_probs * probs, axis=-1, keepdims=True)
    grad_scores = (probs * (grad_probs - row_inner)).astype(jnp.bfloat16)
    grad_queries = [
        jnp.einsum("hqk,khd->qhd", grad_scores, key_heads, preferred_element_type=jnp.float32)
        * score_scale
    ]
    grad_keys = (
        grad_keys
        + jnp.einsum("hqk,qhd->khd", grad_scores, queries, preferred_element_type=jnp.float32)
        * score_scale
    )
    width_all = HEADS * HEAD_DIM
    joined = jnp.concatenate(
        [
            jnp.concatenate(grad_queries, axis=0).reshape(row_count, width_all),
            grad_keys.reshape(row_count, width_all),
            grad_values.reshape(row_count, width_all),
        ],
        axis=1,
    )
    return joined.astype(jnp.bfloat16)


def block_forward(residual, segment_ids, positions, params):
    gain_attn, w_qkv, w_out, gain_mlp, w_up, b_up, w_down, b_down = params
    inv_attn = lax.rsqrt(jnp.mean(residual * residual, axis=-1, keepdims=True) + epsilon)
    normed = (residual * inv_attn * gain_attn.astype(jnp.float32)).astype(jnp.bfloat16)
    qkv = jnp.dot(normed, w_qkv, preferred_element_type=jnp.float32).astype(jnp.bfloat16)
    attended, totals = attend_forward(qkv, segment_ids, positions)
    mixed_attn = jnp.dot(attended, w_out, preferred_element_type=jnp.float32)
    hidden = residual + mixed_attn
    inv_mlp = lax.rsqrt(jnp.mean(hidden * hidden, axis=-1, keepdims=True) + epsilon)
    normed_mlp = (hidden * inv_mlp * gain_mlp.astype(jnp.float32)).astype(jnp.bfloat16)
    up_proj = jnp.dot(normed_mlp, w_up, preferred_element_type=jnp.float32) + b_up.astype(
        jnp.float32
    )
    active = gelu_value(up_proj).astype(jnp.bfloat16)
    down_proj = jnp.dot(active, w_down, preferred_element_type=jnp.float32) + b_down.astype(
        jnp.float32
    )
    stored = (normed, qkv, totals, attended, hidden, inv_mlp, normed_mlp, up_proj, active)
    return (mixed_attn, down_proj, stored)


def block_backward(residual, segment_ids, positions, params, stored, grad_branch, grad_direct):
    gain_attn, w_qkv, w_out, gain_mlp, w_up, b_up, w_down, b_down = params
    normed, qkv, totals, attended, hidden, inv_mlp, normed_mlp, up_proj, active = stored
    grad_down = grad_branch.astype(jnp.bfloat16)
    grad_w_down = over_rows(active, grad_down)
    grad_b_down = jnp.sum(grad_down.astype(jnp.float32), axis=0)
    grad_active = against(grad_down, w_down)
    grad_up = (grad_active * gelu_slope(up_proj)).astype(jnp.bfloat16)
    grad_b_up = jnp.sum(grad_up.astype(jnp.float32), axis=0)
    grad_w_up = over_rows(normed_mlp, grad_up)
    grad_normed_mlp = against(grad_up, w_up)
    unit_mlp = hidden * inv_mlp
    grad_gain_mlp = jnp.sum(grad_normed_mlp * unit_mlp, axis=0)
    scaled_mlp = grad_normed_mlp * gain_mlp.astype(jnp.float32)
    grad_hidden = inv_mlp * (
        scaled_mlp - unit_mlp * jnp.mean(scaled_mlp * unit_mlp, axis=-1, keepdims=True)
    )
    grad_mixed = (grad_branch + grad_hidden).astype(jnp.bfloat16)
    grad_w_out = over_rows(attended, grad_mixed)
    grad_attended = against(grad_mixed, w_out).astype(jnp.bfloat16)
    grad_qkv = attend_backward(qkv, segment_ids, positions, totals, grad_attended)
    grad_w_qkv = over_rows(normed, grad_qkv)
    grad_normed = against(grad_qkv, w_qkv)
    inv_attn = lax.rsqrt(jnp.mean(residual * residual, axis=-1, keepdims=True) + epsilon)
    unit_attn = residual * inv_attn
    grad_gain_attn = jnp.sum(grad_normed * unit_attn, axis=0)
    scaled_attn = grad_normed * gain_attn.astype(jnp.float32)
    grad_input = (
        grad_direct
        + grad_hidden
        + inv_attn
        * (scaled_attn - unit_attn * jnp.mean(scaled_attn * unit_attn, axis=-1, keepdims=True))
    )
    gradients = (
        grad_gain_attn,
        grad_w_qkv,
        grad_w_out,
        grad_gain_mlp,
        grad_w_up,
        grad_b_up,
        grad_w_down,
        grad_b_down,
    )
    return (grad_input, gradients)


def dense_forward(residual_b, segment_ids, params):
    residual = residual_b.astype(jnp.float32)
    positions = jnp.arange(residual.shape[0], dtype=jnp.int32)
    mixed_attn, down_proj, stored = block_forward(residual, segment_ids, positions, params)
    return ((stored[4] + down_proj).astype(jnp.bfloat16), stored)


def dense_backward(residual_b, segment_ids, params, stored, grad_b):
    residual = residual_b.astype(jnp.float32)
    positions = jnp.arange(residual.shape[0], dtype=jnp.int32)
    grad_out = grad_b.astype(jnp.float32)
    grad_input, gradients = block_backward(
        residual, segment_ids, positions, params, stored, grad_out, grad_out
    )
    return (grad_input.astype(jnp.bfloat16), gradients)


def routed_pass(residual_b, grad_out_b, segment_ids, picked, params, router_full):
    residual = residual_b.astype(jnp.float32)
    chosen_b = jnp.take(residual_b, picked, axis=0)
    chosen = chosen_b.astype(jnp.float32)
    chosen_ids = jnp.take(segment_ids, picked, axis=0)
    logits = jnp.dot(chosen_b, router_full, preferred_element_type=jnp.float32)
    router_weight = jax.nn.sigmoid(logits)
    mixed_attn, down_proj, stored = block_forward(chosen, chosen_ids, picked, params)
    change = mixed_attn + down_proj
    output = residual.at[picked].add(router_weight[:, None] * change)
    grad_out = grad_out_b.astype(jnp.float32)
    grad_chosen = jnp.take(grad_out, picked, axis=0)
    grad_logits = jnp.sum(grad_chosen * change, axis=-1) * router_weight * (1.0 - router_weight)
    grad_router = jnp.dot(grad_logits, chosen, precision=lax.Precision.HIGHEST)
    grad_rows, gradients = block_backward(
        chosen, chosen_ids, picked, params, stored, router_weight[:, None] * grad_chosen, 0.0
    )
    grad_rows = grad_rows + grad_logits[:, None] * router_full.astype(jnp.float32)[None, :]
    grad_input = grad_out.at[picked].add(grad_rows)
    return (output.astype(jnp.bfloat16), grad_input.astype(jnp.bfloat16), gradients, grad_router)


def zero_gradients():
    return (
        jnp.zeros((1, D), jnp.float32),
        jnp.zeros((1, D, 3 * D), jnp.float32),
        jnp.zeros((1, D, D), jnp.float32),
        jnp.zeros((1, D), jnp.float32),
        jnp.zeros((1, D, FF), jnp.float32),
        jnp.zeros((1, FF), jnp.float32),
        jnp.zeros((1, FF, D), jnp.float32),
        jnp.zeros((1, D), jnp.float32),
    )


def empty_stored(local_count, length):
    return (
        jnp.zeros((local_count, length, D), jnp.bfloat16),
        jnp.zeros((local_count, length, 3 * D), jnp.bfloat16),
        jnp.zeros((local_count, HEADS, length), jnp.float32),
        jnp.zeros((local_count, length, D), jnp.bfloat16),
        jnp.zeros((local_count, length, D), jnp.float32),
        jnp.zeros((local_count, length, 1), jnp.float32),
        jnp.zeros((local_count, length, D), jnp.bfloat16),
        jnp.zeros((local_count, length, FF), jnp.float32),
        jnp.zeros((local_count, length, FF), jnp.bfloat16),
    )


def add_all(first_set, second_set):
    return tuple((left_part + right_part for left_part, right_part in zip(first_set, second_set)))


def lifted(gradients):
    return tuple((grad_piece[None] for grad_piece in gradients))


def stack_all(groups):
    return tuple(
        (
            jnp.stack([group_item[member] for group_item in groups])
            for member in range(len(groups[0]))
        )
    )


def shards(
    boundary_in,
    segments,
    routed,
    gain_attn,
    w_qkv,
    w_out,
    gain_mlp,
    w_up,
    b_up,
    w_down,
    b_down,
    router,
):
    is_first = lax.axis_index("section") == 0
    gathered = (
        lax.all_gather(gain_attn.astype(jnp.bfloat16), "dp", axis=1, tiled=True),
        lax.all_gather(w_qkv.astype(jnp.bfloat16), "dp", axis=1, tiled=True),
        lax.all_gather(w_out.astype(jnp.bfloat16), "dp", axis=1, tiled=True),
        lax.all_gather(gain_mlp.astype(jnp.bfloat16), "dp", axis=1, tiled=True),
        lax.all_gather(w_up.astype(jnp.bfloat16), "dp", axis=1, tiled=True),
        lax.all_gather(b_up.astype(jnp.bfloat16), "dp", axis=1, tiled=True),
        lax.all_gather(w_down.astype(jnp.bfloat16), "dp", axis=1, tiled=True),
        lax.all_gather(b_down.astype(jnp.bfloat16), "dp", axis=1, tiled=True),
    )
    params = tuple((gathered_one[0] for gathered_one in gathered))
    router_full = lax.all_gather(router.astype(jnp.bfloat16), ("section", "dp"), axis=0, tiled=True)
    micro_count = boundary_in.shape[1]
    local_count = boundary_in.shape[2]
    length = boundary_in.shape[3]
    silent = jnp.zeros((local_count, length, D), jnp.bfloat16)
    no_router = jnp.zeros((D,), jnp.float32)
    received = []
    returned = []
    stored_list = []
    produced = []
    grad_total = zero_gradients()
    grad_shards = None
    router_total = no_router
    for tick_index in range(micro_count + 2):

        def first_section():
            if tick_index < micro_count:
                results = [
                    dense_forward(boundary_in[0, tick_index, 0], segments[tick_index, 0], params)
                ]
                send_next = jnp.stack([entry[0] for entry in results])
                stored_new = stack_all([entry[1] for entry in results])
            else:
                send_next = silent
                stored_new = empty_stored(local_count, length)
            if tick_index >= 2:
                micro_index = tick_index - 2
                gradients = zero_gradients()
                stored_one = tuple((part_item[0] for part_item in stored_list[micro_index]))
                grad_input, grad_set = dense_backward(
                    boundary_in[0, micro_index, 0],
                    segments[micro_index, 0],
                    params,
                    stored_one,
                    returned[micro_index][0],
                )
                rows_back = [grad_input]
                gradients = add_all(gradients, lifted(grad_set))
                kept_rows = jnp.stack(rows_back)
            else:
                kept_rows = silent
                gradients = zero_gradients()
            return (send_next, silent, kept_rows, gradients, no_router, stored_new)

        def second_section():
            if 1 <= tick_index <= micro_count:
                micro_index = tick_index - 1
                gradients = zero_gradients()
                out_rows, back_rows, grad_set, grad_router = routed_pass(
                    received[micro_index][0],
                    boundary_in[0, micro_index, 0],
                    segments[micro_index, 0],
                    routed[micro_index, 0],
                    params,
                    router_full,
                )
                outputs = [out_rows]
                backs = [back_rows]
                gradients = add_all(gradients, lifted(grad_set))
                return (
                    silent,
                    jnp.stack(backs),
                    jnp.stack(outputs),
                    gradients,
                    grad_router,
                    empty_stored(local_count, length),
                )
            return (
                silent,
                silent,
                silent,
                zero_gradients(),
                no_router,
                empty_stored(local_count, length),
            )

        outcome = lax.cond(is_first, first_section, second_section)
        send_next, send_back, kept_rows, gradients, grad_router, stored_new = outcome
        if tick_index < micro_count:
            stored_list.append(stored_new)
            received.append(passed_along(send_next, "section", 1))
        if 1 <= tick_index <= micro_count:
            returned.append(
                passed_along(shortened(send_back), "section", -1).astype(send_back.dtype)
            )
        produced.append(kept_rows)
        router_total = router_total + grad_router
        grad_total = add_all(grad_total, gradients)
    grad_shards = (
        lax.psum_scatter(grad_total[0], "dp", scatter_dimension=1, tiled=True),
        lax.psum_scatter(grad_total[1], "dp", scatter_dimension=1, tiled=True),
        lax.psum_scatter(grad_total[2], "dp", scatter_dimension=1, tiled=True),
        lax.psum_scatter(grad_total[3], "dp", scatter_dimension=1, tiled=True),
        lax.psum_scatter(grad_total[4], "dp", scatter_dimension=1, tiled=True),
        lax.psum_scatter(grad_total[5], "dp", scatter_dimension=1, tiled=True),
        lax.psum_scatter(grad_total[6], "dp", scatter_dimension=1, tiled=True),
        lax.psum_scatter(grad_total[7], "dp", scatter_dimension=1, tiled=True),
    )
    finals = [
        jnp.where(is_first, produced[micro_index + 2], produced[micro_index + 1])
        for micro_index in range(micro_count)
    ]
    boundary_out = jnp.stack(finals)[None]
    router_shard = lax.psum_scatter(
        router_total, ("section", "dp"), scatter_dimension=0, tiled=True
    )
    return (boundary_out,) + tuple(grad_shards) + (router_shard,)


def solution(mesh):
    in_specs = (
        P("section", None, "dp", None, None),
        P(None, "dp", None),
        P(None, "dp", None),
        P("section", "dp"),
        P("section", "dp", None),
        P("section", "dp", None),
        P("section", "dp"),
        P("section", "dp", None),
        P("section", "dp"),
        P("section", "dp", None),
        P("section", "dp"),
        P(("section", "dp")),
    )
    out_specs = (
        P("section", None, "dp", None, None),
        P("section", "dp"),
        P("section", "dp", None),
        P("section", "dp", None),
        P("section", "dp"),
        P("section", "dp", None),
        P("section", "dp"),
        P("section", "dp", None),
        P("section", "dp"),
        P(("section", "dp")),
    )
    return jax.shard_map(shards, mesh=mesh, in_specs=in_specs, out_specs=out_specs, check_vma=False)
```

profile of v0, /device:TPU:0, one launch (start us, length us, event | category | flops | bytes accessed | tf_op | source)
XLA Modules:
  0.0 2326.7 jit_solution(1804666336624686540)
XLA Ops:
  16.3 42.5 %all_gather.32 = bf16[1,4096]{1,0:T(2,128)(2,1)S(1)} all-gather(bf16[1,256]{1,0:T(2,128)(2,1)S(1)} %convert_element_type.469), channel_id=1, replica_groups=mesh['section'=2,'dp'=16] {'dp'}, dimensions={1}, use_global_device_ids=true | all-gather | bytes 8704 | tf_op jit(solution)/shard_map/all_gather | solution.py:297
  58.9 37.6 %all-reduce.5 = (bf16[1024]{0:T(1024)(128)(2,1)S(1)}, bf16[1024]{0:T(1024)(128)(2,1)S(1)}, bf16[1024]{0:T(1024)(128)(2,1)S(1)}) all-reduce(bf16[1024]{0:T(1024)(128)(2,1)S(1)} %dynamic-update-slice, bf16[1024]{0:T(1024)(128)(2,1)S(1)} %dynamic-update-slice.1, ...), channel_id=1, replica_groups=mesh['section'=2,'dp'=16] {'dp'}, use_global_device_ids=true, to_apply=%add | all-reduce | flops 3072 | bytes 12288 | tf_op jit(solution)/shard_map/squeeze | solution.py:301
  96.6 75.2 %all-gather.5.cloned.1.call-done = bf16[1,1024,3072]{2,1,0:T(8,128)(2,1)} async-done(((bf16[1,64,3072]{2,1,0:T(8,128)(2,1)}), bf16[1,1024,3072]{2,1,0:T(8,128)(2,1)}) %all-gather.5.cloned.1.call-update) | async-done | bytes 6291472 | tf_op jit(solution)/shard_map/all_gather | solution.py:293
  171.8 114.5 %all-gather.9.cloned.1.call-done = bf16[1,1024,4096]{2,1,0:T(8,128)(2,1)} async-done(((bf16[1,64,4096]{2,1,0:T(8,128)(2,1)}), bf16[1,1024,4096]{2,1,0:T(8,128)(2,1)}) %all-gather.9.cloned.1.call-update) | async-done | bytes 8388624 | tf_op jit(solution)/shard_map/all_gather | solution.py:296
  286.3 114.3 %all-gather.11.cloned.1.call-done = bf16[1,4096,1024]{2,1,0:T(8,128)(2,1)} async-done(((bf16[1,256,1024]{2,1,0:T(8,128)(2,1)}), bf16[1,4096,1024]{2,1,0:T(8,128)(2,1)}) %all-gather.11.cloned.1.call-update) | async-done | bytes 8388624 | tf_op jit(solution)/shard_map/all_gather | solution.py:298
  400.5 74.3 %conditional.4 = (bf16[1,512,1024]{2,1,0:T(8,128)(2,1)}, bf16[1,512,1024]{2,1,0:T(8,128)(2,1)}, bf16[1,512,3072]{2,1,0:T(8,128)(2,1)}, f32[1,16,512]{2,1,0:T(8,1...) conditional(s32[]{:T(128)} %convert_element_type.463, () %tuple.54, ...), branch_computations={%region_0.0_spmd, %region_1.6_spmd} | conditional | flops 14037024768 | bytes 168165632 | solution.py:378
  477.1 38.4 %all-reduce.3 = bf16[1024]{0:T(1024)(128)(2,1)} all-reduce(bf16[1024]{0:T(1024)(128)(2,1)S(1)} %dynamic-update-slice.3), channel_id=1, replica_groups=mesh['section'=2,'dp'=16] {'section','dp'}, use_global_device_ids=true, to_apply=%add.3 | all-reduce | flops 1024 | bytes 4096
  515.6 113.8 %conditional.5 = (bf16[1,512,1024]{2,1,0:T(8,128)(2,1)}, bf16[1,512,1024]{2,1,0:T(8,128)(2,1)}, bf16[1,512,1024]{2,1,0:T(8,128)(2,1)}, f32[1,1024]{1,0:T(1,128)}...) conditional(s32[]{:T(128)} %convert_element_type.463, ...), branch_computations={%region_6.24_spmd, %region_21.29_spmd} | conditional | flops 14037024768 | bytes 238467552 | solution.py:378
  629.4 31.3 %collective-permute-start.1 = (bf16[1,512,1024]{2,1,0:T(8,128)(2,1)}, bf16[1,512,1024]{2,1,0:T(8,128)(2,1)S(1)}, u32[]{:S(2)}, u32[]{:S(2)}) collective-permute-start(bf16[1,512,1024]{2,1,0:T(8,128)(2,1)} %get-tuple-element.398), channel_id=1, source_target_pairs={{0,16},{1,17},{2,18},{3,19},{4,20},{5,21},{6,22},{7,23},{8,24},{9,... | collective-permute-start | bytes 3145736 | tf_op jit(solution)/shard_map/ppermute | solution.py:22
  665.6 169.8 %conditional.6 = (bf16[1,512,1024]{2,1,0:T(8,128)(2,1)}, bf16[1,512,1024]{2,1,0:T(8,128)(2,1)}, f32[1,1024]{1,0:T(1,128)}, f32[1,1024,3072]{2,1,0:T(8,128)}, f32...) conditional(s32[]{:T(128)} %convert_element_type.463, ...), branch_computations={%region_26.44_spmd, %region_41.53_spmd} | conditional | flops 28557690880 | bytes 558572096 | solution.py:378
  745.0 17.5 copy.163
  840.3 161.1 %conditional.7 = (bf16[1,512,1024]{2,1,0:T(8,128)(2,1)}, f32[1,1024]{1,0:T(1,128)S(1)}, f32[1,1024]{1,0:T(1,128)S(1)}, f32[1,4096]{1,0:T(1,128)S(1)}, f32[1,4096...) conditional(s32[]{:T(128)} %convert_element_type.463, () %tuple.59, ...), branch_computations={%region_50.54_spmd, %region_51.63_spmd} | conditional | flops 28557690880 | bytes 557621888 | solution.py:378
  913.6 17.5 copy.243
  1018.4 19.1 add_add_fusion.2
  1037.5 23.6 %add_add_fusion.1 = f32[1,1024,4096]{2,1,0:T(8,128)} fusion(f32[1,1024,4096]{2,1,0:T(8,128)} %get-tuple-element.688, f32[1,1024,4096]{2,1,0:T(8,128)} %get-tuple-element.436, f32[1,1024,4096]{2,1,0:T(8,128)} %get-tuple-element.435, f32[]{:T(128)} %get-tuple-element.422), kind=kLoop, calls=%fused_computation.421 | loop fusion | flops 12582912 | bytes 67108864 | tf_op jit(solution)/shard_map/add | solution.py:260
  1061.2 23.9 %add_add_fusion = f32[1,4096,1024]{2,1,0:T(8,128)} fusion(f32[1,4096,1024]{2,1,0:T(8,128)} %get-tuple-element.443, f32[1,4096,1024]{2,1,0:T(8,128)} %get-tuple-element.442, f32[1,4096,1024]{2,1,0:T(8,128)} %get-tuple-element.441, f32[]{:T(128)} %get-tuple-element.422), kind=kLoop, calls=%fused_computation.420 | loop fusion | flops 12582912 | bytes 67108864 | tf_op jit(solution)/shard_map/add | solution.py:260
  1085.8 40.2 %all-reduce.4 = f32[1024]{0:T(1024)S(1)} all-reduce(f32[1024]{0:T(1024)S(1)} %add.483), channel_id=10, replica_groups=mesh['section'=2,'dp'=16] {'section','dp'}, use_global_device_ids=true, to_apply=%region_68.72.clone | all-reduce | flops 1024 | bytes 8192
  1131.1 24.7 %reduce-scatter.31.cloned.1.call-done = f32[64,1]{1,0:T(8,128)} async-done(((f32[1024,1]{1,0:T(8,128)}), f32[64,1]{1,0:T(8,128)}) %reduce-scatter.31.cloned.1.call-update) | async-done | bytes 272
  1157.1 73.9 %reduce-scatter.27.cloned.1.call-done = f32[64,1]{1,0:T(8,128)} async-done(((f32[1024,1]{1,0:T(8,128)}), f32[64,1]{1,0:T(8,128)}) %reduce-scatter.27.cloned.1.call-update) | async-done | bytes 272
  1232.3 78.0 %reduce-scatter.29.cloned.1.call-done = f32[256,1]{1,0:T(8,128)} async-done(((f32[4096,1]{1,0:T(8,128)}), f32[256,1]{1,0:T(8,128)}) %reduce-scatter.29.cloned.1.call-update) | async-done | bytes 1040
  1311.9 93.6 %reduce-scatter.19.cloned.1.call-done = f32[1,64,1024]{2,1,0:T(8,128)} async-done(((f32[1,1024,1024]{2,1,0:T(8,128)}), f32[1,64,1024]{2,1,0:T(8,128)}) %reduce-scatter.19.cloned.1.call-update) | async-done | bytes 262160 | tf_op jit(solution)/shard_map/reduce_scatter | solution.py:393
  1405.4 210.6 %reduce-scatter.17.cloned.1.call-done = f32[1,64,3072]{2,1,0:T(8,128)} async-done(((f32[1,1024,3072]{2,1,0:T(8,128)}), f32[1,64,3072]{2,1,0:T(8,128)}) %reduce-scatter.17.cloned.1.call-update) | async-done | bytes 786448 | tf_op jit(solution)/shard_map/reduce_scatter | solution.py:392
  1616.1 348.9 %reduce-scatter.21.cloned.1.call-done = f32[1,64,4096]{2,1,0:T(8,128)} async-done(((f32[1,1024,4096]{2,1,0:T(8,128)}), f32[1,64,4096]{2,1,0:T(8,128)}) %reduce-scatter.21.cloned.1.call-update) | async-done | bytes 1048592 | tf_op jit(solution)/shard_map/reduce_scatter | solution.py:395
  1965.0 354.8 %reduce-scatter.23.cloned.1.call-done = f32[1,256,1024]{2,1,0:T(8,128)} async-done(((f32[1,4096,1024]{2,1,0:T(8,128)}), f32[1,256,1024]{2,1,0:T(8,128)}) %reduce-scatter.23.cloned.1.call-update) | async-done | bytes 1048592 | tf_op jit(solution)/shard_map/reduce_scatter | solution.py:397
  (313 shorter events, 508.8 us)
Async XLA Ops:
  7.2 393.3 %copy-start.63 = (s32[2,1,512]{2,1,0:T(1,128)S(1)}, s32[2,1,512]{2,1,0:T(1,128)}, u32[]{:S(2)}) copy-start(s32[2,1,512]{2,1,0:T(1,128)} %param.27) | copy-start | bytes 12292
  7.3 393.3 %copy-start.2 = (bf16[1,2,1,512,1024]{4,3,2,1,0:T(8,128)(2,1)S(1)}, bf16[1,2,1,512,1024]{4,3,2,1,0:T(8,128)(2,1)}, u32[]{:S(2)}) copy-start(bf16[1,2,1,512,1024]{4,3,2,1,0:T(8,128)(2,1)} %param.26) | copy-start | bytes 6291460
  7.3 89.3 %all-gather.7.cloned.1.call-start = ((), (), s32[]{:S(2)}) async-start(), calls=%async_computation.9 | async-start | bytes 2228224 | tf_op jit(solution)/shard_map/all_gather | solution.py:294
  9.1 162.7 %all-gather.5.cloned.1.call-start = ((), (), s32[]{:S(2)}) async-start(), calls=%async_computation.8 | async-start | bytes 6684672 | tf_op jit(solution)/shard_map/all_gather | solution.py:293
  11.1 275.2 %all-gather.9.cloned.1.call-start = ((), (), s32[]{:S(2)}) async-start(), calls=%async_computation.10 | async-start | bytes 8912896 | tf_op jit(solution)/shard_map/all_gather | solution.py:296
  13.3 387.3 %all-gather.11.cloned.1.call-start = ((), (), s32[]{:S(2)}) async-start(), calls=%async_computation.11 | async-start | bytes 8912896 | tf_op jit(solution)/shard_map/all_gather | solution.py:298
  14.2 1115.5 %reduce-scatter.25.cloned.1.call-start = ((), (), s32[]{:S(2)}) async-start(), calls=%async_computation.16 | async-start | bytes 557056
  58.9 456.6 %copy-start.58 = (bf16[4096]{0:T(1024)(128)(2,1)}, bf16[4096]{0:T(1024)(128)(2,1)S(1)}, u32[]{:S(2)}) copy-start(bf16[4096]{0:T(1024)(128)(2,1)S(1)} %reduce) | copy-start | bytes 24580
  96.6 419.0 %copy-start.60 = (bf16[1024]{0:T(1024)(128)(2,1)}, bf16[1024]{0:T(1024)(128)(2,1)S(1)}, u32[]{:S(2)}) copy-start(bf16[1024]{0:T(1024)(128)(2,1)S(1)} %get-tuple-element.708) | copy-start | bytes 6148
  96.6 419.0 %copy-start.64 = (bf16[1024]{0:T(1024)(128)(2,1)}, bf16[1024]{0:T(1024)(128)(2,1)S(1)}, u32[]{:S(2)}) copy-start(bf16[1024]{0:T(1024)(128)(2,1)S(1)} %get-tuple-element.709) | copy-start | bytes 6148
  96.6 569.0 %copy-start.59 = (bf16[1024]{0:T(1024)(128)(2,1)}, bf16[1024]{0:T(1024)(128)(2,1)S(1)}, u32[]{:S(2)}) copy-start(bf16[1024]{0:T(1024)(128)(2,1)S(1)} %get-tuple-element.707) | copy-start | bytes 6148
  474.9 40.6 %collective-permute-start = (bf16[1,512,1024]{2,1,0:T(8,128)(2,1)}, bf16[1,512,1024]{2,1,0:T(8,128)(2,1)S(1)}, u32[]{:S(2)}, u32[]{:S(2)}) collective-permute-start(bf16[1,512,1024]{2,1,0:T(8,128)(2,1)} %get-tuple-element.397), channel_id=1, source_target_pairs={{0,16},{1,17},{2,18},{3,19},{4,20},{5,21},{6,22},{7,23},{8,24},{9,... | collective-permute-start | bytes 3145736 | tf_op jit(solution)/shard_map/ppermute | solution.py:22
  629.4 33.7 %collective-permute-start.1 = (bf16[1,512,1024]{2,1,0:T(8,128)(2,1)}, bf16[1,512,1024]{2,1,0:T(8,128)(2,1)S(1)}, u32[]{:S(2)}, u32[]{:S(2)}) collective-permute-start(bf16[1,512,1024]{2,1,0:T(8,128)(2,1)} %get-tuple-element.398), channel_id=1, source_target_pairs={{0,16},{1,17},{2,18},{3,19},{4,20},{5,21},{6,22},{7,23},{8,24},{9,... | collective-permute-start | bytes 3145736 | tf_op jit(solution)/shard_map/ppermute | solution.py:22
  660.7 4.9 collective-permute-start.2
  835.4 4.9 collective-permute-start.3
  840.3 161.7 %copy-start.79 = (f32[1,1024]{1,0:T(1,128)S(1)}, f32[1,1024]{1,0:T(1,128)}, u32[]{:S(2)}) copy-start(f32[1,1024]{1,0:T(1,128)} %get-tuple-element.423) | copy-start | bytes 12292
  840.3 161.7 %copy-start.80 = (f32[1,1024]{1,0:T(1,128)S(1)}, f32[1,1024]{1,0:T(1,128)}, u32[]{:S(2)}) copy-start(f32[1,1024]{1,0:T(1,128)} %get-tuple-element.424) | copy-start | bytes 12292
  1003.8 152.0 %reduce-scatter.31.cloned.1.call-start = ((), (), s32[]{:S(2)}) async-start(), calls=%async_computation.19 | async-start | bytes 557056
  1005.6 225.3 %reduce-scatter.27.cloned.1.call-start = ((), (), s32[]{:S(2)}) async-start(), calls=%async_computation.17 | async-start | bytes 557056
  1006.7 303.6 %reduce-scatter.29.cloned.1.call-start = ((), (), s32[]{:S(2)}) async-start(), calls=%async_computation.18 | async-start | bytes 2228224
  1009.6 395.9 %reduce-scatter.19.cloned.1.call-start = ((), (), s32[]{:S(2)}) async-start(), calls=%async_computation.13 | async-start | bytes 4456448 | tf_op jit(solution)/shard_map/reduce_scatter | solution.py:393
  1018.3 597.8 %reduce-scatter.17.cloned.1.call-start = ((), (), s32[]{:S(2)}) async-start(), calls=%async_computation.12 | async-start | bytes 13369344 | tf_op jit(solution)/shard_map/reduce_scatter | solution.py:392
  1037.4 927.5 %reduce-scatter.21.cloned.1.call-start = ((), (), s32[]{:S(2)}) async-start(), calls=%async_computation.14 | async-start | bytes 17825792 | tf_op jit(solution)/shard_map/reduce_scatter | solution.py:395
  1061.1 1258.6 %reduce-scatter.23.cloned.1.call-start = ((), (), s32[]{:S(2)}) async-start(), calls=%async_computation.15 | async-start | bytes 17825792 | tf_op jit(solution)/shard_map/reduce_scatter | solution.py:397
  (53 other events, 481.0 us)
Sparse Core Ops, SparseCore 0:
  11.4 63.9 all-gather.6
  78.7 92.9 all-gather.4
  175.1 111.0 all-gather.8
  289.5 111.0 all-gather.10
  1003.9 76.4 reduce-scatter.24
  1082.6 73.0 reduce-scatter.30
  1158.0 72.9 reduce-scatter.26
  1233.3 76.9 reduce-scatter.28
  1313.3 92.0 reduce-scatter.18
  1412.5 203.5 reduce-scatter.16
  1618.9 345.9 reduce-scatter.20
  1967.7 351.9 reduce-scatter.22
where the time goes:
time: 2340 us; the launch traced here: 2330 us
  waiting for transfers between devices  1500 us (64%)
  matrix products  280 us (12%)
  local copies, waits for them, and re-layouts  164 us (7%)
  blocking collectives  159 us (7%)
  other arithmetic  155 us (7%)
  starting transfers between devices  35.7 us (2%)
    reduce_scatter x1, waiting for transfers between devices, shards(): lax.psum_scatter(grad_total[6], 'dp', scatter_dimension=1, tiled=True)  355 us
    reduce_scatter x1, waiting for transfers between devices, shards(): lax.psum_scatter(grad_total[4], 'dp', scatter_dimension=1, tiled=True)  349 us
    reduce_scatter x1, waiting for transfers between devices, shards(): lax.psum_scatter(grad_total[1], 'dp', scatter_dimension=1, tiled=True)  211 us
    unnamed x16, waiting for transfers between devices  177 us
    all_gather x1, waiting for transfers between devices, shards(): lax.all_gather(w_up.astype(jnp.bfloat16), 'dp', axis=1, tiled=True)  114 us
    all_gather x1, waiting for transfers between devices, shards(): lax.all_gather(w_down.astype(jnp.bfloat16), 'dp', axis=1, tiled=True)  114 us
    reduce_scatter x1, waiting for transfers between devices, shards(): lax.psum_scatter(grad_total[2], 'dp', scatter_dimension=1, tiled=True)  93.6 us
    unnamed x2, blocking collectives  78.6 us
  transfers between devices with their start and end apart: 16, of which 13 were waited for; matrix products, arithmetic and copies ran while one was open for 4% of the time, Pallas kernels for 0%

commit v1 on v0

v1 whole, which is shorter than its diff:
```python
import functools

import jax
import jax.numpy as jnp
from jax import lax
from jax.experimental import pallas as pl
from jax.experimental.pallas import tpu as pltpu
from jax.sharding import Mesh
from jax.sharding import PartitionSpec as P

D = 1024
HEADS = 16
HEAD_DIM = 64
FF = 4096
HALF = D // 2
LANES = 128

epsilon = 1e-06
masked_score = -1e30
root_half = 0.7071067811865476
inverse_root_two_pi = 0.3989422804014327

f32 = jnp.float32
bf16 = jnp.bfloat16


def mm(a, b):
    return jnp.dot(a, b, preferred_element_type=f32)


def mm_rows(a, b):
    return lax.dot_general(a, b, (((0,), (0,)), ((), ())), preferred_element_type=f32)


def mm_t(a, b):
    return lax.dot_general(a, b, (((1,), (1,)), ((), ())), preferred_element_type=f32)


def gelu_value(u):
    return 0.5 * u * (1.0 + lax.erf(u * root_half))


def gelu_slope(u):
    return 0.5 * (1.0 + lax.erf(u * root_half)) + u * jnp.exp(-0.5 * u * u) * inverse_root_two_pi


def swap(v, axis):
    return lax.ppermute(v, axis, [(0, 1), (1, 0)])


def to_plane(v, j):
    return lax.ppermute(v, ("y", "x"), [(i, i ^ j) for i in range(4)])


def place_kernel(splits, me_ref, own, px, py, pd, *rest):
    outs, sems = rest[: len(splits)], rest[len(splits)]
    me = me_ref[0]
    copies = []
    for j, src in enumerate((own, px, py, pd)):
        for k, (low, high) in enumerate(splits):
            copies.append(
                pltpu.make_async_copy(
                    src.at[:, :, low:high], outs[k].at[:, me ^ j], sems.at[j * len(splits) + k]
                )
            )
    for copy in copies:
        copy.start()
    for copy in copies:
        copy.wait()


def place(me, pieces, splits):
    depth, rows, _ = pieces[0].shape
    return pl.pallas_call(
        functools.partial(place_kernel, splits),
        out_shape=[
            jax.ShapeDtypeStruct((depth, 4, rows, high - low), pieces[0].dtype)
            for low, high in splits
        ],
        in_specs=[pl.BlockSpec(memory_space=pltpu.SMEM)] + [pl.BlockSpec(memory_space=pl.ANY)] * 4,
        out_specs=[pl.BlockSpec(memory_space=pltpu.VMEM)] * len(splits),
        scratch_shapes=[pltpu.SemaphoreType.DMA((4 * len(splits),))],
        compiler_params=pltpu.CompilerParams(vmem_limit_bytes=24 << 20),
        cost_estimate=pl.CostEstimate(
            flops=0, bytes_accessed=8 * pieces[0].size * 2, transcendentals=0
        ),
    )(jnp.reshape(me, (1,)), *pieces)


def after(v, other):
    return lax.optimization_barrier((v, other))[0]


def gather_pieces(shard, diagonal_by):
    own = lax.all_gather(shard, "z", axis=0, tiled=False)
    px = swap(own, "x")
    py = swap(own, "y")
    pd = swap(px, "y") if diagonal_by == "y" else swap(py, "x")
    return own, px, py, pd


def reduce_plane(grads, me, diagonal_by):
    def part(j):
        return lax.dynamic_index_in_dim(grads, me ^ j, axis=1, keepdims=False)

    first, second = ("x", "y") if diagonal_by == "y" else ("y", "x")
    near, far = (1, 2) if diagonal_by == "y" else (2, 1)
    across = swap(part(3), second)
    joined = (part(near).astype(f32) + across.astype(f32)).astype(grads.dtype)
    from_near = swap(joined, first)
    from_far = swap(part(far), second)
    return (part(0).astype(f32) + from_near.astype(f32) + from_far.astype(f32)).astype(grads.dtype)


def reduce_z(part):
    return lax.psum_scatter(part, "z", scatter_dimension=0, tiled=False)


def masks_of(seg_col, seg_row, i, block, low):
    width = (i + 1) * block - low
    rows = i * block + lax.broadcasted_iota(jnp.int32, (block, width), 0)
    columns = low + lax.broadcasted_iota(jnp.int32, (block, width), 1)
    same = seg_col[i * block : (i + 1) * block] == seg_row[:, low : (i + 1) * block]
    return same & (rows >= columns)


def head_lanes(h):
    lane = lax.broadcasted_iota(jnp.int32, (1, LANES), 1)
    return (lane // HEAD_DIM == h).astype(bf16)


def softmax_block(q, k, allowed):
    scores = mm_t(q, k)
    scores = jnp.where(allowed, scores, masked_score)
    top = jnp.max(scores, axis=-1, keepdims=True)
    exponent = jnp.exp(scores - top)
    return exponent / jnp.sum(exponent, axis=-1, keepdims=True)


def attend_kernel(block, q_ref, k_ref, v_ref, seg_col_ref, seg_row_ref, o_ref):
    length = q_ref.shape[0]
    seg_col, seg_row = seg_col_ref[0], seg_row_ref[0]
    for i in range(length // block):
        low = max(0, i - 1) * block
        high = (i + 1) * block
        allowed = masks_of(seg_col, seg_row, i, block, low)
        k, v = k_ref[low:high], v_ref[low:high]
        q = q_ref[i * block : high] * jnp.asarray(HEAD_DIM**-0.5, bf16)
        total = None
        for h in range(2):
            lanes = head_lanes(h)
            probs = softmax_block(q * lanes, k, allowed).astype(bf16)
            term = mm(probs, v * lanes)
            total = term if total is None else total + term
        o_ref[i * block : high] = total.astype(bf16)


def attend_back_kernel(
    block, q_ref, k_ref, v_ref, seg_col_ref, seg_row_ref, g_ref, dq_ref, dk_ref, dv_ref, dk_acc, dv_acc
):
    length = q_ref.shape[0]
    seg_col, seg_row = seg_col_ref[0], seg_row_ref[0]
    scale = jnp.asarray(HEAD_DIM**-0.5, bf16)
    dk_acc[...] = jnp.zeros_like(dk_acc)
    dv_acc[...] = jnp.zeros_like(dv_acc)
    for i in range(length // block):
        low = max(0, i - 1) * block
        high = (i + 1) * block
        allowed = masks_of(seg_col, seg_row, i, block, low)
        k, v = k_ref[low:high], v_ref[low:high]
        q = q_ref[i * block : high] * scale
        g = g_ref[i * block : high]
        dq = None
        for h in range(2):
            lanes = head_lanes(h)
            qh, gh = q * lanes, g * lanes
            probs = softmax_block(qh, k, allowed)
            dp = mm_t(gh, v)
            dv_acc[low:high] += mm_rows(probs.astype(bf16), gh)
            inner = jnp.sum(dp * probs, axis=-1, keepdims=True)
            ds = (probs * (dp - inner)).astype(bf16)
            term = mm(ds, k * (lanes * scale))
            dq = term if dq is None else dq + term
            dk_acc[low:high] += mm_rows(ds, qh)
        dq_ref[i * block : high] = dq.astype(bf16)
    dk_ref[...] = dk_acc[...].astype(bf16)
    dv_ref[...] = dv_acc[...].astype(bf16)


def attention_specs(length, pairs):
    def at(base):
        return pl.BlockSpec((length, LANES), lambda s, p: (s, base + p))

    return (
        [at(0), at(pairs), at(2 * pairs)]
        + [
            pl.BlockSpec((1, length, 1), lambda s, p: (s, 0, 0)),
            pl.BlockSpec((1, 1, length), lambda s, p: (s, 0, 0)),
        ],
        at(0),
    )


def attend(qkv, seg, block):
    count, length = seg.shape
    pairs = qkv.shape[1] // (3 * LANES)
    in_specs, one = attention_specs(length, pairs)
    work = count * pairs * 2 * length * 2 * block
    return pl.pallas_call(
        functools.partial(attend_kernel, block),
        grid=(count, pairs),
        out_shape=jax.ShapeDtypeStruct((count * length, pairs * LANES), bf16),
        in_specs=in_specs,
        out_specs=one,
        cost_estimate=pl.CostEstimate(
            flops=work * 4 * LANES, bytes_accessed=qkv.size * 3, transcendentals=work
        ),
    )(qkv, qkv, qkv, seg[:, :, None], seg[:, None, :])


def attend_back(qkv, seg, grad, block):
    count, length = seg.shape
    pairs = qkv.shape[1] // (3 * LANES)
    in_specs, one = attention_specs(length, pairs)
    work = count * pairs * 2 * length * 2 * block
    like = jax.ShapeDtypeStruct((count * length, pairs * LANES), bf16)
    parts = pl.pallas_call(
        functools.partial(attend_back_kernel, block),
        grid=(count, pairs),
        out_shape=[like] * 3,
        in_specs=in_specs + [one],
        out_specs=[one] * 3,
        scratch_shapes=[pltpu.VMEM((length, LANES), f32)] * 2,
        cost_estimate=pl.CostEstimate(
            flops=work * 10 * LANES, bytes_accessed=qkv.size * 5, transcendentals=work
        ),
    )(qkv, qkv, qkv, seg[:, :, None], seg[:, None, :], grad)
    return jnp.concatenate(parts, axis=1)


def inverse_rms(v):
    return lax.rsqrt(jnp.mean(v * v, axis=-1, keepdims=True) + epsilon)


def norm_back(grad, unit, inverse, gain):
    scaled = grad * gain
    return inverse * (scaled - unit * jnp.mean(scaled * unit, axis=-1, keepdims=True))


def shards(
    boundary_in,
    segments,
    routed,
    gain_attn,
    w_qkv,
    w_out,
    gain_mlp,
    w_up,
    b_up,
    w_down,
    b_down,
    router,
):
    core = lax.axis_index("section")
    first = core == 0
    me = 2 * lax.axis_index("y") + lax.axis_index("x")
    depth = lax.axis_size("z")
    rows = w_qkv.shape[1]
    dp = 4 * depth
    units = w_up.shape[2] // dp
    half_units = units // 2
    micro, length = boundary_in.shape[1], boundary_in.shape[3]
    tokens = micro * length

    qkv_halves = w_qkv[0].astype(bf16).reshape(rows, 3, 2, HALF)
    out_halves = w_out[0].astype(bf16).reshape(rows, 2, HALF)
    up_halves = w_up[0].astype(bf16).reshape(rows, dp, 2, half_units)
    down_halves = w_down[0].astype(bf16).reshape(2, half_units, D)
    bias_halves = b_up[0].astype(bf16).reshape(2, half_units // rows, rows)
    column = lambda v: jnp.pad(v.astype(bf16), (0, rows - v.shape[0]))[:, None]
    small = jnp.concatenate(
        [column(gain_attn[0]), column(gain_mlp[0]), column(b_down[0]), column(router)], axis=1
    )
    bias_cols = half_units // rows

    def half(h):
        pick = lambda v, axis: lax.dynamic_index_in_dim(v, h, axis=axis, keepdims=False)
        extra = jnp.concatenate([small, pick(bias_halves, 0).T], axis=1)
        extra = jnp.pad(extra, ((0, 0), (0, LANES - extra.shape[1])))
        attn = jnp.concatenate(
            [pick(qkv_halves, 2).reshape(rows, 3 * HALF), pick(out_halves, 1), extra], axis=1
        )
        return attn, pick(up_halves, 2).reshape(rows, D * 2), pick(down_halves, 0)

    kept, sent = half(core), half(1 - core)
    came = tuple(swap(v, "section") for v in sent)
    shard0 = tuple(jnp.where(first, k, r) for k, r in zip(kept, came))
    shard1 = tuple(jnp.where(first, r, k) for k, r in zip(kept, came))

    mine = boundary_in[0, :, 0].reshape(tokens, D)
    other = swap(mine, "section")
    x_b = jnp.where(first, mine, other)
    cot_b = jnp.where(first, other, mine)
    seg = segments[:, 0]
    picked = routed[:, 0]
    count = picked.shape[1]
    chosen_rows = micro * count

    def attention_weights(shard, by):
        pieces = gather_pieces(shard, by)
        w_q, w_o, extra = place(
            me, pieces, ((0, 3 * HALF), (3 * HALF, 4 * HALF), (4 * HALF, 4 * HALF + LANES))
        )
        w_o = w_o.reshape(D, HALF)
        own = lax.dynamic_slice_in_dim(w_o, core * HALF, HALF, axis=0)
        recv = swap(lax.dynamic_slice_in_dim(w_o, (1 - core) * HALF, HALF, axis=0), "section")
        w_o = jnp.concatenate([jnp.where(first, own, recv), jnp.where(first, recv, own)], axis=1)
        extra = extra.reshape(D, LANES)
        choose = (
            lax.broadcasted_iota(jnp.int32, (8, LANES), 0)
            == lax.broadcasted_iota(jnp.int32, (8, LANES), 1)
        ).astype(bf16)
        vectors = mm_t(choose, extra)
        bias = vectors[4 : 4 + bias_cols].reshape(bias_cols, dp, rows)
        return w_q.reshape(D, 3 * HALF), w_o, vectors, bias, pieces[0]

    w_q0, w_o0, vec0, bias0, w_own = attention_weights(shard0[0], "y")
    pieces = gather_pieces(after(shard0[1], w_own), "x")
    (w_u0,) = place(me, pieces, ((0, D * 2),))
    w_u0 = w_u0.reshape(D, D * 2)
    pieces = gather_pieces(after(shard0[2], pieces[0]), "y")
    last = pieces[0]
    (w_d0,) = place(me, pieces, ((0, D),))
    w_d0 = w_d0.reshape(D * 2, D)
    w_q1, w_o1, vec1, bias1, last = attention_weights(after(shard1[0], last), "x")

    up1 = shard1[1].reshape(rows, depth, 4, half_units)
    pick_up = lambda j: lax.dynamic_index_in_dim(up1, me ^ j, axis=2, keepdims=False)
    relative = [pick_up(0)] + [to_plane(pick_up(j), j) for j in (1, 2, 3)]
    relative = jnp.stack([v.reshape(rows, depth * half_units) for v in relative])
    natural = jnp.concatenate(
        [lax.dynamic_slice_in_dim(relative, me ^ n, 1, axis=0) for n in range(4)], axis=0
    )
    w_u1 = lax.all_gather(after(natural, last), "z", axis=0, tiled=False).reshape(D, depth * half_units)
    w_d1 = lax.all_gather(after(shard1[2], last), "z", axis=0, tiled=False).reshape(depth * half_units, D)

    bias_up0 = bias0.transpose(1, 0, 2).reshape(1, 2 * D)
    gain_attn0, gain_mlp0, b_down0 = vec0[0:1], vec0[1:2], vec0[2:3]
    x = x_b.astype(f32)
    inv_attn0 = inverse_rms(x)
    a0 = (x * inv_attn0 * gain_attn0).astype(bf16)
    qkv0 = mm(a0, w_q0).astype(bf16)
    o0 = attend(qkv0, seg, LANES)
    z_part = mm(o0, w_o0).astype(bf16)
    h0 = x + (z_part.astype(f32) + swap(z_part, "section").astype(f32))
    inv_mlp0 = inverse_rms(h0)
    m0 = (h0 * inv_mlp0 * gain_mlp0).astype(bf16)
    u0 = mm(m0, w_u0) + bias_up0
    g0 = gelu_value(u0).astype(bf16)
    e_part = mm(g0, w_d0).astype(bf16)
    e0 = e_part.astype(f32) + swap(e_part, "section").astype(f32) + b_down0
    y0_b = (h0 + e0).astype(bf16)

    onehot = picked[:, :, None] == lax.broadcasted_iota(jnp.int32, (micro, count, length), 2)
    onehot_b = onehot.astype(bf16)
    take = lambda v: lax.dot_general(
        onehot_b,
        v.reshape(micro, length, D),
        (((2,), (1,)), ((0,), (0,))),
        preferred_element_type=f32,
    ).reshape(chosen_rows, D)
    put = lambda v: lax.dot_general(
        onehot.astype(f32),
        v.reshape(micro, count, D),
        (((1,), (1,)), ((0,), (0,))),
        precision=lax.Precision.HIGHEST,
        preferred_element_type=f32,
    ).reshape(tokens, D)
    seg1 = jnp.sum(jnp.where(onehot, seg[:, None, :], 0), axis=2)
    chosen = take(y0_b)
    grad_chosen = take(cot_b)
    router_full = jnp.concatenate(
        [v[3].reshape(dp, rows)[:, : rows // 2].reshape(1, HALF) for v in (vec0, vec1)], axis=1
    )
    weight = jax.nn.sigmoid(jnp.sum(chosen * router_full, axis=1, keepdims=True))
    gy1 = weight * grad_chosen
    de1 = gy1.astype(bf16)

    def plane_rows(v):
        rest = v.shape[0] // 2
        one = lax.dynamic_slice_in_dim(v, core * rest, rest, axis=0)
        mine_now = jnp.stack([one] + [to_plane(one, j) for j in (1, 2, 3)])
        other_now = swap(mine_now, "section")
        both = jnp.stack(
            [jnp.where(first, mine_now, other_now), jnp.where(first, other_now, mine_now)], axis=1
        )
        both = both.reshape(4, v.shape[0], v.shape[1])
        return both.reshape(4 * v.shape[0], v.shape[1])

    de_all = plane_rows(de1)
    gain_attn1, gain_mlp1, b_down1 = vec1[0:1], vec1[1:2], vec1[2:3]
    bias_mine = lax.dynamic_index_in_dim(
        bias1.reshape(bias_cols, depth, 4, rows), me, axis=2, keepdims=False
    )
    bias_up1 = bias_mine.transpose(1, 0, 2).reshape(1, depth * half_units)
    inv_attn1 = inverse_rms(chosen)
    a1 = (chosen * inv_attn1 * gain_attn1).astype(bf16)
    qkv1 = mm(a1, w_q1).astype(bf16)
    o1 = attend(qkv1, seg1, count)
    z_part = mm(o1, w_o1).astype(bf16)
    z1 = z_part.astype(f32) + swap(z_part, "section").astype(f32)
    h1 = chosen + z1
    inv_mlp1 = inverse_rms(h1)
    m1 = (h1 * inv_mlp1 * gain_mlp1).astype(bf16)
    m_all = plane_rows(m1)
    u1 = mm(m_all, w_u1) + bias_up1
    g1 = gelu_value(u1).astype(bf16)
    e_part = mm(g1, w_d1).astype(bf16)
    du1 = (mm_t(de_all, w_d1) * gelu_slope(u1)).astype(bf16)
    dm_part = mm_t(du1, w_u1).astype(bf16)
    e_part = e_part.reshape(4, chosen_rows, D)
    dm_part = dm_part.reshape(4, chosen_rows, D)
    keep = jnp.where(first, e_part, dm_part)
    recv = swap(jnp.where(first, dm_part, e_part), "section")
    summed = (keep.astype(f32) + recv.astype(f32)).astype(bf16)
    total = summed[0].astype(f32)
    for j in (1, 2, 3):
        total = total + to_plane(summed[j], j).astype(f32)
    total = total.astype(bf16)
    crossed = swap(total, "section")
    e1 = jnp.where(first, total, crossed).astype(f32) + b_down1
    dm1 = jnp.where(first, crossed, total).astype(f32)
    delta = z1 + e1
    y1_b = (y0_b.astype(f32) + put(weight * delta)).astype(bf16)

    grad_logit = jnp.sum(grad_chosen * delta, axis=1, keepdims=True) * weight * (1.0 - weight)
    grad_router = jnp.sum(grad_logit * chosen, axis=0)
    unit_mlp1 = h1 * inv_mlp1
    dh1 = norm_back(dm1, unit_mlp1, inv_mlp1, gain_mlp1)
    dz1 = (gy1 + dh1).astype(bf16)
    do1 = mm_t(dz1, w_o1).astype(bf16)
    dqkv1 = attend_back(qkv1, seg1, do1, count)
    da_part = mm_t(dqkv1, w_q1).astype(bf16)
    da1 = da_part.astype(f32) + swap(da_part, "section").astype(f32)
    unit_attn1 = chosen * inv_attn1
    dx1 = dh1 + norm_back(da1, unit_attn1, inv_attn1, gain_attn1)
    gy0_b = (cot_b.astype(f32) + put(dx1 + grad_logit * router_full)).astype(bf16)

    def extra_of(gain_a, gain_m, down_bias, up_bias, block):
        part = grad_router[block * HALF : (block + 1) * HALF].reshape(dp, rows // 2)
        part = jnp.pad(part, ((0, 0), (0, rows - rows // 2))).reshape(D)
        columns = [v[None] for v in (gain_a, gain_m, down_bias, part)]
        columns = jnp.concatenate(columns + [up_bias], axis=0)
        columns = jnp.pad(columns, ((0, LANES - columns.shape[0]), (0, 0)))
        return columns.T.astype(bf16)

    def out_by_columns(grad):
        own = lax.dynamic_slice_in_dim(grad, core * HALF, HALF, axis=1)
        recv = swap(lax.dynamic_slice_in_dim(grad, (1 - core) * HALF, HALF, axis=1), "section")
        return jnp.concatenate([jnp.where(first, own, recv), jnp.where(first, recv, own)], axis=0)

    gw_d1 = mm_rows(g1, de_all).astype(bf16).reshape(depth, half_units, D)
    gw_u1 = mm_rows(m_all, du1).astype(bf16).reshape(depth, 4, rows, depth * half_units)
    gw_o1 = out_by_columns(mm_rows(o1, dz1).astype(bf16))
    gw_q1 = mm_rows(a1, dqkv1).astype(bf16)
    gb_u1 = jnp.sum(du1.astype(f32), axis=0).reshape(depth, 1, bias_cols, rows)
    here = lax.broadcasted_iota(jnp.int32, (1, 4, 1, 1), 1) == me
    gb_u1 = jnp.where(here, gb_u1, 0.0).transpose(2, 0, 1, 3).reshape(bias_cols, D)
    extra1 = extra_of(
        jnp.sum(da1 * unit_attn1, axis=0),
        jnp.sum(dm1 * unit_mlp1, axis=0),
        jnp.sum(de1.astype(f32), axis=0),
        gb_u1,
        1,
    )
    as_shards = lambda v: v.reshape(depth, 4, v.shape[0] // dp, v.shape[1])
    r_d1 = reduce_z(gw_d1)
    r_u1 = reduce_z(gw_u1)
    attn1 = as_shards(jnp.concatenate([gw_q1, gw_o1, extra1], axis=1))
    r_a1 = reduce_z(reduce_plane(attn1, me, "x"))
    pick_up = lambda j: lax.dynamic_index_in_dim(r_u1, me ^ j, axis=0, keepdims=False)
    relative = [pick_up(0)] + [to_plane(pick_up(j), j) for j in (1, 2, 3)]
    relative = jnp.stack([v.reshape(rows, depth, half_units) for v in relative], axis=2)
    r_u1 = jnp.concatenate(
        [lax.dynamic_slice_in_dim(relative, me ^ n, 1, axis=2) for n in range(4)], axis=2
    ).reshape(rows, 2 * D)

    gw_d0 = mm_rows(g0, gy0_b).astype(bf16)
    r_d0 = reduce_z(reduce_plane(as_shards(gw_d0), me, "y"))
    du0 = (mm_t(gy0_b, w_d0) * gelu_slope(u0)).astype(bf16)
    gw_u0 = mm_rows(m0, du0).astype(bf16)
    r_u0 = reduce_z(reduce_plane(as_shards(gw_u0), me, "x"))
    dm_part = mm_t(du0, w_u0).astype(bf16)
    dm0 = dm_part.astype(f32) + swap(dm_part, "section").astype(f32)
    unit_mlp0 = h0 * inv_mlp0
    dh0 = norm_back(dm0, unit_mlp0, inv_mlp0, gain_mlp0)
    gy0 = gy0_b.astype(f32)
    dz0 = (gy0 + dh0).astype(bf16)
    do0 = mm_t(dz0, w_o0).astype(bf16)
    dqkv0 = attend_back(qkv0, seg, do0, LANES)
    da_part = mm_t(dqkv0, w_q0).astype(bf16)
    da0 = da_part.astype(f32) + swap(da_part, "section").astype(f32)
    gw_o0 = out_by_columns(mm_rows(o0, dz0).astype(bf16))
    gw_q0 = mm_rows(a0, dqkv0).astype(bf16)
    unit_attn0 = x * inv_attn0
    dx0_b = (gy0 + dh0 + norm_back(da0, unit_attn0, inv_attn0, gain_attn0)).astype(bf16)
    gb_u0 = jnp.sum(du0.astype(f32), axis=0).reshape(dp, bias_cols, rows)
    extra0 = extra_of(
        jnp.sum(da0 * unit_attn0, axis=0),
        jnp.sum(dm0 * unit_mlp0, axis=0),
        jnp.sum(gy0, axis=0),
        gb_u0.transpose(1, 0, 2).reshape(bias_cols, D),
        0,
    )
    attn0 = as_shards(jnp.concatenate([gw_q0, gw_o0, extra0], axis=1))
    r_a0 = reduce_z(reduce_plane(attn0, me, "y"))

    def joined(grad0, grad1):
        keep = jnp.where(first, grad0, grad1)
        recv = swap(jnp.where(first, grad1, grad0), "section")
        low, high = jnp.where(first, keep, recv), jnp.where(first, recv, keep)
        return keep.astype(f32), low.astype(f32), high.astype(f32)

    _, low, high = joined(r_d0, r_d1)
    out_down = jnp.concatenate([low, high], axis=0)[None]
    _, low, high = joined(r_u0, r_u1)
    cut = lambda v: v.reshape(rows, dp, half_units)
    out_up = jnp.stack([cut(low), cut(high)], axis=2).reshape(1, rows, FF)
    keep, low, high = joined(r_a0, r_a1)
    cut = lambda v: v[:, : 3 * HALF].reshape(rows, 3, HALF)
    out_qkv = jnp.stack([cut(low), cut(high)], axis=2).reshape(1, rows, 3 * D)
    cut = lambda v: v[:, 3 * HALF : 4 * HALF]
    out_out = jnp.concatenate([cut(low), cut(high)], axis=1)[None]
    small = keep[:, 4 * HALF : 4 * HALF + 8].T
    cut = lambda v: v[:, 4 * HALF + 4 : 4 * HALF + 4 + bias_cols].T
    out_b_up = jnp.stack([cut(low), cut(high)]).reshape(1, units)
    boundary_out = jnp.where(first, dx0_b, y1_b).reshape(1, micro, 1, length, D)
    return (
        boundary_out,
        small[0:1],
        out_qkv,
        out_out,
        small[1:2],
        out_up,
        out_b_up,
        out_down,
        small[2:3],
        small[3, : rows // 2],
    )


def solution(mesh):
    sections, dp = mesh.shape["section"], mesh.shape["dp"]
    grid = Mesh(mesh.devices.reshape(sections, dp // 4, 2, 2), ("section", "z", "y", "x"))
    chips = ("z", "y", "x")
    in_specs = (
        P("section", None, chips, None, None),
        P(None, chips, None),
        P(None, chips, None),
        P("section", chips),
        P("section", chips, None),
        P("section", chips, None),
        P("section", chips),
        P("section", chips, None),
        P("section", chips),
        P("section", chips, None),
        P("section", chips),
        P(("section",) + chips),
    )
    out_specs = (
        P("section", None, chips, None, None),
        P("section", chips),
        P("section", chips, None),
        P("section", chips, None),
        P("section", chips),
        P("section", chips, None),
        P("section", chips),
        P("section", chips, None),
        P("section", chips),
        P(("section",) + chips),
    )
    return jax.shard_map(shards, mesh=grid, in_specs=in_specs, out_specs=out_specs, check_vma=False)
```

time: 2340 us -> 770 us (0.33)
  waiting for transfers between devices: 1500 us -> 301 us
  matrix products: 280 us -> 98.7 us
  blocking collectives: 159 us -> 0 us
  local copies, waits for them, and re-layouts: 164 us -> 91.8 us
  Pallas kernels: 0 us -> 68.2 us
    reduce_scatter x4 -> x6, waiting for transfers between devices: 1010 us -> 13.6 us  [reduce_z(): return lax.psum_scatter(part, 'z', scatter_dimension=0, tiled=False)]
    all_gather x4 -> x6, waiting for transfers between devices: 304 us -> 27.5 us  [the longest x4 27.5 us: gather_pieces(): own = lax.all_gather(shard, 'z', axis=0, tiled=False)]
    ppermute x4 -> x60, waiting for transfers between devices: 7.2 us -> 260 us  [the longest x45 187 us: swap(): return lax.ppermute(v, axis, [(0, 1), (1, 0)])]
    dot_general x38 -> x30, matrix products: 280 us -> 98.7 us  [the longest x8 30.2 us: mm(): return jnp.dot(a, b, preferred_element_type=f32)]
    unnamed x16 -> x12, waiting for transfers between devices: 177 us -> 0.2 us
    unnamed x2 -> x0, blocking collectives: 78.6 us -> none
    add x10 -> x2, other arithmetic: 77.4 us -> 4.98 us  [the longest x1 3.3 us: shards(): gy0 + dh0 + norm_back(da0, unit_attn0, inv_attn0, gain_attn0)]
    pallas_call x0 -> x8, Pallas kernels: none -> 68.2 us  [the longest x2 41.1 us: attend_back(): pl.pallas_call(functools.partial(attend_back_kernel, block), grid=(count,...]
  transfers between devices with their start and end apart: 16 -> 72, of which waited for: 13 -> 25; matrix products, arithmetic and copies ran while one was open for 4% -> 37% of each run, Pallas kernels for 0% -> 9%
where the time goes in v1:
time: 770 us; the launch traced here: 760 us
  waiting for transfers between devices  301 us (39%)
  other arithmetic  135 us (18%)
  matrix products  98.7 us (13%)
  local copies, waits for them, and re-layouts  91.8 us (12%)
  Pallas kernels  68.2 us (9%)
  starting transfers between devices  48.7 us (6%)
  between operations  16.5 us (2%)
    ppermute x45, waiting for transfers between devices, swap(): return lax.ppermute(v, axis, [(0, 1), (1, 0)])  187 us
    ppermute x15, waiting for transfers between devices, to_plane(): return lax.ppermute(v, ('y', 'x'), [(i, i ^ j) for i in range(4)])  72.9 us
    pallas_call x2, Pallas kernels, attend_back(): pl.pallas_call(functools.partial(attend_back_kernel, block), grid=(count,...  41.1 us
    unnamed x250, local copies, waits for them, and re-layouts  32.5 us
    dot_general x8, matrix products, mm(): return jnp.dot(a, b, preferred_element_type=f32)  30.2 us
    dot_general x10, matrix products, mm_t(): lax.dot_general(a, b, (((1,), (1,)), ((), ())), preferred_element_type=f32)  30.2 us
    ppermute x45, starting transfers between devices, swap(): return lax.ppermute(v, axis, [(0, 1), (1, 0)])  29.1 us
    dot_general x8, matrix products, mm_rows(): lax.dot_general(a, b, (((0,), (0,)), ((), ())), preferred_element_type=f32)  29 us
  transfers between devices with their start and end apart: 72, of which 25 were waited for; matrix products, arithmetic and copies ran while one was open for 37% of the time, Pallas kernels for 9%

profile of v1, /device:TPU:0, one launch (start us, length us, event | category | flops | bytes accessed | tf_op | source)
XLA Modules:
  0.0 759.9 jit_solution(6162322060080232711)
XLA Ops:
  22.6 27.5 %all-gather.13.cloned.1.call-done = bf16[256,2176]{1,0:T(8,128)(2,1)} async-done(((bf16[64,2176]{1,0:T(8,128)(2,1)}), bf16[256,2176]{1,0:T(8,128)(2,1)}) %all-gather.13.cloned.1.call-update) | async-done | bytes 1114128 | tf_op jit(solution)/shard_map/all_gather | solution.py:95
  54.9 21.5 %collective-permute-done.2.px = bf16[4,64,2176]{2,1,0:T(8,128)(2,1)S(1)} collective-permute-done((bf16[4,64,2176]{2,1,0:T(8,128)(2,1)}, bf16[4,64,2176]{2,1,0:T(8,128)(2,1)S(1)}, u32[]{:S(2)}, u32[]{:S(2)}) %collective-permute-start.2) | collective-permute-done | bytes 1114144 | tf_op jit(solution)/shard_map/ppermute | solution.py:48
  85.7 19.3 %collective-permute-done.4.pd = bf16[4,64,2176]{2,1,0:T(8,128)(2,1)} collective-permute-done((bf16[4,64,2176]{2,1,0:T(8,128)(2,1)S(1)}, bf16[4,64,2176]{2,1,0:T(8,128)(2,1)}, u32[]{:S(2)}, u32[]{:S(2)}) %collective-permute-start.4) | collective-permute-done | bytes 1114144 | tf_op jit(solution)/shard_map/ppermute | solution.py:48
  113.8 14.4 %shard_map.196 = bf16[1024,512]{1,0:T(8,128)(2,1)} custom-call(bf16[1024,1536]{1,0:T(8,128)(2,1)} %convolution_convert_fusion.2.q_ref.k_ref.v_ref, bf16[1024,1536]{1,0:T(8,128)(2,1)} %convolution_convert_fusion.2.q_ref.k_ref.v_ref, bf16[1024,1536]{1,0:T(8,128)(2,1)} %convolution_convert_fusion.2.q_ref.k_ref.v_ref, ...), custom_call_target="tpu_custom_call" | custom-call | flops 1073741824 | bytes 4718592 | tf_op jit(solution)/shard_map/pallas_call | solution.py:209
  137.5 21.9 %collective-permute-done.8.px = bf16[4,64,2048]{2,1,0:T(8,128)(2,1)} collective-permute-done((bf16[4,64,2048]{2,1,0:T(8,128)(2,1)S(1)}, bf16[4,64,2048]{2,1,0:T(8,128)(2,1)}, u32[]{:S(2)}, u32[]{:S(2)}) %collective-permute-start.8) | collective-permute-done | bytes 1048608 | tf_op jit(solution)/shard_map/ppermute | solution.py:48
  159.4 22.5 %collective-permute-done.10.pd = bf16[4,64,2048]{2,1,0:T(8,128)(2,1)} collective-permute-done((bf16[4,64,2048]{2,1,0:T(8,128)(2,1)}, bf16[4,64,2048]{2,1,0:T(8,128)(2,1)}, u32[]{:S(2)}, u32[]{:S(2)}) %collective-permute-start.10) | collective-permute-done | bytes 1048608 | tf_op jit(solution)/shard_map/ppermute | solution.py:48
  185.8 17.5 %collective-permute-done.12.px = bf16[4,128,1024]{2,1,0:T(8,128)(2,1)S(1)} collective-permute-done((bf16[4,128,1024]{2,1,0:T(8,128)(2,1)}, bf16[4,128,1024]{2,1,0:T(8,128)(2,1)S(1)}, u32[]{:S(2)}, u32[]{:S(2)}) %collective-permute-start.12) | collective-permute-done | bytes 1048608 | tf_op jit(solution)/shard_map/ppermute | solution.py:48
  209.6 7.9 %multiply_convert_fusion = (bf16[1024,2048]{1,0:T(8,128)(2,1)S(1)}, f32[1024,2048]{1,0:T(8,128)}) fusion(f32[2048]{0:T(1024)S(1)} %add.323, bf16[1024,2048]{1,0:T(8,128)(2,1)S(1)} %bitcast.332, f32[1024,1024]{1,0:T(8,128)S(1)} %get-tuple-element.124, f32[1024]{0:T(1024)S(1)} %bitcast.413, f32[1024]{0:T(1024)S(1)} %add_rsqrt_fusion), kind=kOutput, calls=%fused_computation.7 | convolution fusion | flops 4310695936 | bytes 20987904 | tf_op jit(solution)/shard_map/dot_general | solution.py:28
  217.5 12.0 %collective-permute-done.14.pd = bf16[4,128,1024]{2,1,0:T(8,128)(2,1)} collective-permute-done((bf16[4,128,1024]{2,1,0:T(8,128)(2,1)S(1)}, bf16[4,128,1024]{2,1,0:T(8,128)(2,1)}, u32[]{:S(2)}, u32[]{:S(2)}) %collective-permute-start.14) | collective-permute-done | bytes 1048608 | tf_op jit(solution)/shard_map/ppermute | solution.py:48
  240.9 11.3 %collective-permute-done.17.py = bf16[4,64,2176]{2,1,0:T(8,128)(2,1)S(1)} collective-permute-done((bf16[4,64,2176]{2,1,0:T(8,128)(2,1)}, bf16[4,64,2176]{2,1,0:T(8,128)(2,1)S(1)}, u32[]{:S(2)}, u32[]{:S(2)}) %collective-permute-start.17) | collective-permute-done | bytes 1114144 | tf_op jit(solution)/shard_map/ppermute | solution.py:48
  260.4 32.7 %collective-permute-done.25 = bf16[64,4,128]{2,0,1:T(8,128)(2,1)} collective-permute-done((bf16[64,4,128]{2,0,1:T(8,128)(2,1)}, bf16[64,4,128]{2,0,1:T(8,128)(2,1)}, u32[]{:S(2)}, u32[]{:S(2)}) %collective-permute-start.25) | collective-permute-done | bytes 65568 | tf_op jit(solution)/shard_map/ppermute | solution.py:52
  419.1 10.2 %shard_map.201 = (bf16[128,512]{1,0:T(8,128)(2,1)}, bf16[128,512]{1,0:T(8,128)(2,1)}, bf16[128,512]{1,0:T(8,128)(2,1)}) custom-call(bf16[128,1536]{1,0:T(8,128)(2,1)} %convolution_convert_fusion.5.q_ref.k_ref.v_ref, bf16[128,1536]{1,0:T(8,128)(2,1)} %convolution_convert_fusion.5.q_ref.k_ref.v_ref, ...), custom_call_target="tpu_custom_call" | custom-call | flops 167772160 | bytes 983040 | tf_op jit(solution)/shard_map/pallas_call | solution.py:227
  451.9 7.9 %fusion.85 = (bf16[2048]{0:T(1024)(128)(2,1)S(1)}, bf16[1024,2048]{1,0:T(8,128)(2,1)S(1)}) fusion(f32[1024,2048]{1,0:T(8,128)S(1)} %bitcast.443, f32[2048]{0:T(1024)S(1)} %copy-done.93, bf16[1024,1024]{1,0:T(8,128)(2,1)S(1)} %get-tuple-element.121, bf16[2048,1024]{1,0:T(8,128)(2,1)S(1)} %bitcast.335), kind=kOutput, calls=%fused_computation.304 | convolution fusion | flops 4320131072 | bytes 18886656 | tf_op jit(solution)/shard_map/dot_general | solution.py:36
  465.7 7.0 convolution_convert_fusion.4
  481.9 15.1 %pad_maximum_fusion.1 = bf16[1024,2176]{1,0:T(8,128)(2,1)S(1)} fusion(bf16[1024,128]{1,0:T(8,128)(2,1)S(1)} %pad_bitcast_fusion, bf16[512,512]{1,0:T(8,128)(2,1)S(1)} %get-tuple-element.140, bf16[512,512]{1,0:T(8,128)(2,1)S(1)} %get-tuple-element.139, bf16[1024,1536]{1,0:T(8,128)(2,1)S(1)} %convolution_convert_fusion), kind=kLoop, calls=%fused_computation.17 | loop fusion | flops 17825792 | bytes 8912896 | tf_op jit(solution)/shard_map/concatenate | solution.py:479
  512.7 16.0 %collective-permute-done.45 = bf16[4,64,2176]{2,1,0:T(8,128)(2,1)} collective-permute-done((bf16[4,64,2176]{2,1,0:T(8,128)(2,1)S(1)}, bf16[4,64,2176]{2,1,0:T(8,128)(2,1)}, u32[]{:S(2)}, u32[]{:S(2)}) %collective-permute-start.45) | collective-permute-done | bytes 1114144 | tf_op jit(solution)/shard_map/ppermute | solution.py:48
  544.6 31.0 %shard_map.202 = (bf16[1024,512]{1,0:T(8,128)(2,1)}, bf16[1024,512]{1,0:T(8,128)(2,1)}, bf16[1024,512]{1,0:T(8,128)(2,1)}) custom-call(bf16[1024,1536]{1,0:T(8,128)(2,1)} %convolution_convert_fusion.2.q_ref.k_ref.v_ref, bf16[1024,1536]{1,0:T(8,128)(2,1)} %convolution_convert_fusion.2.q_ref.k_ref.v_ref, ...), custom_call_target="tpu_custom_call" | custom-call | flops 2684354560 | bytes 7864320 | tf_op jit(solution)/shard_map/pallas_call | solution.py:227
  579.2 17.9 %collective-permute-done.57 = bf16[4,128,1024]{2,1,0:T(8,128)(2,1)} collective-permute-done((bf16[4,128,1024]{2,1,0:T(8,128)(2,1)}, bf16[4,128,1024]{2,1,0:T(8,128)(2,1)}, u32[]{:S(2)}, u32[]{:S(2)}) %collective-permute-start.57) | collective-permute-done | bytes 1048608 | tf_op jit(solution)/shard_map/ppermute | solution.py:48
  618.6 7.2 convolution_convert_fusion.1
  631.2 16.7 %pad_maximum_fusion = bf16[1024,2176]{1,0:T(8,128)(2,1)S(1)} fusion(bf16[1024,128]{1,0:T(8,128)(2,1)S(1)} %pad_bitcast_fusion.1, bf16[512,512]{1,0:T(8,128)(2,1)S(1)} %get-tuple-element.138, bf16[512,512]{1,0:T(8,128)(2,1)S(1)} %get-tuple-element.137, bf16[1024,1536]{1,0:T(8,128)(2,1)} %convolution_convert_fusion.1), kind=kLoop, calls=%fused_computation.16 | loop fusion | flops 17825792 | bytes 8912896 | tf_op jit(solution)/shard_map/concatenate | solution.py:515
  657.1 22.2 %collective-permute-done.41 = bf16[4,64,2176]{2,1,0:T(8,128)(2,1)} collective-permute-done((bf16[4,64,2176]{2,1,0:T(8,128)(2,1)}, bf16[4,64,2176]{2,1,0:T(8,128)(2,1)}, u32[]{:S(2)}, u32[]{:S(2)}) %collective-permute-start.41) | collective-permute-done | bytes 1114144 | tf_op jit(solution)/shard_map/ppermute | solution.py:48
  691.8 18.4 %collective-permute-done.54 = bf16[64,512]{1,0:T(8,128)(2,1)S(1)} collective-permute-done((bf16[64,512]{1,0:T(8,128)(2,1)S(1)}, bf16[64,512]{1,0:T(8,128)(2,1)S(1)}, u32[]{:S(2)}, u32[]{:S(2)}) %collective-permute-start.54) | collective-permute-done | bytes 65568 | tf_op jit(solution)/shard_map/ppermute | solution.py:52
  717.3 7.8 %fusion.28 = bf16[1024,1024]{1,0:T(8,128)(2,1)} fusion(f32[2,512,1024]{2,1,0:T(8,128)} %fusion.63, bf16[1024,1024]{1,0:T(8,128)(2,1)} %copy-done.26, f32[1024,1024]{1,0:T(8,128)} %copy-done.29, bf16[1024,1024]{1,0:T(8,128)(2,1)S(1)} %copy-done.23, bf16[1024,1024]{1,0:T(8,128)(2,1)} %collective-permute-done.39, ...), kind=kLoop, calls=%fused_computation.56 | loop fusion | flops 15728640 | bytes 18886656 | tf_op jit(solution)/shard_map/jit(_where)/select_n | solution.py:537
  728.0 13.6 %reduce-scatter.7.cloned.1.call-done = bf16[1,64,2176]{2,1,0:T(8,128)(2,1)} async-done(((bf16[4,64,2176]{2,1,0:T(8,128)(2,1)}), bf16[1,64,2176]{2,1,0:T(8,128)(2,1)}) %reduce-scatter.7.cloned.1.call-update) | async-done | bytes 278544 | tf_op jit(solution)/shard_map/reduce_scatter | solution.py:116
  (620 shorter events, 344.0 us)
Async XLA Ops:
  18.3 66.2 %all-gather.15.cloned.1.call-start = ((), (), s32[]{:S(2)}) async-start(), calls=%async_computation.13 | async-start | bytes 1310720 | tf_op jit(solution)/shard_map/all_gather | solution.py:95
  18.4 62.4 %collective-permute-start = (bf16[1024,1024]{1,0:T(8,128)(2,1)}, bf16[1024,1024]{1,0:T(8,128)(2,1)}, u32[]{:S(2)}, u32[]{:S(2)}) collective-permute-start(bf16[1024,1024]{1,0:T(8,128)(2,1)} %bitcast), channel_id=1, source_target_pairs={{0,16},{16,0},{1,17},{17,1},{2,18},{18,2},{3,19},{19,3},{4,20},{20... | collective-permute-start | bytes 6291464 | tf_op jit(solution)/shard_map/ppermute | solution.py:48
  52.5 80.6 %all-gather.17.cloned.1.call-start = ((), (), s32[]{:S(2)}) async-start(), calls=%async_computation.14 | async-start | bytes 1310720 | tf_op jit(solution)/shard_map/all_gather | solution.py:95
  85.1 119.6 %all-gather.19.cloned.1.call-start = ((), (), s32[]{:S(2)}) async-start(), calls=%async_computation.15 | async-start | bytes 1392640 | tf_op jit(solution)/shard_map/all_gather | solution.py:95
  132.6 72.7 %collective-permute-start.6 = (bf16[1024,1024]{1,0:T(8,128)(2,1)}, bf16[1024,1024]{1,0:T(8,128)(2,1)}, u32[]{:S(2)}, u32[]{:S(2)}) collective-permute-start(bf16[1024,1024]{1,0:T(8,128)(2,1)} %convolution_convert_fusion.9), channel_id=1, source_target_pairs={{0,16},{16,0},{1,17},{17,1},{2,18},{18,2},{3,19},{19,3},{4,20},{20... | collective-permute-start | bytes 6291464 | tf_op jit(solution)/shard_map/ppermute | solution.py:48
  133.1 236.8 %all-gather.21.cloned.1.call-start = ((), (), s32[]{:S(2)}) async-start(), calls=%async_computation.16 | async-start | bytes 1310720 | tf_op jit(solution)/shard_map/all_gather | solution.py:344
  135.3 68.0 %collective-permute-start.12 = (bf16[4,128,1024]{2,1,0:T(8,128)(2,1)}, bf16[4,128,1024]{2,1,0:T(8,128)(2,1)S(1)}, u32[]{:S(2)}, u32[]{:S(2)}) collective-permute-start(bf16[4,128,1024]{2,1,0:T(8,128)(2,1)} %bitcast.345), channel_id=1, source_target_pairs={{0,1},{1,0},{2,3},{3,2},{4,5},{5,4},{6,7},{7,6},{8,9},{9,8},{10,11... | collective-permute-start | bytes 3145736 | tf_op jit(solution)/shard_map/ppermute | solution.py:48
  136.0 81.5 %collective-permute-start.13 = (bf16[4,128,1024]{2,1,0:T(8,128)(2,1)}, bf16[4,128,1024]{2,1,0:T(8,128)(2,1)S(1)}, u32[]{:S(2)}, u32[]{:S(2)}) collective-permute-start(bf16[4,128,1024]{2,1,0:T(8,128)(2,1)} %bitcast.346), channel_id=1, source_target_pairs={{0,2},{2,0},{1,3},{3,1},{4,6},{6,4},{5,7},{7,5},{8,10},{10,8},{9,1... | collective-permute-start | bytes 3145736 | tf_op jit(solution)/shard_map/ppermute | solution.py:48
  236.8 77.7 %collective-permute-start.15 = (bf16[1024,1024]{1,0:T(8,128)(2,1)}, bf16[1024,1024]{1,0:T(8,128)(2,1)}, u32[]{:S(2)}, u32[]{:S(2)}) collective-permute-start(bf16[1024,1024]{1,0:T(8,128)(2,1)} %convolution_convert_fusion.8), channel_id=1, source_target_pairs={{0,16},{16,0},{1,17},{17,1},{2,18},{18,2},{3,19},{19,3},{4,20},{20... | collective-permute-start | bytes 6291464 | tf_op jit(solution)/shard_map/ppermute | solution.py:48
  240.3 63.9 %collective-permute-start.16 = (bf16[4,64,2176]{2,1,0:T(8,128)(2,1)S(1)}, bf16[4,64,2176]{2,1,0:T(8,128)(2,1)S(1)}, u32[]{:S(2)}, u32[]{:S(2)}) collective-permute-start(bf16[4,64,2176]{2,1,0:T(8,128)(2,1)S(1)} %bitcast.337), channel_id=1, source_target_pairs={{0,1},{1,0},{2,3},{3,2},{4,5},{5,4},{6,7},{7,6},{8,9},{9,8},{10,11... | collective-permute-start | bytes 3342344 | tf_op jit(solution)/shard_map/ppermute | solution.py:48
  304.0 69.4 %all-gather.23.cloned.1.call-start = ((), (), s32[]{:S(2)}) async-start(), calls=%async_computation.17 | async-start | bytes 1310720 | tf_op jit(solution)/shard_map/all_gather | solution.py:345
  338.8 348.4 %reduce-scatter.13.cloned.1.call-start = ((), (), s32[]{:S(2)}) async-start(), calls=%async_computation.9 | async-start | bytes 1310720 | tf_op jit(solution)/shard_map/reduce_scatter | solution.py:116
  406.3 308.4 %reduce-scatter.17.cloned.1.call-start = ((), (), s32[]{:S(2)}) async-start(), calls=%async_computation.11 | async-start | bytes 1310720 | tf_op jit(solution)/shard_map/reduce_scatter | solution.py:116
  477.0 55.5 %collective-permute-start.38 = (bf16[1024,1024]{1,0:T(8,128)(2,1)}, bf16[1024,1024]{1,0:T(8,128)(2,1)}, u32[]{:S(2)}, u32[]{:S(2)}) collective-permute-start(bf16[1024,1024]{1,0:T(8,128)(2,1)} %convolution_convert_fusion.7), channel_id=1, source_target_pairs={{0,16},{16,0},{1,17},{17,1},{2,18},{18,2},{3,19},{19,3},{4,20},{20... | collective-permute-start | bytes 6291464 | tf_op jit(solution)/shard_map/ppermute | solution.py:48
  503.2 211.5 %reduce-scatter.15.cloned.1.call-start = ((), (), s32[]{:S(2)}) async-start(), calls=%async_computation.10 | async-start | bytes 1310720 | tf_op jit(solution)/shard_map/reduce_scatter | solution.py:116
  503.6 74.3 %collective-permute-start.58 = (bf16[4,128,1024]{2,1,0:T(8,128)(2,1)}, bf16[4,128,1024]{2,1,0:T(8,128)(2,1)}, u32[]{:S(2)}, u32[]{:S(2)}) collective-permute-start(bf16[4,128,1024]{2,1,0:T(8,128)(2,1)} %get-tuple-element.132), channel_id=1, source_target_pairs={{0,2},{2,0},{1,3},{3,1},{4,6},{6,4},{5,7},{7,5},{8,10},{10,8},{9,1... | collective-permute-start | bytes 3145736 | tf_op jit(solution)/shard_map/ppermute | solution.py:48
  504.8 109.6 %collective-permute-start.51 = (bf16[4,64,2048]{2,1,0:T(8,128)(2,1)}, bf16[4,64,2048]{2,1,0:T(8,128)(2,1)}, u32[]{:S(2)}, u32[]{:S(2)}) collective-permute-start(bf16[4,64,2048]{2,1,0:T(8,128)(2,1)} %get-tuple-element.134), channel_id=1, source_target_pairs={{0,1},{1,0},{2,3},{3,2},{4,5},{5,4},{6,7},{7,6},{8,9},{9,8},{10,11... | collective-permute-start | bytes 3145736 | tf_op jit(solution)/shard_map/ppermute | solution.py:48
  508.5 144.4 %collective-permute-start.47 = (bf16[4,64,2176]{2,1,0:T(8,128)(2,1)}, bf16[4,64,2176]{2,1,0:T(8,128)(2,1)}, u32[]{:S(2)}, u32[]{:S(2)}) collective-permute-start(bf16[4,64,2176]{2,1,0:T(8,128)(2,1)} %get-tuple-element.130), channel_id=1, source_target_pairs={{0,1},{1,0},{2,3},{3,2},{4,5},{5,4},{6,7},{7,6},{8,9},{9,8},{10,11... | collective-permute-start | bytes 3342344 | tf_op jit(solution)/shard_map/ppermute | solution.py:48
  528.7 68.4 %collective-permute-start.57 = (bf16[4,128,1024]{2,1,0:T(8,128)(2,1)}, bf16[4,128,1024]{2,1,0:T(8,128)(2,1)}, u32[]{:S(2)}, u32[]{:S(2)}) collective-permute-start(bf16[4,128,1024]{2,1,0:T(8,128)(2,1)} %fusion.29), channel_id=1, source_target_pairs={{0,1},{1,0},{2,3},{3,2},{4,5},{5,4},{6,7},{7,6},{8,9},{9,8},{10,11... | collective-permute-start | bytes 3145736 | tf_op jit(solution)/shard_map/ppermute | solution.py:48
  532.5 82.5 %collective-permute-start.50 = (bf16[4,64,2048]{2,1,0:T(8,128)(2,1)}, bf16[4,64,2048]{2,1,0:T(8,128)(2,1)}, u32[]{:S(2)}, u32[]{:S(2)}) collective-permute-start(bf16[4,64,2048]{2,1,0:T(8,128)(2,1)} %fusion.32), channel_id=1, source_target_pairs={{0,2},{2,0},{1,3},{3,1},{4,6},{6,4},{5,7},{7,5},{8,10},{10,8},{9,1... | collective-permute-start | bytes 3145736 | tf_op jit(solution)/shard_map/ppermute | solution.py:48
  577.9 74.9 %collective-permute-start.46 = (bf16[4,64,2176]{2,1,0:T(8,128)(2,1)}, bf16[4,64,2176]{2,1,0:T(8,128)(2,1)}, u32[]{:S(2)}, u32[]{:S(2)}) collective-permute-start(bf16[4,64,2176]{2,1,0:T(8,128)(2,1)} %fusion.22), channel_id=1, source_target_pairs={{0,2},{2,0},{1,3},{3,1},{4,6},{6,4},{5,7},{7,5},{8,10},{10,8},{9,1... | collective-permute-start | bytes 3342344 | tf_op jit(solution)/shard_map/ppermute | solution.py:48
  600.6 115.2 %reduce-scatter.11.cloned.1.call-start = ((), (), s32[]{:S(2)}) async-start(), calls=%async_computation.8 | async-start | bytes 1310720 | tf_op jit(solution)/shard_map/reduce_scatter | solution.py:116
  618.5 109.5 %reduce-scatter.9.cloned.1.call-start = ((), (), s32[]{:S(2)}) async-start(), calls=%async_computation.7 | async-start | bytes 1392640 | tf_op jit(solution)/shard_map/reduce_scatter | solution.py:116
  656.2 85.3 %reduce-scatter.7.cloned.1.call-start = ((), (), s32[]{:S(2)}) async-start(), calls=%async_computation.6 | async-start | bytes 1392640 | tf_op jit(solution)/shard_map/reduce_scatter | solution.py:116
  (161 other events, 2374.0 us)
Sparse Core Ops, SparseCore 0:
  18.5 31.6 all-gather.12
  52.6 27.0 all-gather.14
  85.3 27.7 all-gather.16
  133.2 27.8 all-gather.18
  304.2 26.5 all-gather.20
  338.9 26.5 all-gather.22
  406.4 25.6 reduce-scatter.12
  503.3 25.8 reduce-scatter.16
  600.7 25.8 reduce-scatter.14
  629.4 25.7 reduce-scatter.10
  657.6 26.8 reduce-scatter.8
  714.8 26.7 reduce-scatter.6

commit v2 on v1

v2 whole, which is shorter than its diff:
```python
import functools

import jax
import jax.numpy as jnp
from jax import lax
from jax.experimental import pallas as pl
from jax.experimental.pallas import tpu as pltpu
from jax.sharding import Mesh
from jax.sharding import PartitionSpec as P

D = 1024
HEADS = 16
HEAD_DIM = 64
FF = 4096
HALF = D // 2
LANES = 128

epsilon = 1e-06
masked_score = -1e30
root_half = 0.7071067811865476
inverse_root_two_pi = 0.3989422804014327

f32 = jnp.float32
bf16 = jnp.bfloat16


def mm(a, b):
    return jnp.dot(a, b, preferred_element_type=f32)


def mm_rows(a, b):
    return lax.dot_general(a, b, (((0,), (0,)), ((), ())), preferred_element_type=f32)


def mm_t(a, b):
    return lax.dot_general(a, b, (((1,), (1,)), ((), ())), preferred_element_type=f32)


def inverse_rms(v):
    return lax.rsqrt(jnp.mean(v * v, axis=-1, keepdims=True) + epsilon)


def norm_back(grad, unit, inverse, gain):
    scaled = grad * gain
    return inverse * (scaled - unit * jnp.mean(scaled * unit, axis=-1, keepdims=True))


def swap(v, axis):
    return lax.ppermute(v, axis, [(0, 1), (1, 0)])


def to_plane(v, j):
    return lax.ppermute(v, ("y", "x"), [(i, i ^ j) for i in range(4)])


def fence(*values):
    return lax.optimization_barrier(values)


def over_z(shard):
    return lax.all_gather(shard, "z", axis=0, tiled=False)


def reduce_z(part):
    return lax.psum_scatter(part, "z", scatter_dimension=0, tiled=False)


light = pl.CostEstimate(flops=1, bytes_accessed=1, transcendentals=0)


near_memory = pl.BlockSpec(memory_space=pltpu.VMEM)
far_memory = pl.BlockSpec(memory_space=pltpu.HBM)


def place_kernel(splits, spans, plane_first, me_ref, *rest):
    pieces = rest[: len(spans)]
    outs, sems = rest[len(spans) : len(spans) + len(splits)], rest[-1]
    me = me_ref[0]
    copies = []
    for p, (src, (j, start, stop)) in enumerate(zip(pieces, spans)):
        for k, (low, high) in enumerate(splits):
            out = outs[k].at[me ^ j, start:stop] if plane_first else outs[k].at[start:stop, me ^ j]
            copies.append(
                pltpu.make_async_copy(src.at[:, :, low:high], out, sems.at[p * len(splits) + k])
            )
    for copy in copies:
        copy.start()
    for copy in copies:
        copy.wait()


def place(me, pieces, spans, splits, plane_first=False):
    depth, rows, _ = pieces[0].shape
    lead = (4, depth) if plane_first else (depth, 4)
    return pl.pallas_call(
        functools.partial(place_kernel, splits, spans, plane_first),
        out_shape=[
            jax.ShapeDtypeStruct((*lead, rows, high - low), bf16) for low, high in splits
        ],
        in_specs=[pl.BlockSpec(memory_space=pltpu.SMEM)] + [far_memory] * len(spans),
        out_specs=[near_memory] * len(splits),
        scratch_shapes=[pltpu.SemaphoreType.DMA((len(spans) * len(splits),))],
        compiler_params=pltpu.CompilerParams(vmem_limit_bytes=24 << 20),
        cost_estimate=light,
    )(jnp.reshape(me, (1,)), *pieces)


def mask_of(seg_col, seg_row, low, start, stop):
    keys = low + lax.broadcasted_iota(jnp.int32, (stop - low, stop - start), 0)
    queries = start + lax.broadcasted_iota(jnp.int32, (stop - low, stop - start), 1)
    return (seg_col[low:stop] == seg_row[:, start:stop]) & (keys <= queries)


def head_lanes(h):
    lane = lax.broadcasted_iota(jnp.int32, (1, LANES), 1)
    return (lane // HEAD_DIM == h).astype(bf16)


def softmax_down(q, k, allowed):
    scores = jnp.where(allowed, mm_t(k, q), masked_score)
    exponent = jnp.exp(scores - jnp.max(scores, axis=0, keepdims=True))
    return exponent / jnp.sum(exponent, axis=0, keepdims=True)


def attend_pair(q, k, v, masks, block):
    scale = jnp.asarray(HEAD_DIM**-0.5, bf16)
    rows = []
    for i, allowed in enumerate(masks):
        low, high = max(0, i - 1) * block, (i + 1) * block
        total = None
        for h in range(2):
            lanes = head_lanes(h)
            probs = softmax_down(q[i * block : high] * (lanes * scale), k[low:high], allowed)
            term = mm_rows(probs.astype(bf16), v[low:high] * lanes)
            total = term if total is None else total + term
        rows.append(total)
    return rows


def attend_pair_back(q, k, v, g, masks, block):
    scale = jnp.asarray(HEAD_DIM**-0.5, bf16)
    dq = []
    dk = [None] * len(masks)
    dv = [None] * len(masks)

    def add(parts, low, high, term):
        for b in range(low, high):
            piece = term[(b - low) * block : (b - low + 1) * block]
            parts[b] = piece if parts[b] is None else parts[b] + piece

    for i, allowed in enumerate(masks):
        first = max(0, i - 1)
        low, high = first * block, (i + 1) * block
        total = None
        for h in range(2):
            lanes = head_lanes(h)
            qh = q[i * block : high] * (lanes * scale)
            gh = g[i * block : high] * lanes
            probs = softmax_down(qh, k[low:high], allowed)
            dp = mm_t(v[low:high], gh)
            add(dv, first, i + 1, mm(probs.astype(bf16), gh))
            inner = jnp.sum(dp * probs, axis=0, keepdims=True)
            ds = (probs * (dp - inner)).astype(bf16)
            term = mm_rows(ds, k[low:high] * (lanes * scale))
            total = term if total is None else total + term
            add(dk, first, i + 1, mm(ds, qh))
        dq.append(total)
    return dq, dk, dv


def masks_for(seg_col, seg_row, length, block):
    return [
        mask_of(seg_col, seg_row, max(0, i - 1) * block, i * block, (i + 1) * block)
        for i in range(length // block)
    ]


def attend_kernel(block, pairs, length, qkv_ref, seg_col_ref, seg_row_ref, o_ref):
    for s in range(seg_col_ref.shape[0]):
        masks = masks_for(seg_col_ref[s], seg_row_ref[s], length, block)
        at = slice(s * length, (s + 1) * length)
        for p in range(pairs):
            cut = lambda t: qkv_ref[at, (t * pairs + p) * LANES : (t * pairs + p + 1) * LANES]
            for i, rows in enumerate(attend_pair(cut(0), cut(1), cut(2), masks, block)):
                low = s * length + i * block
                o_ref[low : low + block, p * LANES : (p + 1) * LANES] = rows.astype(bf16)


def attend_out_kernel(block, pairs, length, qkv_ref, sc_ref, sr_ref, w_ref, o_ref, z_ref):
    attend_kernel(block, pairs, length, qkv_ref, sc_ref, sr_ref, o_ref)
    z_ref[...] = mm(o_ref[...], w_ref[...]).astype(bf16)


def attend_back_out_kernel(
    block, pairs, length, qkv_ref, sc_ref, sr_ref, g_ref, w_ref, d_ref, z_ref
):
    attend_back_kernel(block, pairs, length, qkv_ref, sc_ref, sr_ref, g_ref, d_ref)
    z_ref[...] = mm_t(d_ref[...], w_ref[...]).astype(bf16)


def attend_back_kernel(block, pairs, length, qkv_ref, seg_col_ref, seg_row_ref, g_ref, d_ref):
    for s in range(seg_col_ref.shape[0]):
        masks = masks_for(seg_col_ref[s], seg_row_ref[s], length, block)
        at = slice(s * length, (s + 1) * length)
        for p in range(pairs):
            cut = lambda t: qkv_ref[at, (t * pairs + p) * LANES : (t * pairs + p + 1) * LANES]
            g = g_ref[at, p * LANES : (p + 1) * LANES]
            grads = attend_pair_back(cut(0), cut(1), cut(2), g, masks, block)
            for t, parts in enumerate(grads):
                for i, rows in enumerate(parts):
                    low, lane = s * length + i * block, (t * pairs + p) * LANES
                    d_ref[low : low + block, lane : lane + LANES] = rows.astype(bf16)


def attention_call(kernel, seg, arrays, weights, width):
    count, length = seg.shape
    pairs = arrays[0].shape[1] // (3 * LANES)
    at = lambda columns: pl.BlockSpec((length, columns), lambda s: (s, 0))
    return pl.pallas_call(
        functools.partial(kernel, LANES, pairs, length),
        grid=(count,),
        out_shape=[
            jax.ShapeDtypeStruct((count * length, width), bf16),
            jax.ShapeDtypeStruct((count * length, D), bf16),
        ],
        in_specs=[at(arrays[0].shape[1])]
        + [
            pl.BlockSpec((1, length, 1), lambda s: (s, 0, 0)),
            pl.BlockSpec((1, 1, length), lambda s: (s, 0, 0)),
        ]
        + [at(v.shape[1]) for v in arrays[1:]]
        + [pl.BlockSpec(weights.shape, lambda s: (0, 0))],
        out_specs=[at(width), at(D)],
        compiler_params=pltpu.CompilerParams(vmem_limit_bytes=40 << 20),
        cost_estimate=light,
    )(arrays[0], seg[:, :, None], seg[:, None, :], *arrays[1:], weights)


def attn_grad_kernel(relative, count, me_ref, a_ref, d_ref, *refs):
    beside, refs = refs[:count], refs[count:]
    out = refs[-1] if relative else refs[0]
    product = mm_rows(a_ref[...], d_ref[...]).astype(bf16)
    out[:, :, :, : 3 * HALF] = product.reshape(*out.shape[:3], 3 * HALF)
    low = 3 * HALF
    for ref in beside:
        out[:, :, :, low : low + ref.shape[1]] = ref[...].reshape(*out.shape[:3], ref.shape[1])
        low += ref.shape[1]
    if relative:
        for j in range(4):
            refs[j][...] = out[:, me_ref[0] ^ j]


def attn_grad(me, relative, depth, a, dqkv, *beside):
    tokens, step = a.shape[0], 256
    rows = D // (4 * depth)
    deep = step // (4 * rows)
    width = 3 * HALF + sum(v.shape[1] for v in beside)
    if relative:
        outs = [((depth, rows, width), bf16, pl.BlockSpec((deep, rows, width), lambda i: (i, 0, 0)))]
        outs = outs * 4
    else:
        block = pl.BlockSpec((deep, 4, rows, width), lambda i: (i, 0, 0, 0))
        outs = [((depth, 4, rows, width), bf16, block)]
    return tiled_call(
        functools.partial(attn_grad_kernel, relative, len(beside)),
        D // step,
        outs,
        [
            (jnp.reshape(me, (1,)), pl.BlockSpec(memory_space=pltpu.SMEM)),
            (a, pl.BlockSpec((tokens, step), lambda i: (0, i))),
            (dqkv, resident(dqkv.shape)),
        ]
        + [(v, pl.BlockSpec((step, v.shape[1]), lambda i: (i, 0))) for v in beside],
        [pltpu.VMEM((deep, 4, rows, width), bf16)] if relative else [],
    )


def whole(kernel, outs, scalars, arrays, scratch=(), anywhere=0):
    near = len(arrays) - anywhere
    return pl.pallas_call(
        kernel,
        out_shape=[jax.ShapeDtypeStruct(shape, dtype) for shape, dtype in outs],
        in_specs=[pl.BlockSpec(memory_space=pltpu.SMEM)] * len(scalars)
        + [near_memory] * near
        + [far_memory] * anywhere,
        out_specs=[near_memory] * len(outs),
        scratch_shapes=list(scratch),
        compiler_params=pltpu.CompilerParams(vmem_limit_bytes=40 << 20),
        cost_estimate=light,
    )(*[jnp.reshape(v, (1,)) for v in scalars], *arrays)


def resident(shape):
    return pl.BlockSpec(shape, lambda i: (0, 0), pipeline_mode=pl.Buffered(1))


def tiled_call(kernel, steps, outs, ins, scratch=()):
    return pl.pallas_call(
        kernel,
        grid=(steps,),
        out_shape=[jax.ShapeDtypeStruct(shape, dtype) for shape, dtype, _ in outs],
        in_specs=[spec for _, spec in ins],
        out_specs=[spec for _, _, spec in outs],
        scratch_shapes=list(scratch),
        compiler_params=pltpu.CompilerParams(vmem_limit_bytes=48 << 20),
        cost_estimate=light,
    )(*[v for v, _ in ins])


def copy_weights(spans, low, high, me, pieces, w_ref, sems):
    copies = [
        pltpu.make_async_copy(src.at[:, :, low:high], w_ref.at[start:stop, me ^ j], sems.at[p])
        for p, (src, (j, start, stop)) in enumerate(zip(pieces, spans))
    ]
    for copy in copies:
        copy.start()
    return copies


def qkv_kernel(spans, step, me_ref, x_ref, gain_ref, *rest):
    pieces = rest[: len(spans)]
    w_ref, a_ref, qkv_ref, sems = rest[len(spans) :]
    copies = copy_weights(spans, 0, 3 * HALF, me_ref[0], pieces, w_ref, sems)
    for i in range(0, x_ref.shape[0], step):
        x = x_ref[i : i + step].astype(f32)
        a_ref[i : i + step] = (x * inverse_rms(x) * gain_ref[...]).astype(bf16)
    for copy in copies:
        copy.wait()
    weights = w_ref[...].reshape(D, 3 * HALF)
    for i in range(0, x_ref.shape[0], step):
        qkv_ref[i : i + step] = mm(a_ref[i : i + step], weights).astype(bf16)


def hidden_kernel(x_ref, part_ref, recv_ref, gain_ref, h_ref, m_ref):
    h = x_ref[...].astype(f32) + (part_ref[...].astype(f32) + recv_ref[...].astype(f32))
    h_ref[...] = h
    m_ref[...] = (h * inverse_rms(h) * gain_ref[...]).astype(bf16)


def hidden_rows(x, part, recv, gain, step=256):
    tokens = x.shape[0]
    down = pl.BlockSpec((step, D), lambda i: (i, 0))
    row = pl.BlockSpec((1, D), lambda i: (0, 0))
    return tiled_call(
        hidden_kernel,
        tokens // step,
        [((tokens, D), f32, down), ((tokens, D), bf16, down)],
        [(x, down), (part, down), (recv, down), (gain, row)],
    )


def down_kernel(g_ref, w_ref, out_ref):
    out_ref[...] = mm(g_ref[...], w_ref[...]).astype(bf16)


def down_product(g, w, step=256):
    tokens, width = g.shape
    return tiled_call(
        down_kernel,
        tokens // step,
        [((tokens, D), bf16, pl.BlockSpec((step, D), lambda i: (i, 0)))],
        [(g, pl.BlockSpec((step, width), lambda i: (i, 0))), (w, resident(w.shape))],
    )[0]


def choose_kernel(
    h_ref, part_ref, recv_ref, bias_ref, cot_ref, picked_ref, router_ref, gain_ref, *outs
):
    y_ref, chosen_ref, grad_ref, weight_ref, de_ref, a_ref = outs
    e = part_ref[...].astype(f32) + recv_ref[...].astype(f32) + bias_ref[...]
    y = (h_ref[...] + e).astype(bf16)
    y_ref[...] = y
    picked = picked_ref[0]
    places = lax.broadcasted_iota(jnp.int32, (picked.shape[0], y.shape[0]), 1) == picked
    onehot = places.astype(bf16)
    chosen, grad = mm(onehot, y), mm(onehot, cot_ref[...])
    weight = jax.nn.sigmoid(jnp.sum(chosen * router_ref[...], axis=1, keepdims=True))
    chosen_ref[...] = chosen
    grad_ref[...] = grad
    weight_ref[...] = weight
    de_ref[...] = (weight * grad).astype(bf16)
    a_ref[...] = (chosen * inverse_rms(chosen) * gain_ref[...]).astype(bf16)


def choose_rows(h, part, recv, bias, cot, picked, router, gain):
    micro, count = picked.shape
    tokens = h.shape[0]
    down = pl.BlockSpec((tokens // micro, D), lambda i: (i, 0))
    row = pl.BlockSpec((1, D), lambda i: (0, 0))
    few = lambda width: pl.BlockSpec((count, width), lambda i: (i, 0))
    rows = micro * count
    return tiled_call(
        choose_kernel,
        micro,
        [
            ((tokens, D), bf16, down),
            ((rows, D), f32, few(D)),
            ((rows, D), f32, few(D)),
            ((rows, 1), f32, few(1)),
            ((rows, D), bf16, few(D)),
            ((rows, D), bf16, few(D)),
        ],
        [
            (h, down),
            (part, down),
            (recv, down),
            (bias, row),
            (cot, down),
            (picked[:, :, None], pl.BlockSpec((1, count, 1), lambda i: (i, 0, 0))),
            (router, row),
            (gain, row),
        ],
    )


def last_kernel(part_ref, recv_ref, x_ref, gain_ref, sum_ref, dx_ref, gain_g):
    da = part_ref[...].astype(f32) + recv_ref[...].astype(f32)
    x = x_ref[...].astype(f32)
    inverse = inverse_rms(x)
    unit = x * inverse
    dx_ref[...] = (sum_ref[...] + norm_back(da, unit, inverse, gain_ref[...])).astype(bf16)
    grad = jnp.sum(da * unit, axis=0, keepdims=True)

    @pl.when(pl.program_id(0) == 0)
    def _():
        gain_g[...] = grad

    @pl.when(pl.program_id(0) > 0)
    def _():
        gain_g[...] += grad


def last_rows(part, recv, x, gain, total, step=256):
    tokens = x.shape[0]
    down = pl.BlockSpec((step, D), lambda i: (i, 0))
    row = pl.BlockSpec((1, D), lambda i: (0, 0))
    return tiled_call(
        last_kernel,
        tokens // step,
        [((tokens, D), bf16, down), ((1, D), f32, row)],
        [(part, down), (recv, down), (x, down), (gain, row), (total, down)],
    )


def up_kernel(m_ref, w_ref, b_ref, g_ref, slope_ref):
    u = mm(m_ref[...], w_ref[...]) + b_ref[...]
    bell = 0.5 * (1.0 + lax.erf(u * root_half))
    g_ref[...] = (u * bell).astype(bf16)
    slope_ref[...] = (bell + u * jnp.exp(-0.5 * u * u) * inverse_root_two_pi).astype(bf16)


def up_product(m, w, bias, step=512):
    tokens, width = m.shape[0], w.shape[1]
    across = pl.BlockSpec((tokens, step), lambda i: (0, i))
    return tiled_call(
        up_kernel,
        width // step,
        [((tokens, width), bf16, across)] * 2,
        [
            (m, resident(m.shape)),
            (w, pl.BlockSpec((w.shape[0], step), lambda i: (0, i))),
            (bias, pl.BlockSpec((1, step), lambda i: (0, i))),
        ],
    )


def down_grad_kernel(me_ref, g_ref, d_ref, *outs):
    product = mm_rows(g_ref[...], d_ref[...]).astype(bf16)
    for j, out in enumerate(outs):

        @pl.when(pl.program_id(0) == j)
        def _(out=out):
            out[...] = product.reshape(out.shape)


def down_grad(me, depth, g, d):
    tokens, width = g.shape
    units = width // (4 * depth)
    return pl.pallas_call(
        down_grad_kernel,
        grid_spec=pltpu.PrefetchScalarGridSpec(
            num_scalar_prefetch=1,
            grid=(4,),
            in_specs=[
                pl.BlockSpec((tokens, width // 4), lambda j, me: (0, me[0] ^ j)),
                pl.BlockSpec(d.shape, lambda j, me: (0, 0), pipeline_mode=pl.Buffered(1)),
            ],
            out_specs=[pl.BlockSpec((depth, units, D), lambda j, me: (0, 0, 0))] * 4,
        ),
        out_shape=[jax.ShapeDtypeStruct((depth, units, D), bf16)] * 4,
        compiler_params=pltpu.CompilerParams(vmem_limit_bytes=48 << 20),
        cost_estimate=light,
    )(jnp.reshape(me, (1,)), g, d)


def mlp_back_kernel(me_ref, d_ref, wd_ref, slope_ref, m_ref, wu_ref, *refs):
    gw_refs, (dm_ref, gb_ref, acc, gw) = refs[:4], refs[4:]
    du = (mm_t(d_ref[...], wd_ref[...]) * slope_ref[...].astype(f32)).astype(bf16)
    gb_ref[...] = jnp.sum(du.astype(f32), axis=0, keepdims=True)
    gw[...] = mm_rows(m_ref[...], du).astype(bf16).reshape(gw.shape)
    for j, gw_ref in enumerate(gw_refs):
        gw_ref[...] = gw[:, me_ref[0] ^ j]
    part = mm_t(du, wu_ref[...])
    step, last = pl.program_id(0), pl.num_programs(0) - 1

    @pl.when(step == 0)
    def _():
        acc[...] = part

    @pl.when((step > 0) & (step < last))
    def _():
        acc[...] += part

    @pl.when(step == last)
    def _():
        dm_ref[...] = (acc[...] + part).astype(bf16)


def mlp_back(me, depth, d, w_down, slope, m, w_up, step=512):
    tokens, width = slope.shape
    rows = D // (4 * depth)
    across = pl.BlockSpec((tokens, step), lambda i: (0, i))
    return tiled_call(
        mlp_back_kernel,
        width // step,
        [
            *[
                ((depth, rows, width), bf16, pl.BlockSpec((depth, rows, step), lambda i: (0, 0, i)))
            ]
            * 4,
            ((tokens, D), bf16, pl.BlockSpec((tokens, D), lambda i: (0, 0))),
            ((1, width), f32, pl.BlockSpec((1, step), lambda i: (0, i))),
        ],
        [
            (jnp.reshape(me, (1,)), pl.BlockSpec(memory_space=pltpu.SMEM)),
            (d, resident(d.shape)),
            (w_down, pl.BlockSpec((step, D), lambda i: (i, 0))),
            (slope, across),
            (m, resident(m.shape)),
            (w_up, pl.BlockSpec((D, step), lambda i: (0, i))),
        ],
        [pltpu.VMEM((tokens, D), f32), pltpu.VMEM((depth, 4, rows, step), bf16)],
    )


def norm_back_kernel(
    part_ref, recv_ref, h_ref, gain_ref, gy_ref, w_ref, dz_ref, sum_ref, do_ref, gain_g, bias_g
):
    dm = part_ref[...].astype(f32) + recv_ref[...].astype(f32)
    h, gy = h_ref[...], gy_ref[...].astype(f32)
    inverse = inverse_rms(h)
    unit = h * inverse
    dh = norm_back(dm, unit, inverse, gain_ref[...])
    total = gy + dh
    dz = total.astype(bf16)
    sum_ref[...] = total
    dz_ref[...] = dz
    do_ref[...] = mm_t(dz, w_ref[...]).astype(bf16)
    grads = jnp.sum(dm * unit, axis=0, keepdims=True), jnp.sum(gy, axis=0, keepdims=True)

    @pl.when(pl.program_id(0) == 0)
    def _():
        gain_g[...], bias_g[...] = grads

    @pl.when(pl.program_id(0) > 0)
    def _():
        gain_g[...] += grads[0]
        bias_g[...] += grads[1]


def norm_back_product(part, recv, h, gain, gy, w_out, step=256):
    tokens = part.shape[0]
    down = lambda width: pl.BlockSpec((step, width), lambda i: (i, 0))
    row = pl.BlockSpec((1, D), lambda i: (0, 0))
    return tiled_call(
        norm_back_kernel,
        tokens // step,
        [
            ((tokens, D), bf16, down(D)),
            ((tokens, D), f32, down(D)),
            ((tokens, HALF), bf16, down(HALF)),
            ((1, D), f32, row),
            ((1, D), f32, row),
        ],
        [
            (part, down(D)),
            (recv, down(D)),
            (h, down(D)),
            (gain, row),
            (gy, down(D)),
            (w_out, resident(w_out.shape)),
        ],
    )


def order_rows_kernel(me_ref, *refs):
    for j, ref in enumerate(refs[:-1]):
        refs[-1][me_ref[0] ^ j] = ref[...]


def order_mlp_kernel(me_ref, u0, u1, u2, u3, d_ref, out_ref):
    rows, width = u0.shape
    units = d_ref.shape[0]
    for j, ref in enumerate((u0, u1, u2, u3)):
        start = pl.multiple_of((me_ref[0] ^ j) * rows, rows)
        out_ref[pl.ds(start, rows)] = ref[...]
    for k in range(2):
        low = 4 * rows + k * units
        out_ref[low : low + units] = d_ref[:, k * width : (k + 1) * width]


def order_columns_kernel(me_ref, *refs):
    out_ref = refs[-1]
    width = refs[0].shape[1]
    for j, ref in enumerate(refs[:-1]):
        start = pl.multiple_of((me_ref[0] ^ j) * width, width)
        out_ref[:, pl.ds(start, width)] = ref[...]


def routed_attn_kernel(count, a_ref, seg_col_ref, seg_row_ref, w_ref, qkv_ref, o_ref):
    weights = w_ref[:, :, :, : 3 * HALF].reshape(D, 3 * HALF)
    qkv_ref[...] = mm(a_ref[...], weights).astype(bf16)
    attend_kernel(count, HALF // LANES, count, qkv_ref, seg_col_ref, seg_row_ref, o_ref)


def routed_hidden_kernel(part_ref, recv_ref, chosen_ref, gain_ref, z_ref, h_ref, m_ref):
    z = part_ref[...].astype(f32) + recv_ref[...].astype(f32)
    h = chosen_ref[...] + z
    z_ref[...] = z
    h_ref[...] = h
    m_ref[...] = (h * inverse_rms(h) * gain_ref[...]).astype(bf16)


def routed_mlp_kernel(core_ref, m0, m1, m2, m3, d0, d1, d2, d3, w_ref, b_ref, *rest):
    g_ref, du_ref, keep_ref, send_ref, gb_ref, m_ref, d_ref = rest
    rows = m0.shape[0]
    for j, (m, d) in enumerate(zip((m0, m1, m2, m3), (d0, d1, d2, d3))):
        m_ref[j * rows : (j + 1) * rows] = m[...]
        d_ref[j * rows : (j + 1) * rows] = d[...]
    hidden = w_ref.shape[2]
    own_rows = D // w_ref.shape[0]
    units = (w_ref.shape[1] - own_rows) // 2
    w_up = w_ref[:, :own_rows].reshape(D, hidden)
    w_down = [
        w_ref[:, own_rows + k * units : own_rows + (k + 1) * units].reshape(hidden, hidden)
        for k in range(2)
    ]
    u = mm(m_ref[...], w_up) + b_ref[...]
    bell = 0.5 * (1.0 + lax.erf(u * root_half))
    g = (u * bell).astype(bf16)
    slope = bell + u * jnp.exp(-0.5 * u * u) * inverse_root_two_pi
    dg = mm_t(d_ref[:, :hidden], w_down[0]) + mm_t(d_ref[:, hidden:], w_down[1])
    du = (dg * slope).astype(bf16)
    g_ref[...] = g
    du_ref[...] = du
    gb_ref[...] = jnp.sum(du.astype(f32), axis=0, keepdims=True)
    e = jnp.concatenate([mm(g, w).astype(bf16) for w in w_down], axis=1).reshape(keep_ref.shape)
    dm = mm_t(du, w_up).astype(bf16).reshape(keep_ref.shape)

    @pl.when(core_ref[0] == 0)
    def _():
        keep_ref[...] = e
        send_ref[...] = dm

    @pl.when(core_ref[0] != 0)
    def _():
        keep_ref[...] = dm
        send_ref[...] = e


def routed_grads_kernel(g_ref, d_ref, m_ref, du_ref, out_ref):
    depth, all_rows, hidden = out_ref.shape
    rows = D // depth
    units = (all_rows - rows) // 2
    up = mm_rows(m_ref[...], du_ref[...]).astype(bf16)
    out_ref[:, :rows] = up.reshape(depth, rows, hidden)
    for k in range(2):
        down = mm_rows(g_ref[...], d_ref[:, k * hidden : (k + 1) * hidden]).astype(bf16)
        low = rows + k * units
        out_ref[:, low : low + units] = down.reshape(depth, units, hidden)


def routed_back_kernel(count, core_ref, *refs):
    ins, outs = refs[:13], refs[13:]
    total, crossed, bias, z_ref, chosen_g, weight_ref, h_ref, gain, wo_ref, wq_ref = ins[:10]
    qkv_ref, seg_col_ref, seg_row_ref = ins[10:]
    delta_ref, logit_ref, dh_ref, dz_ref, gain_g, dqkv_ref, da_ref, do_scr = outs
    first = core_ref[0] == 0
    a, b = total[...].astype(f32), crossed[...].astype(f32)
    e = jnp.where(first, a, b) + bias[...]
    dm = jnp.where(first, b, a)
    delta = z_ref[...] + e
    delta_ref[...] = delta
    weight, grad = weight_ref[...], chosen_g[...]
    logit_ref[...] = jnp.sum(grad * delta, axis=1, keepdims=True) * weight * (1.0 - weight)
    h = h_ref[...]
    inverse = inverse_rms(h)
    unit = h * inverse
    gain_g[...] = jnp.sum(dm * unit, axis=0, keepdims=True)
    dh = norm_back(dm, unit, inverse, gain[...])
    dh_ref[...] = dh
    dz = (weight * grad + dh).astype(bf16)
    dz_ref[...] = dz
    do_scr[...] = mm_t(dz, wo_ref[...]).astype(bf16)
    attend_back_kernel(
        count, HALF // LANES, count, qkv_ref, seg_col_ref, seg_row_ref, do_scr, dqkv_ref
    )
    weights = wq_ref[:, :, :, : 3 * HALF].reshape(D, 3 * HALF)
    da_ref[...] = mm_t(dqkv_ref[...], weights).astype(bf16)


def put_rows(base, rows, picked, length):
    places = lax.broadcasted_iota(jnp.int32, (length, picked.shape[1]), 0) == picked
    onehot = places.astype(bf16)
    high = rows.astype(bf16)
    low = (rows - high.astype(f32)).astype(bf16)
    return base.astype(f32) + (mm(onehot, high) + mm(onehot, low))


def routed_out_kernel(
    part_ref, recv_ref, chosen_ref, gain, dh_ref, logit_ref, router, picked_ref, cot_ref, *outs
):
    gy_ref, gain_g, router_g = outs
    da = part_ref[...].astype(f32) + recv_ref[...].astype(f32)
    chosen, logit = chosen_ref[...], logit_ref[...]
    inverse = inverse_rms(chosen)
    unit = chosen * inverse
    gain_g[...] = jnp.sum(da * unit, axis=0, keepdims=True)
    router_g[...] = jnp.sum(logit * chosen, axis=0, keepdims=True)
    rows = dh_ref[...] + norm_back(da, unit, inverse, gain[...]) + logit * router[...]
    micro, count = picked_ref.shape[0], picked_ref.shape[2]
    length = cot_ref.shape[0] // micro
    for s in range(micro):
        at = slice(s * length, (s + 1) * length)
        cut = rows[s * count : (s + 1) * count]
        gy_ref[at] = put_rows(cot_ref[at], cut, picked_ref[s], length).astype(bf16)


def routed_sum_kernel(y_ref, delta_ref, weight_ref, picked_ref, out_ref):
    rows = weight_ref[...] * delta_ref[...]
    micro, count = picked_ref.shape[0], picked_ref.shape[2]
    length = y_ref.shape[0] // micro
    for s in range(micro):
        at = slice(s * length, (s + 1) * length)
        cut = rows[s * count : (s + 1) * count]
        out_ref[at] = put_rows(y_ref[at], cut, picked_ref[s], length).astype(bf16)


def finish_kernel(core_ref, keep_ref, recv_ref, qkv_ref, out_ref):
    keep, recv = keep_ref[...].astype(f32), recv_ref[:, : 4 * HALF].astype(f32)
    first = core_ref[0] == 0
    low, high = jnp.where(first, keep, recv), jnp.where(first, recv, keep)
    for t in range(3):
        qkv_ref[:, t * D : t * D + HALF] = low[:, t * HALF : (t + 1) * HALF]
        qkv_ref[:, t * D + HALF : (t + 1) * D] = high[:, t * HALF : (t + 1) * HALF]
    out_ref[:, :HALF] = low[:, 3 * HALF : 4 * HALF]
    out_ref[:, HALF:] = high[:, 3 * HALF : 4 * HALF]


def shards(
    boundary_in,
    segments,
    routed,
    gain_attn,
    w_qkv,
    w_out,
    gain_mlp,
    w_up,
    b_up,
    w_down,
    b_down,
    router,
):
    core = lax.axis_index("section")
    first = core == 0
    me = 2 * lax.axis_index("y") + lax.axis_index("x")
    depth = lax.axis_size("z")
    rows = w_qkv.shape[1]
    dp = 4 * depth
    units = w_up.shape[2] // dp
    half_units = units // 2
    micro, length = boundary_in.shape[1], boundary_in.shape[3]
    tokens = micro * length

    qkv_halves = w_qkv[0].astype(bf16).reshape(rows, 3, 2, HALF)
    out_halves = w_out[0].astype(bf16).reshape(rows, 2, HALF)
    up_halves = w_up[0].astype(bf16).reshape(rows, depth, 4, 2, half_units)
    down_halves = w_down[0].astype(bf16).reshape(2, half_units, D)
    bias_cols = half_units // rows
    bias_halves = b_up[0].astype(bf16).reshape(2, bias_cols, rows)
    column = lambda v: jnp.pad(v.astype(bf16), (0, rows - v.shape[0]))[:, None]
    small = jnp.concatenate(
        [column(gain_attn[0]), column(gain_mlp[0]), column(b_down[0]), column(router)], axis=1
    )

    def half(h):
        pick = lambda v, axis: lax.dynamic_index_in_dim(v, h, axis=axis, keepdims=False)
        strip = jnp.concatenate([small, pick(bias_halves, 0).T], axis=1)
        strip = jnp.pad(strip, ((0, 0), (0, 8 - strip.shape[1])))
        none = jnp.zeros_like(strip)
        strip = jnp.concatenate(
            [jnp.where(first, strip, none), jnp.where(first, none, strip)], axis=1
        )
        strip = jnp.pad(strip, ((0, 0), (0, LANES - 16)))
        attn = jnp.concatenate(
            [pick(qkv_halves, 2).reshape(rows, 3 * HALF), pick(out_halves, 1), strip], axis=1
        )
        up = pick(up_halves, 3).transpose(0, 2, 1, 3).reshape(rows, D * 2)
        return attn, up, pick(down_halves, 0)

    kept, sent = half(core), half(1 - core)
    came = tuple(swap(v, "section") for v in sent)
    width = 4 * HALF
    shard0 = [jnp.where(first, k, r) for k, r in zip(kept, came)]
    shard1 = [jnp.where(first, r, k) for k, r in zip(kept, came)]
    strip = kept[0][:, width:] + came[0][:, width:]
    shard0[0] = jnp.concatenate([shard0[0][:, :width], strip], axis=1)
    shard1[0] = shard1[0][:, :width]

    mine = boundary_in[0, :, 0].reshape(tokens, D)
    other = swap(mine, "section")
    x_b = jnp.where(first, mine, other)
    cot_b = jnp.where(first, other, mine)
    seg = segments[:, 0]
    picked = routed[:, 0]
    count = picked.shape[1]
    chosen_rows = micro * count

    def whole_out(w_o):
        w_o = w_o.reshape(D, HALF)
        own = lax.dynamic_slice_in_dim(w_o, core * HALF, HALF, axis=0)
        recv = swap(lax.dynamic_slice_in_dim(w_o, (1 - core) * HALF, HALF, axis=0), "section")
        return jnp.concatenate([jnp.where(first, own, recv), jnp.where(first, recv, own)], axis=1)

    halfway = depth // 2

    own_q = over_z(shard0[0])
    rest = [shard1[0]] + [to_plane(shard1[0], j) for j in (1, 2, 3)]
    (rest,) = whole(order_rows_kernel, [((4, rows, width), bf16)], [me], rest)
    hidden = depth * half_units
    pick_up = lambda j: lax.dynamic_slice_in_dim(shard1[1], (me ^ j) * hidden, hidden, axis=1)
    mlp = [pick_up(0)] + [to_plane(pick_up(j), j) for j in (1, 2, 3)]
    mlp_rows = 4 * rows + 2 * half_units
    (mlp,) = whole(order_mlp_kernel, [((mlp_rows, hidden), bf16)], [me], [*mlp, shard1[2]])
    onehot = picked[:, :, None] == lax.broadcasted_iota(jnp.int32, (micro, count, length), 2)
    seg1 = jnp.sum(jnp.where(onehot, seg[:, None, :], 0), axis=2)
    seg1_col, seg1_row = seg1[:, :, None], seg1[:, None, :]
    own_q, rest, mlp, shard_u = fence(own_q, rest, mlp, shard0[1])

    px_q, py_q = swap(own_q, "x"), swap(own_q, "y")
    own_u = over_z(shard_u)
    own_q, px_q, py_q, own_u, shard_d, x_b, cot_b, seg1_col, seg1_row = fence(
        own_q, px_q, py_q, own_u, shard0[2], x_b, cot_b, seg1_col, seg1_row
    )
    pd_q, px_u = swap(px_q, "y"), swap(own_u, "x")
    own_d = over_z(shard_d)
    own_q, px_q, py_q, pd_q, own_u, px_u, own_d, rest = fence(
        own_q, px_q, py_q, pd_q, own_u, px_u, own_d, rest
    )
    py_u = swap(own_u, "y")
    px_d, py_d = swap(own_d, "x"), swap(own_d, "y")
    w_r1 = over_z(rest)

    spans_all = [(j, 0, depth) for j in range(4)]
    w_o0, strip = place(
        me, [own_q, px_q, py_q, pd_q], spans_all, ((3 * HALF, width), (width, width + LANES))
    )
    w_o0 = whole_out(w_o0)
    choose = (
        lax.broadcasted_iota(jnp.int32, (16, LANES), 0)
        == lax.broadcasted_iota(jnp.int32, (16, LANES), 1)
    ).astype(bf16)
    vectors = mm_t(choose, strip.reshape(D, LANES))
    gain_attn0, gain_mlp0, b_down0 = vectors[0:1], vectors[1:2], vectors[2:3]
    gain_attn1, gain_mlp1, b_down1 = vectors[8:9], vectors[9:10], vectors[10:11]
    router_full = jnp.concatenate(
        [vectors[b].reshape(dp, rows)[:, : rows // 2].reshape(1, HALF) for b in (3, 11)], axis=1
    )
    biases = lambda b: (
        vectors[b : b + bias_cols].reshape(bias_cols, depth, 4, rows).transpose(2, 1, 0, 3)
    )
    bias_up0 = biases(4).reshape(1, 2 * D)
    bias_up1 = lax.dynamic_index_in_dim(biases(12), me, axis=0, keepdims=False)
    bias_up1 = bias_up1.reshape(1, hidden)
    w_q0, a0, qkv0 = whole(
        functools.partial(qkv_kernel, spans_all, 256),
        [
            ((depth, 4, rows, 3 * HALF), bf16),
            ((tokens, D), bf16),
            ((tokens, 3 * HALF), bf16),
        ],
        [me],
        [x_b, gain_attn0, own_q, px_q, py_q, pd_q],
        [pltpu.SemaphoreType.DMA((4,))],
        anywhere=4,
    )
    w_q0 = w_q0.reshape(D, 3 * HALF)
    o0, z_part = attention_call(attend_out_kernel, seg, [qkv0], w_o0, HALF)
    o0, z_part, own_u, px_u, py_u, px_d = fence(o0, z_part, own_u, px_u, py_u, px_d)

    pd_u = swap(py_u, "x")
    pd_d0 = swap(px_d[:halfway], "y")
    h0, m0 = hidden_rows(x_b, z_part, swap(z_part, "section"), gain_mlp0)
    m0, pd_u, py_d = fence(m0, pd_u, py_d)

    pd_d1 = swap(py_d[halfway:], "x")
    (w_u0,) = place(me, [own_u, px_u, py_u, pd_u], spans_all, ((0, D * 2),))
    w_u0 = w_u0.reshape(D, D * 2)
    g0, slope0 = up_product(m0, w_u0, bias_up0)
    g0, pd_d0, pd_d1, mlp, w_r1 = fence(g0, pd_d0, pd_d1, mlp, w_r1)

    w_m1 = over_z(mlp)
    spans_cut = spans_all[:3] + [(3, 0, halfway), (3, halfway, depth)]
    (w_d0,) = place(
        me, [own_d, px_d, py_d, pd_d0, pd_d1], spans_cut, ((0, D),), plane_first=True
    )
    w_d0 = w_d0.reshape(D * 2, D)
    e_part = down_product(g0, w_d0)
    w_o1 = whole_out(w_r1[..., 3 * HALF :])

    y0_b, chosen, grad_chosen, weight, de1, a1 = choose_rows(
        h0, e_part, swap(e_part, "section"), b_down0, cot_b, picked, router_full, gain_attn1
    )
    de_all = [de1] + [to_plane(de1, j) for j in (1, 2, 3)]
    qkv1, o1 = whole(
        functools.partial(routed_attn_kernel, count),
        [((chosen_rows, 3 * HALF), bf16), ((chosen_rows, HALF), bf16)],
        [],
        [a1, seg1_col, seg1_row, w_r1],
    )
    de_all, o1, w_o1 = fence(de_all, o1, w_o1)
    z_part = mm(o1, w_o1).astype(bf16)
    z1, h1, m1 = whole(
        routed_hidden_kernel,
        [((chosen_rows, D), f32)] * 2 + [((chosen_rows, D), bf16)],
        [],
        [z_part, swap(z_part, "section"), chosen, gain_mlp1],
    )
    m_all = [m1] + [to_plane(m1, j) for j in (1, 2, 3)]
    g1, du1, keep, send, gb_u1, m_rows, de_rows = whole(
        routed_mlp_kernel,
        [((4 * chosen_rows, hidden), bf16)] * 2
        + [((4, chosen_rows, D), bf16)] * 2
        + [((1, hidden), f32)]
        + [((4 * chosen_rows, D), bf16)] * 2,
        [core],
        [*m_all, *de_all, w_m1, bias_up1],
    )
    plus = lambda *terms: sum(t.astype(f32) for t in terms).astype(bf16)
    summed = plus(keep, swap(send, "section"))
    (gw_m1,) = whole(
        routed_grads_kernel,
        [((depth, mlp_rows, hidden), bf16)],
        [],
        [g1, de_rows, m_rows, du1],
    )
    total = plus(summed[0], *[to_plane(summed[j], j) for j in (1, 2, 3)])
    crossed = swap(total, "section")
    total, crossed, gw_m1 = fence(total, crossed, gw_m1)

    r_m1 = reduce_z(gw_m1)
    delta, grad_logit, dh1, dz1, gg_mlp1, dqkv1, da_part = whole(
        functools.partial(routed_back_kernel, count),
        [
            ((chosen_rows, D), f32),
            ((chosen_rows, 1), f32),
            ((chosen_rows, D), f32),
            ((chosen_rows, D), bf16),
            ((1, D), f32),
            ((chosen_rows, 3 * HALF), bf16),
            ((chosen_rows, D), bf16),
        ],
        [core],
        [
            total,
            crossed,
            b_down1,
            z1,
            grad_chosen,
            weight,
            h1,
            gain_mlp1,
            w_o1,
            w_r1,
            qkv1,
            seg1_col,
            seg1_row,
        ],
        [pltpu.VMEM((chosen_rows, HALF), bf16)],
    )

    def out_by_columns(grad):
        own = lax.dynamic_slice_in_dim(grad, core * HALF, HALF, axis=1)
        recv = swap(lax.dynamic_slice_in_dim(grad, (1 - core) * HALF, HALF, axis=1), "section")
        return jnp.concatenate([jnp.where(first, own, recv), jnp.where(first, recv, own)], axis=0)

    gw_o1 = out_by_columns(mm_rows(o1, dz1).astype(bf16))
    gy0_b, gg_attn1, grad_router = whole(
        routed_out_kernel,
        [((tokens, D), bf16), ((1, D), f32), ((1, D), f32)],
        [],
        [
            da_part,
            swap(da_part, "section"),
            chosen,
            gain_attn1,
            dh1,
            grad_logit,
            router_full,
            picked[:, None, :],
            cot_b,
        ],
    )
    (attn1,) = attn_grad(me, False, depth, a1, dqkv1, gw_o1)
    gw_d0 = down_grad(me, depth, g0, gy0_b)
    gw_d0, attn1, gy0_b, r_m1 = fence(gw_d0, attn1, gy0_b, r_m1)

    r_a1 = reduce_z(attn1)
    diag_d = swap(gw_d0[3], "x")
    *gw_u0, dm_part, gb_u0 = mlp_back(me, depth, gy0_b, w_d0, slope0, m0, w_u0)
    gw_u0, dm_part, gw_d0, diag_d = fence(gw_u0, dm_part, gw_d0, diag_d)

    far_d, diag_u = swap(gw_d0[1], "x"), swap(gw_u0[3], "y")
    sum_d = plus(gw_d0[2], diag_d)
    dz0, gy_dh0, do0, gg_mlp0, g_down0 = norm_back_product(
        dm_part, swap(dm_part, "section"), h0, gain_mlp0, gy0_b, w_o0
    )
    dqkv0, da_part = attention_call(attend_back_out_kernel, seg, [qkv0, do0], w_q0, 3 * HALF)
    gw_o0 = out_by_columns(mm_rows(o0, dz0).astype(bf16))
    far_d, diag_u, sum_d, dqkv0, da_part, gw_o0 = fence(far_d, diag_u, sum_d, dqkv0, da_part, gw_o0)

    near_u, near_d = swap(plus(gw_u0[1], diag_u), "x"), swap(sum_d, "y")
    dx0_b, gg_attn0 = last_rows(da_part, swap(da_part, "section"), x_b, gain_attn0, gy_dh0)
    here = lax.broadcasted_iota(jnp.int32, (depth, 4, bias_cols, rows), 1) == me
    gb_u1 = gb_u1.reshape(depth, 1, bias_cols, rows)
    gb_u1 = jnp.where(here, gb_u1, 0.0).transpose(2, 0, 1, 3).reshape(bias_cols, D)
    gb_u0 = gb_u0.reshape(4, depth, bias_cols, rows).transpose(2, 1, 0, 3).reshape(bias_cols, D)
    router_rows = jnp.pad(
        grad_router.reshape(2, dp, rows // 2), ((0, 0), (0, 0), (0, rows - rows // 2))
    ).reshape(2, D)
    g_down1 = jnp.sum(de1.astype(f32), axis=0, keepdims=True)
    blank = jnp.zeros((4 - bias_cols, D), f32)
    strip = jnp.concatenate(
        [gg_attn0, gg_mlp0, g_down0, router_rows[0:1], gb_u0, blank]
        + [gg_attn1, gg_mlp1, g_down1, router_rows[1:2], gb_u1, blank]
    )
    strip = jnp.pad(strip, ((0, LANES - 16), (0, 0))).T.astype(bf16)
    attn0 = attn_grad(me, True, depth, a0, dqkv0, gw_o0, strip)
    attn0, near_u, near_d, far_d, r_a1 = fence(attn0, near_u, near_d, far_d, r_a1)

    diag_q, far_u = swap(attn0[3], "x"), swap(gw_u0[2], "y")
    r_d0 = reduce_z(plus(gw_d0[0], near_d, far_d))
    (y1_b,) = whole(
        routed_sum_kernel,
        [((tokens, D), bf16)],
        [],
        [y0_b, delta, weight, picked[:, None, :]],
    )
    boundary_out = jnp.where(first, dx0_b, y1_b).reshape(1, micro, 1, length, D)
    boundary_out, diag_q, far_u, r_a1, r_m1 = fence(boundary_out, diag_q, far_u, r_a1, r_m1)

    far_q, near_q = swap(attn0[1], "x"), swap(plus(attn0[2], diag_q), "y")
    r_u0 = reduce_z(plus(gw_u0[0], near_u, far_u))
    part = lambda v, j: lax.dynamic_index_in_dim(v, me ^ j, axis=0, keepdims=False)
    r_a1 = plus(part(r_a1, 0), *[to_plane(part(r_a1, j), j) for j in (1, 2, 3)])
    up = r_m1[: 4 * rows].reshape(4, rows, hidden)
    up = [part(up, 0)] + [to_plane(part(up, j), j) for j in (1, 2, 3)]
    (r_u1,) = whole(order_columns_kernel, [((rows, 2 * D), bf16)], [me], up)
    low = 4 * rows + half_units
    r_d1 = jnp.concatenate([r_m1[4 * rows : low], r_m1[low:]], axis=1)
    far_q, near_q, r_a1, r_u1, r_d1, r_d0 = fence(far_q, near_q, r_a1, r_u1, r_d1, r_d0)
    r_a0 = reduce_z(plus(attn0[0], near_q, far_q))

    def joined(grad0, grad1):
        keep = jnp.where(first, grad0, grad1)
        recv = swap(jnp.where(first, grad1, grad0), "section")
        return jnp.where(first, keep, recv).astype(f32), jnp.where(first, recv, keep).astype(f32)

    low, high = joined(r_d0, r_d1)
    out_down = jnp.concatenate([low, high], axis=0)[None]
    low, high = joined(r_u0, r_u1)
    cut = lambda v: v.reshape(rows, 4, depth, half_units).transpose(0, 2, 1, 3)
    out_up = jnp.stack([cut(low), cut(high)], axis=3).reshape(1, rows, FF)
    r_a0, out_up, out_down, boundary_out = fence(r_a0, out_up, out_down, boundary_out)
    strip = r_a0[:, width:]
    strip_mine = jnp.where(first, strip[:, :8], strip[:, 8:16])
    strip_other = jnp.where(first, strip[:, 8:16], strip[:, :8])
    keep = jnp.where(first, r_a0[:, :width], r_a1)
    send = jnp.where(first, r_a1, r_a0[:, :width])
    pad = lambda v: jnp.pad(v, ((0, 0), (0, LANES - 8)))
    recv = swap(jnp.concatenate([send, pad(strip_other)], axis=1), "section")
    out_qkv, out_out = whole(
        finish_kernel,
        [((rows, 3 * D), f32), ((rows, D), f32)],
        [core],
        [keep, recv],
    )
    small = strip_mine.astype(f32).T
    bias_half = small[4 : 4 + bias_cols]
    bias_other = recv[:, width + 4 : width + 4 + bias_cols].astype(f32).T
    out_b_up = jnp.concatenate(
        [jnp.where(first, bias_half, bias_other), jnp.where(first, bias_other, bias_half)]
    ).reshape(1, units)
    return (
        boundary_out,
        small[0:1],
        out_qkv[None],
        out_out[None],
        small[1:2],
        out_up,
        out_b_up,
        out_down,
        small[2:3],
        small[3, : rows // 2],
    )


def solution(mesh):
    sections, dp = mesh.shape["section"], mesh.shape["dp"]
    grid = Mesh(mesh.devices.reshape(sections, dp // 4, 2, 2), ("section", "z", "y", "x"))
    chips = ("z", "y", "x")
    in_specs = (
        P("section", None, chips, None, None),
        P(None, chips, None),
        P(None, chips, None),
        P("section", chips),
        P("section", chips, None),
        P("section", chips, None),
        P("section", chips),
        P("section", chips, None),
        P("section", chips),
        P("section", chips, None),
        P("section", chips),
        P(("section",) + chips),
    )
    out_specs = (
        P("section", None, chips, None, None),
        P("section", chips),
        P("section", chips, None),
        P("section", chips, None),
        P("section", chips),
        P("section", chips, None),
        P("section", chips),
        P("section", chips, None),
        P("section", chips),
        P(("section",) + chips),
    )
    return jax.shard_map(shards, mesh=grid, in_specs=in_specs, out_specs=out_specs, check_vma=False)
```

time: 770 us -> 541 us (0.70)
  matrix products: 98.7 us -> 2.19 us
  other arithmetic: 135 us -> 38.9 us
  waiting for transfers between devices: 301 us -> 206 us
  Pallas kernels: 68.2 us -> 138 us
  local copies, waits for them, and re-layouts: 91.8 us -> 76.7 us
    ppermute x45 -> x38, waiting for transfers between devices: 187 us -> 91.9 us  [swap(): return lax.ppermute(v, axis, [(0, 1), (1, 0)])]
    pallas_call x8 -> x27, Pallas kernels: 68.2 us -> 138 us  [the longest x9 71.2 us: tiled_call(): pl.pallas_call(kernel, grid=(steps,), out_shape=[jax.ShapeDtypeStruct(sha...]
    concatenate x5 -> x9, other arithmetic: 32.8 us -> 1.29 us  [the longest x1 0.73 us: shards(): shard0[0] = jnp.concatenate([shard0[0][:, :width], strip], axis=1)]
    dot_general x10 -> x1, matrix products: 30.2 us -> 0.17 us  [mm_t(): lax.dot_general(a, b, (((1,), (1,)), ((), ())), preferred_element_type=f32)]
    dot_general x8 -> x1, matrix products: 30.2 us -> 0.31 us  [mm(): return jnp.dot(a, b, preferred_element_type=f32)]
    dot_general x8 -> x2, matrix products: 29 us -> 1.72 us  [mm_rows(): lax.dot_general(a, b, (((0,), (0,)), ((), ())), preferred_element_type=f32)]
    reduce_sum x9 -> x1, other arithmetic: 23.5 us -> 0.06 us  [shards(): g_down1 = jnp.sum(de1.astype(f32), axis=0, keepdims=True)]
    unnamed x250 -> x222, local copies, waits for them, and re-layouts: 32.5 us -> 55.4 us
  transfers between devices with their start and end apart: 72 -> 69, of which waited for: 25 -> 34; matrix products, arithmetic and copies ran while one was open for 37% -> 9% of each run, Pallas kernels for 9% -> 23%
where the time goes in v2:
time: 541 us; the launch traced here: 533 us
  waiting for transfers between devices  206 us (38%)
  Pallas kernels  138 us (26%)
  local copies, waits for them, and re-layouts  76.7 us (14%)
  starting transfers between devices  56.4 us (10%)
  other arithmetic  38.9 us (7%)
  between operations  15.8 us (3%)
    ppermute x38, waiting for transfers between devices, swap(): return lax.ppermute(v, axis, [(0, 1), (1, 0)])  91.9 us
    ppermute x21, waiting for transfers between devices, to_plane(): return lax.ppermute(v, ('y', 'x'), [(i, i ^ j) for i in range(4)])  72 us
    pallas_call x9, Pallas kernels, tiled_call(): pl.pallas_call(kernel, grid=(steps,), out_shape=[jax.ShapeDtypeStruct(sha...  71.2 us
    unnamed x222, local copies, waits for them, and re-layouts  55.4 us
    reduce_scatter x5, waiting for transfers between devices, reduce_z(): return lax.psum_scatter(part, 'z', scatter_dimension=0, tiled=False)  31.9 us
    ppermute x38, starting transfers between devices, swap(): return lax.ppermute(v, axis, [(0, 1), (1, 0)])  29.2 us
    pallas_call x2, Pallas kernels, attention_call(): pl.pallas_call(functools.partial(kernel, LANES, pairs, length), grid=(cou...  28.3 us
    ppermute x21, starting transfers between devices, to_plane(): return lax.ppermute(v, ('y', 'x'), [(i, i ^ j) for i in range(4)])  25.7 us
  transfers between devices with their start and end apart: 69, of which 34 were waited for; matrix products, arithmetic and copies ran while one was open for 9% of the time, Pallas kernels for 23%

profile of v2, /device:TPU:0, one launch (start us, length us, event | category | flops | bytes accessed | tf_op | source)
XLA Modules:
  0.0 533.2 jit_solution(12151781296794802701)
XLA Ops:
  32.6 9.6 %collective-permute-done.7.u3 = bf16[64,512]{1,0:T(8,128)(2,1)S(1)} collective-permute-done((bf16[64,512]{1,0:T(8,128)(2,1)S(1)}, bf16[64,512]{1,0:T(8,128)(2,1)S(1)}, u32[]{:S(2)}, u32[]{:S(2)}) %collective-permute-start.7) | collective-permute-done | bytes 65568 | tf_op jit(solution)/shard_map/ppermute | solution.py:53
  56.9 18.8 %collective-permute-done.10.rest_2_ = bf16[4,64,2176]{2,1,0:T(8,128)(2,1)S(1)} collective-permute-done((bf16[4,64,2176]{2,1,0:T(8,128)(2,1)}, bf16[4,64,2176]{2,1,0:T(8,128)(2,1)S(1)}, u32[]{:S(2)}, u32[]{:S(2)}) %collective-permute-start.10) | collective-permute-done | bytes 1114144 | tf_op jit(solution)/shard_map/ppermute | solution.py:49
  81.9 23.2 %collective-permute-done.13.rest_1_ = bf16[4,64,2048]{2,1,0:T(8,128)(2,1)S(1)} collective-permute-done((bf16[4,64,2048]{2,1,0:T(8,128)(2,1)}, bf16[4,64,2048]{2,1,0:T(8,128)(2,1)S(1)}, u32[]{:S(2)}, u32[]{:S(2)}) %collective-permute-start.13) | collective-permute-done | bytes 1048608 | tf_op jit(solution)/shard_map/ppermute | solution.py:49
  123.0 6.4 %shard_map.198 = (bf16[4,4,64,1536]{3,2,1,0:T(8,128)(2,1)S(1)}, bf16[1024,1024]{1,0:T(8,128)(2,1)S(1)}, bf16[1024,1536]{1,0:T(8,128)(2,1)}) custom-call(s32[1]{0:T(128)} %bitcast.me_ref, bf16[1024,1024]{1,0:T(8,128)(2,1)S(1)} %get-tuple-element.165.x_ref, f32[1,1024]{1,0:T(1,128)S(1)} %get-tuple-element.435.gain_ref, bf16[4,64,2176]{2,1,0:T(8,128)(2,1)S(1)} %bitcast.160, ...), custom_call_target="tpu_custom_call" | custom-call | flops 1 | bytes 1 | tf_op jit(solution)/shard_map/pallas_call | solution.py:280
  133.9 11.1 %shard_map.199 = (bf16[1024,512]{1,0:T(8,128)(2,1)S(1)}, bf16[1024,1024]{1,0:T(8,128)(2,1)S(1)}) custom-call(bf16[1024,1536]{1,0:T(8,128)(2,1)S(1)} %copy-done.8, s32[2,512,1]{2,1,0:T(8,128)S(1)} %copy-done.13, s32[2,1,512]{2,1,0:T(1,128)S(1)} %copy-done.73, bf16[512,1024]{1,0:T(8,128)(2,1)S(1)} %pad_maximum_fusion.w_ref), custom_call_target="tpu_custom_call" | custom-call | flops 1 | bytes 1 | tf_op jit(solution)/shard_map/pallas_call | solution.py:219
  157.9 13.8 %collective-permute-done.19.rest_2_ = bf16[4,128,1024]{2,1,0:T(8,128)(2,1)S(1)} collective-permute-done((bf16[4,128,1024]{2,1,0:T(8,128)(2,1)S(1)}, bf16[4,128,1024]{2,1,0:T(8,128)(2,1)S(1)}, u32[]{:S(2)}, u32[]{:S(2)}) %collective-permute-start.19) | collective-permute-done | bytes 1048608 | tf_op jit(solution)/shard_map/ppermute | solution.py:49
  182.5 10.6 %shard_map.202 = (bf16[1024,2048]{1,0:T(8,128)(2,1)}, bf16[1024,2048]{1,0:T(8,128)(2,1)}) custom-call(bf16[1024,1024]{1,0:T(8,128)(2,1)S(1)} %copy-done.11, bf16[1024,2048]{1,0:T(8,128)(2,1)} %bitcast.150, f32[1,2048]{1,0:T(1,128)S(1)} %reshape.195.b_ref), custom_call_target="tpu_custom_call" | custom-call | flops 1 | bytes 1 | tf_op jit(solution)/shard_map/pallas_call | solution.py:298
  196.9 7.6 %shard_map.204.part_ref = bf16[1024,1024]{1,0:T(8,128)(2,1)S(1)} custom-call(bf16[1024,2048]{1,0:T(8,128)(2,1)} %get-tuple-element.197.g_ref, bf16[2048,1024]{1,0:T(8,128)(2,1)} %bitcast.152), custom_call_target="tpu_custom_call" | custom-call | flops 1 | bytes 1 | tf_op jit(solution)/shard_map/pallas_call | solution.py:298
  224.2 6.0 %collective-permute-done.24.d2 = bf16[128,1024]{1,0:T(8,128)(2,1)S(1)} collective-permute-done((bf16[128,1024]{1,0:T(8,128)(2,1)S(1)}, bf16[128,1024]{1,0:T(8,128)(2,1)S(1)}, u32[]{:S(2)}, u32[]{:S(2)}) %collective-permute-start.24) | collective-permute-done | bytes 262176 | tf_op jit(solution)/shard_map/ppermute | solution.py:53
  237.6 5.8 %collective-permute-done.28.m1 = bf16[128,1024]{1,0:T(8,128)(2,1)} collective-permute-done((bf16[128,1024]{1,0:T(8,128)(2,1)}, bf16[128,1024]{1,0:T(8,128)(2,1)}, u32[]{:S(2)}, u32[]{:S(2)}) %collective-permute-start.28) | collective-permute-done | bytes 262176 | tf_op jit(solution)/shard_map/ppermute | solution.py:53
  265.1 5.7 %collective-permute-done.32 = bf16[128,1024]{1,0:T(8,128)(2,1)S(1)} collective-permute-done((bf16[128,1024]{1,0:T(8,128)(2,1)S(1)}, bf16[128,1024]{1,0:T(8,128)(2,1)S(1)}, u32[]{:S(2)}, u32[]{:S(2)}) %collective-permute-start.32) | collective-permute-done | bytes 262176 | tf_op jit(solution)/shard_map/ppermute | solution.py:53
  270.8 6.0 %collective-permute-done.33 = bf16[128,1024]{1,0:T(8,128)(2,1)S(1)} collective-permute-done((bf16[128,1024]{1,0:T(8,128)(2,1)S(1)}, bf16[128,1024]{1,0:T(8,128)(2,1)S(1)}, u32[]{:S(2)}, u32[]{:S(2)}) %collective-permute-start.33) | collective-permute-done | bytes 262176 | tf_op jit(solution)/shard_map/ppermute | solution.py:53
  297.2 8.5 %shard_map.212 = (bf16[4,128,1024]{2,1,0:T(8,128)(2,1)S(1)}, bf16[4,128,1024]{2,1,0:T(8,128)(2,1)S(1)}, bf16[4,128,1024]{2,1,0:T(8,128)(2,1)S(1)}, bf16[4,128,1024]{2,1,0:T(8,128)(2,1)}) custom-call(s32[1]{0:T(128)} %bitcast.me_ref, bf16[1024,2048]{1,0:T(8,128)(2,1)} %get-tuple-element.197.g_ref, bf16[1024,1024]{1,0:T(8,128)(2,1)} %copy-done.5), custom_call_target="tpu_custom_call" | custom-call | flops 1 | bytes 1 | tf_op jit(solution)/shard_map/pallas_call | solution.py:479
  310.7 11.0 %reduce-scatter.6.cloned.1.call-done = bf16[1,512,512]{2,1,0:T(8,128)(2,1)} async-done(((bf16[4,512,512]{2,1,0:T(8,128)(2,1)}), bf16[1,512,512]{2,1,0:T(8,128)(2,1)}) %reduce-scatter.6.cloned.1.call-update) | async-done | bytes 524304 | tf_op jit(solution)/shard_map/reduce_scatter | solution.py:65
  323.8 21.0 %shard_map.214 = (bf16[4,64,2048]{2,1,0:T(8,128)(2,1)S(1)}, bf16[4,64,2048]{2,1,0:T(8,128)(2,1)S(1)}, bf16[4,64,2048]{2,1,0:T(8,128)(2,1)S(1)}, bf16[4,64,2048]{...) custom-call(s32[1]{0:T(128)} %bitcast.me_ref, bf16[1024,1024]{1,0:T(8,128)(2,1)} %copy-done.5, ...), custom_call_target="tpu_custom_call" | custom-call | flops 1 | bytes 1 | tf_op jit(solution)/shard_map/pallas_call | solution.py:298
  353.0 8.1 %shard_map.215 = (bf16[1024,1024]{1,0:T(8,128)(2,1)S(1)}, f32[1024,1024]{1,0:T(8,128)}, bf16[1024,512]{1,0:T(8,128)(2,1)S(1)}, f32[1,1024]{1,0:T(1,128)S(1)}, f32[1,1024]{1,0:T(1,128)S(1)}) custom-call(bf16[1024,1024]{1,0:T(8,128)(2,1)} %get-tuple-element.256.part_ref, bf16[1024,1024]{1,0:T(8,128)(2,1)} %copy-done.94, ...), custom_call_target="tpu_custom_call" | custom-call | flops 1 | bytes 1 | tf_op jit(solution)/shard_map/pallas_call | solution.py:298
  364.9 17.2 %shard_map.216 = (bf16[1024,1536]{1,0:T(8,128)(2,1)S(1)}, bf16[1024,1024]{1,0:T(8,128)(2,1)S(1)}) custom-call(bf16[1024,1536]{1,0:T(8,128)(2,1)S(1)} %copy-done.9, s32[2,512,1]{2,1,0:T(8,128)S(1)} %copy-done.14, s32[2,1,512]{2,1,0:T(1,128)S(1)} %copy-done.73, bf16[1024,512]{1,0:T(8,128)(2,1)S(1)} %get-tuple-element.257.g_ref, bf16[1024,1536]{1,0:T(8,128)(2,1)S(1)} %bitcast.161), custom_call_target="tpu_custom_call" | custom-call | flops 1 | bytes 1 | tf_op jit(solution)/shard_map/pallas_call | solution.py:219
  391.1 5.3 shard_map.217
  398.1 7.2 %shard_map.218 = (bf16[4,64,2176]{2,1,0:T(8,128)(2,1)S(1)}, bf16[4,64,2176]{2,1,0:T(8,128)(2,1)}, bf16[4,64,2176]{2,1,0:T(8,128)(2,1)S(1)}, bf16[4,64,2176]{2,1,0:T(8,128)(2,1)S(1)}) custom-call(s32[1]{0:T(128)} %bitcast.me_ref, bf16[1024,1024]{1,0:T(8,128)(2,1)} %copy-done.30, bf16[1024,1536]{1,0:T(8,128)(2,1)} %copy-done.25, ...), custom_call_target="tpu_custom_call" | custom-call | flops 1 | bytes 1 | tf_op jit(solution)/shard_map/pallas_call | solution.py:298
  423.9 17.4 %collective-permute-done.48 = bf16[4,64,2048]{2,1,0:T(8,128)(2,1)} collective-permute-done((bf16[4,64,2048]{2,1,0:T(8,128)(2,1)}, bf16[4,64,2048]{2,1,0:T(8,128)(2,1)}, u32[]{:S(2)}, u32[]{:S(2)}) %collective-permute-start.48) | collective-permute-done | bytes 1048608 | tf_op jit(solution)/shard_map/ppermute | solution.py:49
  455.2 13.1 %collective-permute-done.53.refs_1_ = bf16[64,512]{1,0:T(8,128)(2,1)S(1)} collective-permute-done((bf16[64,512]{1,0:T(8,128)(2,1)S(1)}, bf16[64,512]{1,0:T(8,128)(2,1)S(1)}, u32[]{:S(2)}, u32[]{:S(2)}) %collective-permute-start.53) | collective-permute-done | bytes 65568 | tf_op jit(solution)/shard_map/ppermute | solution.py:53
  468.9 11.7 %collective-permute-done.54.refs_2_ = bf16[64,512]{1,0:T(8,128)(2,1)S(1)} collective-permute-done((bf16[64,512]{1,0:T(8,128)(2,1)S(1)}, bf16[64,512]{1,0:T(8,128)(2,1)S(1)}, u32[]{:S(2)}, u32[]{:S(2)}) %collective-permute-start.54) | collective-permute-done | bytes 65568 | tf_op jit(solution)/shard_map/ppermute | solution.py:53
  482.8 6.9 %collective-permute-done.51 = bf16[64,2048]{1,0:T(8,128)(2,1)S(1)} collective-permute-done((bf16[64,2048]{1,0:T(8,128)(2,1)S(1)}, bf16[64,2048]{1,0:T(8,128)(2,1)S(1)}, u32[]{:S(2)}, u32[]{:S(2)}) %collective-permute-start.51) | collective-permute-done | bytes 262176 | tf_op jit(solution)/shard_map/ppermute | solution.py:53
  498.8 20.9 %reduce-scatter.12.cloned.1.call-done = bf16[1,64,2176]{2,1,0:T(8,128)(2,1)} async-done(((bf16[4,64,2176]{2,1,0:T(8,128)(2,1)}), bf16[1,64,2176]{2,1,0:T(8,128)(2,1)}) %reduce-scatter.12.cloned.1.call-update) | async-done | bytes 278544 | tf_op jit(solution)/shard_map/reduce_scatter | solution.py:65
  (517 shorter events, 244.6 us)
Async XLA Ops:
  7.2 42.1 %all-gather.11.cloned.1.call-start = ((), (), s32[]{:S(2)}) async-start(), calls=%async_computation.10 | async-start | bytes 1392640 | tf_op jit(solution)/shard_map/all_gather | solution.py:61
  17.5 61.4 %all-gather.13.cloned.1.call-start = ((), (), s32[]{:S(2)}) async-start(), calls=%async_computation.11 | async-start | bytes 1310720 | tf_op jit(solution)/shard_map/all_gather | solution.py:61
  19.8 33.3 %collective-permute-start.11 = (bf16[1024,1024]{1,0:T(8,128)(2,1)}, bf16[1024,1024]{1,0:T(8,128)(2,1)}, u32[]{:S(2)}, u32[]{:S(2)}) collective-permute-start(bf16[1024,1024]{1,0:T(8,128)(2,1)} %bitcast.182), channel_id=1, source_target_pairs={{0,16},{16,0},{1,17},{17,1},{2,18},{18,2},{3,19},{19,3},{4,20},{20... | collective-permute-start | bytes 6291464 | tf_op jit(solution)/shard_map/ppermute | solution.py:49
  49.3 59.2 %all-gather.15.cloned.1.call-start = ((), (), s32[]{:S(2)}) async-start(), calls=%async_computation.12 | async-start | bytes 1310720 | tf_op jit(solution)/shard_map/all_gather | solution.py:61
  49.3 26.4 %collective-permute-start.10 = (bf16[4,64,2176]{2,1,0:T(8,128)(2,1)}, bf16[4,64,2176]{2,1,0:T(8,128)(2,1)S(1)}, u32[]{:S(2)}, u32[]{:S(2)}) collective-permute-start(bf16[4,64,2176]{2,1,0:T(8,128)(2,1)} %bitcast.157), channel_id=1, source_target_pairs={{0,2},{2,0},{1,3},{3,1},{4,6},{6,4},{5,7},{7,5},{8,10},{10,8},{9,1... | collective-permute-start | bytes 3342344 | tf_op jit(solution)/shard_map/ppermute | solution.py:49
  50.9 26.2 %collective-permute-start.9 = (bf16[4,64,2176]{2,1,0:T(8,128)(2,1)}, bf16[4,64,2176]{2,1,0:T(8,128)(2,1)}, u32[]{:S(2)}, u32[]{:S(2)}) collective-permute-start(bf16[4,64,2176]{2,1,0:T(8,128)(2,1)} %bitcast.158), channel_id=1, source_target_pairs={{0,1},{1,0},{2,3},{3,2},{4,5},{5,4},{6,7},{7,6},{8,9},{9,8},{10,11... | collective-permute-start | bytes 3342344 | tf_op jit(solution)/shard_map/ppermute | solution.py:49
  78.9 114.3 %all-gather.17.cloned.1.call-start = ((), (), s32[]{:S(2)}) async-start(), calls=%async_computation.13 | async-start | bytes 5242880 | tf_op jit(solution)/shard_map/all_gather | solution.py:61
  78.9 27.2 %collective-permute-start.12 = (bf16[4,64,2176]{2,1,0:T(8,128)(2,1)}, bf16[4,64,2176]{2,1,0:T(8,128)(2,1)S(1)}, u32[]{:S(2)}, u32[]{:S(2)}) collective-permute-start(bf16[4,64,2176]{2,1,0:T(8,128)(2,1)} %collective-permute-done.9.rest_1_), channel_id=1, source_target_pairs={{0,2},{2,0},{1,3},{3,1},{4,6},{6,4},{5,7},{7,5},{8,10},{10,8},{9,1... | collective-permute-start | bytes 3342344 | tf_op jit(solution)/shard_map/ppermute | solution.py:49
  108.5 141.5 %all-gather.19.cloned.1.call-start = ((), (), s32[]{:S(2)}) async-start(), calls=%async_computation.14 | async-start | bytes 2621440 | tf_op jit(solution)/shard_map/all_gather | solution.py:61
  108.5 36.6 %collective-permute-start.15 = (bf16[4,64,2048]{2,1,0:T(8,128)(2,1)}, bf16[4,64,2048]{2,1,0:T(8,128)(2,1)}, u32[]{:S(2)}, u32[]{:S(2)}) collective-permute-start(bf16[4,64,2048]{2,1,0:T(8,128)(2,1)} %bitcast.164), channel_id=1, source_target_pairs={{0,2},{2,0},{1,3},{3,1},{4,6},{6,4},{5,7},{7,5},{8,10},{10,8},{9,1... | collective-permute-start | bytes 3145736 | tf_op jit(solution)/shard_map/ppermute | solution.py:49
  110.1 35.1 %collective-permute-start.16 = (bf16[4,128,1024]{2,1,0:T(8,128)(2,1)}, bf16[4,128,1024]{2,1,0:T(8,128)(2,1)}, u32[]{:S(2)}, u32[]{:S(2)}) collective-permute-start(bf16[4,128,1024]{2,1,0:T(8,128)(2,1)} %bitcast.166), channel_id=1, source_target_pairs={{0,1},{1,0},{2,3},{3,2},{4,5},{5,4},{6,7},{7,6},{8,9},{9,8},{10,11... | collective-permute-start | bytes 3145736 | tf_op jit(solution)/shard_map/ppermute | solution.py:49
  148.8 44.3 %collective-permute-start.20 = (bf16[2,128,1024]{2,1,0:T(8,128)(2,1)}, bf16[2,128,1024]{2,1,0:T(8,128)(2,1)}, u32[]{:S(2)}, u32[]{:S(2)}) collective-permute-start(bf16[2,128,1024]{2,1,0:T(8,128)(2,1)} %slice.128), channel_id=1, source_target_pairs={{0,2},{2,0},{1,3},{3,1},{4,6},{6,4},{5,7},{7,5},{8,10},{10,8},{9,1... | collective-permute-start | bytes 1572872 | tf_op jit(solution)/shard_map/ppermute | solution.py:49
  204.6 117.1 %reduce-scatter.6.cloned.1.call-start = ((), (), s32[]{:S(2)}) async-start(), calls=%async_computation.5 | async-start | bytes 2621440 | tf_op jit(solution)/shard_map/reduce_scatter | solution.py:65
  279.7 132.6 %reduce-scatter.8.cloned.1.call-start = ((), (), s32[]{:S(2)}) async-start(), calls=%async_computation.6 | async-start | bytes 5242880 | tf_op jit(solution)/shard_map/reduce_scatter | solution.py:65
  321.7 168.1 %reduce-scatter.10.cloned.1.call-start = ((), (), s32[]{:S(2)}) async-start(), calls=%async_computation.7 | async-start | bytes 1310720 | tf_op jit(solution)/shard_map/reduce_scatter | solution.py:65
  347.3 36.5 %collective-permute-start.39 = (bf16[4,128,1024]{2,1,0:T(8,128)(2,1)S(1)}, bf16[4,128,1024]{2,1,0:T(8,128)(2,1)S(1)}, u32[]{:S(2)}, u32[]{:S(2)}) collective-permute-start(bf16[4,128,1024]{2,1,0:T(8,128)(2,1)S(1)} %copy-done.91), channel_id=1, source_target_pairs={{0,1},{1,0},{2,3},{3,2},{4,5},{5,4},{6,7},{7,6},{8,9},{9,8},{10,11... | collective-permute-start | bytes 3145736 | tf_op jit(solution)/shard_map/ppermute | solution.py:49
  348.8 35.0 %collective-permute-start.40 = (bf16[4,64,2048]{2,1,0:T(8,128)(2,1)S(1)}, bf16[4,64,2048]{2,1,0:T(8,128)(2,1)S(1)}, u32[]{:S(2)}, u32[]{:S(2)}) collective-permute-start(bf16[4,64,2048]{2,1,0:T(8,128)(2,1)S(1)} %get-tuple-element.253), channel_id=1, source_target_pairs={{0,2},{2,0},{1,3},{3,1},{4,6},{6,4},{5,7},{7,5},{8,10},{10,8},{9,1... | collective-permute-start | bytes 3145736 | tf_op jit(solution)/shard_map/ppermute | solution.py:49
  415.9 76.8 %reduce-scatter.14.cloned.1.call-start = ((), (), s32[]{:S(2)}) async-start(), calls=%async_computation.9 | async-start | bytes 1310720 | tf_op jit(solution)/shard_map/reduce_scatter | solution.py:65
  416.2 27.9 %collective-permute-start.47 = (bf16[4,64,2176]{2,1,0:T(8,128)(2,1)}, bf16[4,64,2176]{2,1,0:T(8,128)(2,1)}, u32[]{:S(2)}, u32[]{:S(2)}) collective-permute-start(bf16[4,64,2176]{2,1,0:T(8,128)(2,1)} %copy-done.88), channel_id=1, source_target_pairs={{0,1},{1,0},{2,3},{3,2},{4,5},{5,4},{6,7},{7,6},{8,9},{9,8},{10,11... | collective-permute-start | bytes 3342344 | tf_op jit(solution)/shard_map/ppermute | solution.py:49
  422.6 67.3 %collective-permute-start.46 = (bf16[4,64,2176]{2,1,0:T(8,128)(2,1)}, bf16[4,64,2176]{2,1,0:T(8,128)(2,1)}, u32[]{:S(2)}, u32[]{:S(2)}) collective-permute-start(bf16[4,64,2176]{2,1,0:T(8,128)(2,1)} %get-tuple-element.285), channel_id=1, source_target_pairs={{0,1},{1,0},{2,3},{3,2},{4,5},{5,4},{6,7},{7,6},{8,9},{9,8},{10,11... | collective-permute-start | bytes 3342344 | tf_op jit(solution)/shard_map/ppermute | solution.py:49
  447.3 72.4 %reduce-scatter.12.cloned.1.call-start = ((), (), s32[]{:S(2)}) async-start(), calls=%async_computation.8 | async-start | bytes 1392640 | tf_op jit(solution)/shard_map/reduce_scatter | solution.py:65
  450.0 39.9 %collective-permute-start.49 = (bf16[4,64,2176]{2,1,0:T(8,128)(2,1)}, bf16[4,64,2176]{2,1,0:T(8,128)(2,1)S(1)}, u32[]{:S(2)}, u32[]{:S(2)}) collective-permute-start(bf16[4,64,2176]{2,1,0:T(8,128)(2,1)} %add_convert_fusion.1), channel_id=1, source_target_pairs={{0,2},{2,0},{1,3},{3,1},{4,6},{6,4},{5,7},{7,5},{8,10},{10,8},{9,1... | collective-permute-start | bytes 3342344 | tf_op jit(solution)/shard_map/ppermute | solution.py:49
  452.2 28.4 %collective-permute-start.54 = (bf16[64,512]{1,0:T(8,128)(2,1)S(1)}, bf16[64,512]{1,0:T(8,128)(2,1)S(1)}, u32[]{:S(2)}, u32[]{:S(2)}) collective-permute-start(bf16[64,512]{1,0:T(8,128)(2,1)S(1)} %get-tuple-element.419), channel_id=1, source_target_pairs={{0,2},{1,3},{2,0},{3,1},{4,6},{5,7},{6,4},{7,5},{8,10},{9,11},{10,... | collective-permute-start | bytes 196616 | tf_op jit(solution)/shard_map/ppermute | solution.py:53
  452.7 29.2 %collective-permute-start.55 = (bf16[64,512]{1,0:T(8,128)(2,1)S(1)}, bf16[64,512]{1,0:T(8,128)(2,1)S(1)}, u32[]{:S(2)}, u32[]{:S(2)}) collective-permute-start(bf16[64,512]{1,0:T(8,128)(2,1)S(1)} %get-tuple-element.418), channel_id=1, source_target_pairs={{0,3},{1,2},{2,1},{3,0},{4,7},{5,6},{6,5},{7,4},{8,11},{9,10},{10,... | collective-permute-start | bytes 196616 | tf_op jit(solution)/shard_map/ppermute | solution.py:53
  (151 other events, 1128.2 us)
Sparse Core Ops, SparseCore 0:
  17.6 31.6 all-gather.10
  51.4 27.3 all-gather.12
  81.0 27.4 all-gather.14
  109.9 80.2 all-gather.16
  204.8 45.1 all-gather.18
  279.8 41.8 reduce-scatter.5
  324.1 76.0 reduce-scatter.7
  416.1 25.7 reduce-scatter.9
  447.4 25.7 reduce-scatter.13
  492.7 26.8 reduce-scatter.11

commit v3 on v2

--- a/solution.py
+++ b/solution.py
@@ -65,6 +65,7 @@
     return lax.psum_scatter(part, "z", scatter_dimension=0, tiled=False)
 
 
+mark = ((8, LANES), f32)
 light = pl.CostEstimate(flops=1, bytes_accessed=1, transcendentals=0)
 
 
@@ -100,7 +101,7 @@
         in_specs=[pl.BlockSpec(memory_space=pltpu.SMEM)] + [far_memory] * len(spans),
         out_specs=[near_memory] * len(splits),
         scratch_shapes=[pltpu.SemaphoreType.DMA((len(spans) * len(splits),))],
-        compiler_params=pltpu.CompilerParams(vmem_limit_bytes=24 << 20),
+        compiler_params=pltpu.CompilerParams(vmem_limit_bytes=16 << 20),
         cost_estimate=light,
     )(jnp.reshape(me, (1,)), *pieces)
 
@@ -108,16 +109,24 @@
 def mask_of(seg_col, seg_row, low, start, stop):
     keys = low + lax.broadcasted_iota(jnp.int32, (stop - low, stop - start), 0)
     queries = start + lax.broadcasted_iota(jnp.int32, (stop - low, stop - start), 1)
-    return (seg_col[low:stop] == seg_row[:, start:stop]) & (keys <= queries)
-
-
-def head_lanes(h):
+    allowed = (seg_col[low:stop] == seg_row[:, start:stop]) & (keys <= queries)
+    return allowed.astype(jnp.int32)
+
+
+def both_heads(v):
     lane = lax.broadcasted_iota(jnp.int32, (1, LANES), 1)
-    return (lane // HEAD_DIM == h).astype(bf16)
+    upper = (lane >= HEAD_DIM).astype(bf16)
+    return jnp.concatenate([v * (1 - upper), v * upper], axis=0)
+
+
+def merged_heads(v):
+    half = v.shape[0] // 2
+    lane = lax.broadcasted_iota(jnp.int32, (1, LANES), 1)
+    return jnp.where(lane < HEAD_DIM, v[:half], v[half:])
 
 
 def softmax_down(q, k, allowed):
-    scores = jnp.where(allowed, mm_t(k, q), masked_score)
+    scores = jnp.where(allowed != 0, mm_t(k, q), masked_score)
     exponent = jnp.exp(scores - jnp.max(scores, axis=0, keepdims=True))
     return exponent / jnp.sum(exponent, axis=0, keepdims=True)
 
@@ -127,13 +136,8 @@
     rows = []
     for i, allowed in enumerate(masks):
         low, high = max(0, i - 1) * block, (i + 1) * block
-        total = None
-        for h in range(2):
-            lanes = head_lanes(h)
-            probs = softmax_down(q[i * block : high] * (lanes * scale), k[low:high], allowed)
-            term = mm_rows(probs.astype(bf16), v[low:high] * lanes)
-            total = term if total is None else total + term
-        rows.append(total)
+        probs = softmax_down(both_heads(q[i * block : high] * scale), k[low:high], allowed)
+        rows.append(merged_heads(mm_rows(probs.astype(bf16), v[low:high])))
     return rows
 
 
@@ -151,28 +155,23 @@
     for i, allowed in enumerate(masks):
         first = max(0, i - 1)
         low, high = first * block, (i + 1) * block
-        total = None
-        for h in range(2):
-            lanes = head_lanes(h)
-            qh = q[i * block : high] * (lanes * scale)
-            gh = g[i * block : high] * lanes
-            probs = softmax_down(qh, k[low:high], allowed)
-            dp = mm_t(v[low:high], gh)
-            add(dv, first, i + 1, mm(probs.astype(bf16), gh))
-            inner = jnp.sum(dp * probs, axis=0, keepdims=True)
-            ds = (probs * (dp - inner)).astype(bf16)
-            term = mm_rows(ds, k[low:high] * (lanes * scale))
-            total = term if total is None else total + term
-            add(dk, first, i + 1, mm(ds, qh))
-        dq.append(total)
+        qh, gh = both_heads(q[i * block : high] * scale), both_heads(g[i * block : high])
+        probs = softmax_down(qh, k[low:high], allowed)
+        dp = mm_t(v[low:high], gh)
+        add(dv, first, i + 1, mm(probs.astype(bf16), gh))
+        inner = jnp.sum(dp * probs, axis=0, keepdims=True)
+        ds = (probs * (dp - inner)).astype(bf16)
+        dq.append(merged_heads(mm_rows(ds, k[low:high] * scale)))
+        add(dk, first, i + 1, mm(ds, qh))
     return dq, dk, dv
 
 
 def masks_for(seg_col, seg_row, length, block):
-    return [
+    masks = [
         mask_of(seg_col, seg_row, max(0, i - 1) * block, i * block, (i + 1) * block)
         for i in range(length // block)
     ]
+    return [jnp.concatenate([m, m], axis=1) for m in masks]
 
 
 def attend_kernel(block, pairs, length, qkv_ref, seg_col_ref, seg_row_ref, o_ref):
@@ -192,10 +191,21 @@
 
 
 def attend_back_out_kernel(
-    block, pairs, length, qkv_ref, sc_ref, sr_ref, g_ref, w_ref, d_ref, z_ref
+    block, pairs, length, qkv_ref, sc_ref, sr_ref, g_ref, x_ref, w_ref, d_ref, z_ref, gain_g
 ):
     attend_back_kernel(block, pairs, length, qkv_ref, sc_ref, sr_ref, g_ref, d_ref)
-    z_ref[...] = mm_t(d_ref[...], w_ref[...]).astype(bf16)
+    da = mm_t(d_ref[...], w_ref[...])
+    z_ref[...] = da.astype(bf16)
+    x = x_ref[...].astype(f32)
+    grad = jnp.sum(da * (x * inverse_rms(x)), axis=0, keepdims=True)
+
+    @pl.when(pl.program_id(0) == 0)
+    def _():
+        gain_g[...] = grad
+
+    @pl.when(pl.program_id(0) > 0)
+    def _():
+        gain_g[...] += grad
 
 
 def attend_back_kernel(block, pairs, length, qkv_ref, seg_col_ref, seg_row_ref, g_ref, d_ref):
@@ -212,7 +222,7 @@
                     d_ref[low : low + block, lane : lane + LANES] = rows.astype(bf16)
 
 
-def attention_call(kernel, seg, arrays, weights, width):
+def attention_call(kernel, seg, arrays, weights, width, sums=0):
     count, length = seg.shape
     pairs = arrays[0].shape[1] // (3 * LANES)
     at = lambda columns: pl.BlockSpec((length, columns), lambda s: (s, 0))
@@ -222,7 +232,8 @@
         out_shape=[
             jax.ShapeDtypeStruct((count * length, width), bf16),
             jax.ShapeDtypeStruct((count * length, D), bf16),
-        ],
+        ]
+        + [jax.ShapeDtypeStruct((1, D), f32)] * sums,
         in_specs=[at(arrays[0].shape[1])]
         + [
             pl.BlockSpec((1, length, 1), lambda s: (s, 0, 0)),
@@ -230,8 +241,8 @@
         ]
         + [at(v.shape[1]) for v in arrays[1:]]
         + [pl.BlockSpec(weights.shape, lambda s: (0, 0))],
-        out_specs=[at(width), at(D)],
-        compiler_params=pltpu.CompilerParams(vmem_limit_bytes=40 << 20),
+        out_specs=[at(width), at(D)] + [pl.BlockSpec((1, D), lambda s: (0, 0))] * sums,
+        compiler_params=pltpu.CompilerParams(vmem_limit_bytes=16 << 20),
         cost_estimate=light,
     )(arrays[0], seg[:, :, None], seg[:, None, :], *arrays[1:], weights)
 
@@ -245,23 +256,28 @@
     for ref in beside:
         out[:, :, :, low : low + ref.shape[1]] = ref[...].reshape(*out.shape[:3], ref.shape[1])
         low += ref.shape[1]
-    if relative:
-        for j in range(4):
-            refs[j][...] = out[:, me_ref[0] ^ j]
+    for h in range(2 if relative else 0):
+
+        @pl.when(pl.program_id(0) // 2 == h)
+        def _(h=h):
+            for j in range(4):
+                refs[2 * j + h][...] = out[:, me_ref[0] ^ j]
 
 
 def attn_grad(me, relative, depth, a, dqkv, *beside):
-    tokens, step = a.shape[0], 256
+    tokens, step = a.shape[0], D // 4
     rows = D // (4 * depth)
     deep = step // (4 * rows)
     width = 3 * HALF + sum(v.shape[1] for v in beside)
     if relative:
-        outs = [((depth, rows, width), bf16, pl.BlockSpec((deep, rows, width), lambda i: (i, 0, 0)))]
-        outs = outs * 4
+        half = lambda h: pl.BlockSpec(
+            (deep, rows, width), lambda i: (jnp.clip(i - 2 * h, 0, 1), 0, 0)
+        )
+        outs = [((depth // 2, rows, width), bf16, half(h)) for _ in range(4) for h in range(2)]
     else:
         block = pl.BlockSpec((deep, 4, rows, width), lambda i: (i, 0, 0, 0))
         outs = [((depth, 4, rows, width), bf16, block)]
-    return tiled_call(
+    found = tiled_call(
         functools.partial(attn_grad_kernel, relative, len(beside)),
         D // step,
         outs,
@@ -273,6 +289,11 @@
         + [(v, pl.BlockSpec((step, v.shape[1]), lambda i: (i, 0))) for v in beside],
         [pltpu.VMEM((deep, 4, rows, width), bf16)] if relative else [],
     )
+    return pairs_of(found) if relative else found[0]
+
+
+def pairs_of(arrays):
+    return [tuple(arrays[2 * j : 2 * j + 2]) for j in range(len(arrays) // 2)]
 
 
 def whole(kernel, outs, scalars, arrays, scratch=(), anywhere=0):
@@ -285,7 +306,7 @@
         + [far_memory] * anywhere,
         out_specs=[near_memory] * len(outs),
         scratch_shapes=list(scratch),
-        compiler_params=pltpu.CompilerParams(vmem_limit_bytes=40 << 20),
+        compiler_params=pltpu.CompilerParams(vmem_limit_bytes=16 << 20),
         cost_estimate=light,
     )(*[jnp.reshape(v, (1,)) for v in scalars], *arrays)
 
@@ -302,7 +323,7 @@
         in_specs=[spec for _, spec in ins],
         out_specs=[spec for _, _, spec in outs],
         scratch_shapes=list(scratch),
-        compiler_params=pltpu.CompilerParams(vmem_limit_bytes=48 << 20),
+        compiler_params=pltpu.CompilerParams(vmem_limit_bytes=20 << 20),
         cost_estimate=light,
     )(*[v for v, _ in ins])
 
@@ -375,8 +396,8 @@
     onehot = places.astype(bf16)
     chosen, grad = mm(onehot, y), mm(onehot, cot_ref[...])
     weight = jax.nn.sigmoid(jnp.sum(chosen * router_ref[...], axis=1, keepdims=True))
-    chosen_ref[...] = chosen
-    grad_ref[...] = grad
+    chosen_ref[...] = chosen.astype(bf16)
+    grad_ref[...] = grad.astype(bf16)
     weight_ref[...] = weight
     de_ref[...] = (weight * grad).astype(bf16)
     a_ref[...] = (chosen * inverse_rms(chosen) * gain_ref[...]).astype(bf16)
@@ -394,8 +415,8 @@
         micro,
         [
             ((tokens, D), bf16, down),
-            ((rows, D), f32, few(D)),
-            ((rows, D), f32, few(D)),
+            ((rows, D), bf16, few(D)),
+            ((rows, D), bf16, few(D)),
             ((rows, 1), f32, few(1)),
             ((rows, D), bf16, few(D)),
             ((rows, D), bf16, few(D)),
@@ -413,21 +434,12 @@
     )
 
 
-def last_kernel(part_ref, recv_ref, x_ref, gain_ref, sum_ref, dx_ref, gain_g):
+def last_kernel(part_ref, recv_ref, x_ref, gain_ref, sum_ref, dx_ref):
     da = part_ref[...].astype(f32) + recv_ref[...].astype(f32)
     x = x_ref[...].astype(f32)
     inverse = inverse_rms(x)
     unit = x * inverse
     dx_ref[...] = (sum_ref[...] + norm_back(da, unit, inverse, gain_ref[...])).astype(bf16)
-    grad = jnp.sum(da * unit, axis=0, keepdims=True)
-
-    @pl.when(pl.program_id(0) == 0)
-    def _():
-        gain_g[...] = grad
-
-    @pl.when(pl.program_id(0) > 0)
-    def _():
-        gain_g[...] += grad
 
 
 def last_rows(part, recv, x, gain, total, step=256):
@@ -437,9 +449,9 @@
     return tiled_call(
         last_kernel,
         tokens // step,
-        [((tokens, D), bf16, down), ((1, D), f32, row)],
+        [((tokens, D), bf16, down)],
         [(part, down), (recv, down), (x, down), (gain, row), (total, down)],
-    )
+    )[0]
 
 
 def up_kernel(m_ref, w_ref, b_ref, g_ref, slope_ref):
@@ -466,81 +478,31 @@
 
 def down_grad_kernel(me_ref, g_ref, d_ref, *outs):
     product = mm_rows(g_ref[...], d_ref[...]).astype(bf16)
-    for j, out in enumerate(outs):
-
-        @pl.when(pl.program_id(0) == j)
+    for i, out in enumerate(outs):
+
+        @pl.when(pl.program_id(0) == i)
         def _(out=out):
             out[...] = product.reshape(out.shape)
 
 
-def down_grad(me, depth, g, d):
+def down_grad(me, depth, chips, g, d):
     tokens, width = g.shape
     units = width // (4 * depth)
     return pl.pallas_call(
         down_grad_kernel,
         grid_spec=pltpu.PrefetchScalarGridSpec(
             num_scalar_prefetch=1,
-            grid=(4,),
+            grid=(len(chips),),
             in_specs=[
-                pl.BlockSpec((tokens, width // 4), lambda j, me: (0, me[0] ^ j)),
-                pl.BlockSpec(d.shape, lambda j, me: (0, 0), pipeline_mode=pl.Buffered(1)),
+                pl.BlockSpec((tokens, width // 4), lambda i, me: (0, me[0] ^ (i + chips[0]))),
+                pl.BlockSpec(d.shape, lambda i, me: (0, 0), pipeline_mode=pl.Buffered(1)),
             ],
-            out_specs=[pl.BlockSpec((depth, units, D), lambda j, me: (0, 0, 0))] * 4,
+            out_specs=[pl.BlockSpec((depth, units, D), lambda i, me: (0, 0, 0))] * len(chips),
         ),
-        out_shape=[jax.ShapeDtypeStruct((depth, units, D), bf16)] * 4,
-        compiler_params=pltpu.CompilerParams(vmem_limit_bytes=48 << 20),
+        out_shape=[jax.ShapeDtypeStruct((depth, units, D), bf16)] * len(chips),
+        compiler_params=pltpu.CompilerParams(vmem_limit_bytes=20 << 20),
         cost_estimate=light,
     )(jnp.reshape(me, (1,)), g, d)
-
-
-def mlp_back_kernel(me_ref, d_ref, wd_ref, slope_ref, m_ref, wu_ref, *refs):
-    gw_refs, (dm_ref, gb_ref, acc, gw) = refs[:4], refs[4:]
-    du = (mm_t(d_ref[...], wd_ref[...]) * slope_ref[...].astype(f32)).astype(bf16)
-    gb_ref[...] = jnp.sum(du.astype(f32), axis=0, keepdims=True)
-    gw[...] = mm_rows(m_ref[...], du).astype(bf16).reshape(gw.shape)
-    for j, gw_ref in enumerate(gw_refs):
-        gw_ref[...] = gw[:, me_ref[0] ^ j]
-    part = mm_t(du, wu_ref[...])
-    step, last = pl.program_id(0), pl.num_programs(0) - 1
-
-    @pl.when(step == 0)
-    def _():
-        acc[...] = part
-
-    @pl.when((step > 0) & (step < last))
-    def _():
-        acc[...] += part
-
-    @pl.when(step == last)
-    def _():
-        dm_ref[...] = (acc[...] + part).astype(bf16)
-
-
-def mlp_back(me, depth, d, w_down, slope, m, w_up, step=512):
-    tokens, width = slope.shape
-    rows = D // (4 * depth)
-    across = pl.BlockSpec((tokens, step), lambda i: (0, i))
-    return tiled_call(
-        mlp_back_kernel,
-        width // step,
-        [
-            *[
-                ((depth, rows, width), bf16, pl.BlockSpec((depth, rows, step), lambda i: (0, 0, i)))
-            ]
-            * 4,
-            ((tokens, D), bf16, pl.BlockSpec((tokens, D), lambda i: (0, 0))),
-            ((1, width), f32, pl.BlockSpec((1, step), lambda i: (0, i))),
-        ],
-        [
-            (jnp.reshape(me, (1,)), pl.BlockSpec(memory_space=pltpu.SMEM)),
-            (d, resident(d.shape)),
-            (w_down, pl.BlockSpec((step, D), lambda i: (i, 0))),
-            (slope, across),
-            (m, resident(m.shape)),
-            (w_up, pl.BlockSpec((D, step), lambda i: (0, i))),
-        ],
-        [pltpu.VMEM((tokens, D), f32), pltpu.VMEM((depth, 4, rows, step), bf16)],
-    )
 
 
 def norm_back_kernel(
@@ -593,9 +555,207 @@
     )
 
 
+def take_rows_kernel(picked_ref, *refs):
+    sources, (first_out, second_out, done_ref) = refs[1:3], refs[3:]
+    picked = picked_ref[0]
+    length = sources[0].shape[0]
+    places = lax.broadcasted_iota(jnp.int32, (picked.shape[0], length), 1) == picked
+    onehot = places.astype(bf16)
+    for source, out in zip(sources, (first_out, second_out)):
+        out[...] = mm(onehot, source[...]).astype(bf16)
+    done_ref[...] = jnp.zeros_like(done_ref)
+
+
+def take_rows(picked, earlier, *sources):
+    micro, count = picked.shape
+    width = sources[0].shape[1]
+    length = sources[0].shape[0] // micro
+    few = ((micro * count, width), bf16, pl.BlockSpec((count, width), lambda i: (i, 0)))
+    corner = pl.BlockSpec((1, 8, LANES), lambda i: (0, 0, 0))
+    return tiled_call(
+        take_rows_kernel,
+        micro,
+        [few, few, (*mark, pl.BlockSpec(mark[0], lambda i: (0, 0)))],
+        [
+            (picked[:, :, None], pl.BlockSpec((1, count, 1), lambda i: (i, 0, 0))),
+            (earlier, corner),
+        ]
+        + [(v, pl.BlockSpec((length, width), lambda i: (i, 0))) for v in sources],
+    )
+
+
+def mlp_pre_kernel(d_ref, wd_ref, slope_ref, wu_ref, du_ref, dm_ref, done_ref, acc):
+    du = (mm_t(d_ref[...], wd_ref[...]) * slope_ref[...].astype(f32)).astype(bf16)
+    du_ref[...] = du
+    part = mm_t(du, wu_ref[...])
+    step, last = pl.program_id(0), pl.num_programs(0) - 1
+
+    @pl.when(step == 0)
+    def _():
+        acc[...] = part
+
+    @pl.when((step > 0) & (step < last))
+    def _():
+        acc[...] += part
+
+    @pl.when(step == last)
+    def _():
+        dm_ref[...] = (acc[...] + part).astype(bf16)
+        done_ref[...] = jnp.zeros_like(done_ref)
+
+
+def mlp_pre(d, w_down, slope, w_up, step=512):
+    tokens, width = slope.shape
+    across = pl.BlockSpec((tokens, step), lambda i: (0, i))
+    return tiled_call(
+        mlp_pre_kernel,
+        width // step,
+        [
+            ((tokens, width), bf16, across),
+            ((tokens, D), bf16, pl.BlockSpec((tokens, D), lambda i: (0, 0))),
+            (*mark, pl.BlockSpec(mark[0], lambda i: (0, 0))),
+        ],
+        [
+            (d, resident(d.shape)),
+            (w_down, pl.BlockSpec((step, D), lambda i: (i, 0))),
+            (slope, across),
+            (w_up, pl.BlockSpec((D, step), lambda i: (0, i))),
+        ],
+        [pltpu.VMEM((tokens, D), f32)],
+    )
+
+
+def down_rest_kernel(me_ref, gy_ref, g_ref, *refs):
+    ins, outs = refs[:4], refs[4:]
+    more = mm_rows(g_ref[...], gy_ref[...])
+    for j in range(4):
+
+        @pl.when(pl.program_id(0) == j)
+        def _(j=j):
+            total = (ins[j][...].astype(f32) + more.reshape(ins[j].shape)).astype(bf16)
+            half = total.shape[0] // 2
+            outs[2 * j][...] = total[:half]
+            outs[2 * j + 1][...] = total[half:]
+
+
+def down_rest(me, gy, g, pre):
+    rows, width = g.shape
+    fixed = lambda shape: pl.BlockSpec(
+        shape, lambda i, me: (0,) * len(shape), pipeline_mode=pl.Buffered(1)
+    )
+    half = (pre[0].shape[0] // 2, *pre[0].shape[1:])
+    found = pl.pallas_call(
+        down_rest_kernel,
+        grid_spec=pltpu.PrefetchScalarGridSpec(
+            num_scalar_prefetch=1,
+            grid=(4,),
+            in_specs=[
+                fixed(gy.shape),
+                pl.BlockSpec((rows, width // 4), lambda i, me: (0, me[0] ^ i)),
+            ]
+            + [fixed(v.shape) for v in pre],
+            out_specs=[pl.BlockSpec(half, lambda i, me: (0, 0, 0))] * 8,
+        ),
+        out_shape=[jax.ShapeDtypeStruct(half, bf16)] * 8,
+        compiler_params=pltpu.CompilerParams(vmem_limit_bytes=16 << 20),
+        cost_estimate=light,
+    )(jnp.reshape(me, (1,)), gy, g, *pre)
+    return pairs_of(found)
+
+
+def up_rest_kernel(
+    me_ref, picked_ref, gy_ref, wd_ref, slope_ref, du_ref, m_ref, wu_ref, dm_in, *refs
+):
+    outs, (dm_ref, gb_ref, du, acc, gw) = refs[:8], refs[8:]
+    half = gw.shape[0] // 2
+    micro, count = picked_ref.shape[0], picked_ref.shape[2]
+    length = dm_in.shape[0] // micro
+    rows = (mm_t(gy_ref[...], wd_ref[...]) * slope_ref[...].astype(f32)).astype(bf16)
+    for s in range(micro):
+        at = slice(s * length, (s + 1) * length)
+        places = lax.broadcasted_iota(jnp.int32, (length, count), 0) == picked_ref[s]
+        more = mm(places.astype(bf16), rows[s * count : (s + 1) * count])
+        du[at] = du_ref[at] + more.astype(bf16)
+    gb_ref[...] = jnp.sum(du[...].astype(f32), axis=0, keepdims=True)
+    gw[...] = mm_rows(m_ref[...], du[...]).astype(bf16).reshape(gw.shape)
+    for j in range(4):
+        outs[2 * j][...] = gw[:half, me_ref[0] ^ j]
+        outs[2 * j + 1][...] = gw[half:, me_ref[0] ^ j]
+    part = mm_t(rows, wu_ref[...])
+
+    @pl.when(pl.program_id(0) == 0)
+    def _():
+        acc[...] = part
+
+    @pl.when(pl.program_id(0) > 0)
+    def _():
+        acc[...] += part
+
+    @pl.when(pl.program_id(0) == pl.num_programs(0) - 1)
+    def _():
+        for s in range(micro):
+            at = slice(s * length, (s + 1) * length)
+            cut = acc[s * count : (s + 1) * count]
+            dm_ref[at] = put_rows(dm_in[at], cut, picked_ref[s], length).astype(bf16)
+
+
+def up_rest(me, depth, picked, gy, w_down, slope, du, m, w_up, dm, step=512):
+    tokens, width = du.shape
+    rows = D // (4 * depth)
+    tall = lambda height: pl.BlockSpec((height, step), lambda i: (0, i))
+    once = lambda v: pl.BlockSpec(v.shape, lambda i: (0,) * v.ndim, pipeline_mode=pl.Buffered(1))
+    block = pl.BlockSpec((depth // 2, rows, step), lambda i: (0, 0, i))
+    return tiled_call(
+        up_rest_kernel,
+        width // step,
+        [((depth // 2, rows, width), bf16, block)] * 8
+        + [
+            ((tokens, D), bf16, pl.BlockSpec((tokens, D), lambda i: (0, 0))),
+            ((1, width), f32, tall(1)),
+        ],
+        [
+            (jnp.reshape(me, (1,)), pl.BlockSpec(memory_space=pltpu.SMEM)),
+            (picked, once(picked)),
+            (gy, once(gy)),
+            (w_down, pl.BlockSpec((step, D), lambda i: (i, 0))),
+            (slope, tall(gy.shape[0])),
+            (du, tall(tokens)),
+            (m, once(m)),
+            (w_up, tall(D)),
+            (dm, once(dm)),
+        ],
+        [
+            pltpu.VMEM((tokens, step), bf16),
+            pltpu.VMEM((gy.shape[0], D), f32),
+            pltpu.VMEM((depth, 4, rows, step), bf16),
+        ],
+    )
+
+
+def sum_both_kernel(*refs):
+    out_ref = refs[-1]
+    for h in range(2):
+        down, up = refs[3 * h : 3 * h + 3], refs[6 + 3 * h : 9 + 3 * h]
+        depth, rows = up[0].shape[:2]
+        at = slice(h * depth, (h + 1) * depth)
+        add = lambda these: sum(ref[...].astype(f32) for ref in these).astype(bf16)
+        out_ref[at, :rows] = add(up)
+        total = add(down)
+        out_ref[at, rows:, :D] = total[:, :rows]
+        out_ref[at, rows:, D:] = total[:, rows:]
+
+
 def order_rows_kernel(me_ref, *refs):
     for j, ref in enumerate(refs[:-1]):
         refs[-1][me_ref[0] ^ j] = ref[...]
+
+
+def halves_kernel(*refs):
+    out_ref = refs[-1]
+    half = refs[0].shape[0]
+    for h in range(2):
+        total = sum(ref[...].astype(f32) for ref in refs[3 * h : 3 * h + 3])
+        out_ref[h * half : (h + 1) * half] = total.astype(bf16)
 
 
 def order_mlp_kernel(me_ref, u0, u1, u2, u3, d_ref, out_ref):
@@ -623,15 +783,13 @@
     attend_kernel(count, HALF // LANES, count, qkv_ref, seg_col_ref, seg_row_ref, o_ref)
 
 
-def routed_hidden_kernel(part_ref, recv_ref, chosen_ref, gain_ref, z_ref, h_ref, m_ref):
+def routed_hidden_kernel(part_ref, recv_ref, chosen_ref, gain_ref, m_ref):
     z = part_ref[...].astype(f32) + recv_ref[...].astype(f32)
-    h = chosen_ref[...] + z
-    z_ref[...] = z
-    h_ref[...] = h
+    h = chosen_ref[...].astype(f32) + z
     m_ref[...] = (h * inverse_rms(h) * gain_ref[...]).astype(bf16)
 
 
-def routed_mlp_kernel(core_ref, m0, m1, m2, m3, d0, d1, d2, d3, w_ref, b_ref, *rest):
+def routed_mlp_kernel(core_ref, m0, m1, m2, m3, d0, d1, d2, d3, w_ref, b_ref, _, *rest):
     g_ref, du_ref, keep_ref, send_ref, gb_ref, m_ref, d_ref = rest
     rows = m0.shape[0]
     for j, (m, d) in enumerate(zip((m0, m1, m2, m3), (d0, d1, d2, d3))):
@@ -668,7 +826,7 @@
         send_ref[...] = e
 
 
-def routed_grads_kernel(g_ref, d_ref, m_ref, du_ref, out_ref):
+def routed_grads_kernel(g_ref, d_ref, m_ref, du_ref, out_ref, done_ref):
     depth, all_rows, hidden = out_ref.shape
     rows = D // depth
     units = (all_rows - rows) // 2
@@ -678,22 +836,33 @@
         down = mm_rows(g_ref[...], d_ref[:, k * hidden : (k + 1) * hidden]).astype(bf16)
         low = rows + k * units
         out_ref[:, low : low + units] = down.reshape(depth, units, hidden)
+    done_ref[...] = jnp.zeros_like(done_ref)
+
+
+def add_parts_kernel(a_ref, b_ref, _, *outs):
+    for j, out in enumerate(outs):
+        out[...] = (a_ref[j].astype(f32) + b_ref[j].astype(f32)).astype(bf16)
+
+
+def add_kernel(*refs):
+    refs[-1][...] = sum(ref[...].astype(f32) for ref in refs[:-2]).astype(bf16)
 
 
 def routed_back_kernel(count, core_ref, *refs):
-    ins, outs = refs[:13], refs[13:]
-    total, crossed, bias, z_ref, chosen_g, weight_ref, h_ref, gain, wo_ref, wq_ref = ins[:10]
-    qkv_ref, seg_col_ref, seg_row_ref = ins[10:]
+    ins, outs = refs[:14], refs[14:]
+    total, crossed, bias, z_ref, z_recv, chosen_ref, chosen_g, weight_ref, gain = ins[:9]
+    wo_ref, wq_ref, qkv_ref, seg_col_ref, seg_row_ref = ins[9:]
     delta_ref, logit_ref, dh_ref, dz_ref, gain_g, dqkv_ref, da_ref, do_scr = outs
     first = core_ref[0] == 0
     a, b = total[...].astype(f32), crossed[...].astype(f32)
     e = jnp.where(first, a, b) + bias[...]
     dm = jnp.where(first, b, a)
-    delta = z_ref[...] + e
+    z = z_ref[...].astype(f32) + z_recv[...].astype(f32)
+    delta = z + e
     delta_ref[...] = delta
-    weight, grad = weight_ref[...], chosen_g[...]
+    weight, grad = weight_ref[...], chosen_g[...].astype(f32)
     logit_ref[...] = jnp.sum(grad * delta, axis=1, keepdims=True) * weight * (1.0 - weight)
-    h = h_ref[...]
+    h = chosen_ref[...].astype(f32) + z
     inverse = inverse_rms(h)
     unit = h * inverse
     gain_g[...] = jnp.sum(dm * unit, axis=0, keepdims=True)
@@ -720,12 +889,13 @@
 def routed_out_kernel(
     part_ref, recv_ref, chosen_ref, gain, dh_ref, logit_ref, router, picked_ref, cot_ref, *outs
 ):
-    gy_ref, gain_g, router_g = outs
-    da = part_ref[...].astype(f32) + recv_ref[...].astype(f32)
-    chosen, logit = chosen_ref[...], logit_ref[...]
+    gy_ref, gy_rows, gain_g, router_g = outs
+    own = part_ref[...].astype(f32)
+    da = own + recv_ref[...].astype(f32)
+    chosen, logit = chosen_ref[...].astype(f32), logit_ref[...]
     inverse = inverse_rms(chosen)
     unit = chosen * inverse
-    gain_g[...] = jnp.sum(da * unit, axis=0, keepdims=True)
+    gain_g[...] = jnp.sum(own * unit, axis=0, keepdims=True)
     router_g[...] = jnp.sum(logit * chosen, axis=0, keepdims=True)
     rows = dh_ref[...] + norm_back(da, unit, inverse, gain[...]) + logit * router[...]
     micro, count = picked_ref.shape[0], picked_ref.shape[2]
@@ -733,7 +903,10 @@
     for s in range(micro):
         at = slice(s * length, (s + 1) * length)
         cut = rows[s * count : (s + 1) * count]
-        gy_ref[at] = put_rows(cot_ref[at], cut, picked_ref[s], length).astype(bf16)
+        gy = put_rows(cot_ref[at], cut, picked_ref[s], length).astype(bf16)
+        gy_ref[at] = gy
+        places = lax.broadcasted_iota(jnp.int32, (length, count), 0) == picked_ref[s]
+        gy_rows[s * count : (s + 1) * count] = mm_rows(places.astype(bf16), gy).astype(bf16)
 
 
 def routed_sum_kernel(y_ref, delta_ref, weight_ref, picked_ref, out_ref):
@@ -845,12 +1018,14 @@
     onehot = picked[:, :, None] == lax.broadcasted_iota(jnp.int32, (micro, count, length), 2)
     seg1 = jnp.sum(jnp.where(onehot, seg[:, None, :], 0), axis=2)
     seg1_col, seg1_row = seg1[:, :, None], seg1[:, None, :]
+    is_routed = jnp.any(onehot, axis=1).reshape(tokens, 1)
+    cot_other = jnp.where(is_routed, jnp.zeros_like(cot_b), cot_b)
     own_q, rest, mlp, shard_u = fence(own_q, rest, mlp, shard0[1])
 
     px_q, py_q = swap(own_q, "x"), swap(own_q, "y")
     own_u = over_z(shard_u)
-    own_q, px_q, py_q, own_u, shard_d, x_b, cot_b, seg1_col, seg1_row = fence(
-        own_q, px_q, py_q, own_u, shard0[2], x_b, cot_b, seg1_col, seg1_row
+    own_q, px_q, py_q, own_u, shard_d, x_b, cot_b, cot_other, seg1_col, seg1_row = fence(
+        own_q, px_q, py_q, own_u, shard0[2], x_b, cot_b, cot_other, seg1_col, seg1_row
     )
     pd_q, px_u = swap(px_q, "y"), swap(own_u, "x")
     own_d = over_z(shard_d)
@@ -896,20 +1071,22 @@
     )
     w_q0 = w_q0.reshape(D, 3 * HALF)
     o0, z_part = attention_call(attend_out_kernel, seg, [qkv0], w_o0, HALF)
-    o0, z_part, own_u, px_u, py_u, px_d = fence(o0, z_part, own_u, px_u, py_u, px_d)
+    o0, z_part, own_u, px_u, py_u, px_d, mlp = fence(o0, z_part, own_u, px_u, py_u, px_d, mlp)
+    w_m1 = over_z(mlp)
 
     pd_u = swap(py_u, "x")
     pd_d0 = swap(px_d[:halfway], "y")
     h0, m0 = hidden_rows(x_b, z_part, swap(z_part, "section"), gain_mlp0)
-    m0, pd_u, py_d = fence(m0, pd_u, py_d)
+    m0, pd_u, py_d, bias_up0, bias_up1, router_full = fence(
+        m0, pd_u, py_d, bias_up0, bias_up1, router_full
+    )
 
     pd_d1 = swap(py_d[halfway:], "x")
     (w_u0,) = place(me, [own_u, px_u, py_u, pd_u], spans_all, ((0, D * 2),))
     w_u0 = w_u0.reshape(D, D * 2)
     g0, slope0 = up_product(m0, w_u0, bias_up0)
-    g0, pd_d0, pd_d1, mlp, w_r1 = fence(g0, pd_d0, pd_d1, mlp, w_r1)
-
-    w_m1 = over_z(mlp)
+    g0, pd_d0, pd_d1, w_r1 = fence(g0, pd_d0, pd_d1, w_r1)
+
     spans_cut = spans_all[:3] + [(3, 0, halfway), (3, halfway, depth)]
     (w_d0,) = place(
         me, [own_d, px_d, py_d, pd_d0, pd_d1], spans_cut, ((0, D),), plane_first=True
@@ -928,15 +1105,16 @@
         [],
         [a1, seg1_col, seg1_row, w_r1],
     )
-    de_all, o1, w_o1 = fence(de_all, o1, w_o1)
     z_part = mm(o1, w_o1).astype(bf16)
-    z1, h1, m1 = whole(
+    z_recv = swap(z_part, "section")
+    (m1,) = whole(
         routed_hidden_kernel,
-        [((chosen_rows, D), f32)] * 2 + [((chosen_rows, D), bf16)],
+        [((chosen_rows, D), bf16)],
         [],
-        [z_part, swap(z_part, "section"), chosen, gain_mlp1],
+        [z_part, z_recv, chosen, gain_mlp1],
     )
     m_all = [m1] + [to_plane(m1, j) for j in (1, 2, 3)]
+    pre_du, pre_dm, pre_done = mlp_pre(cot_other, w_d0, slope0, w_u0)
     g1, du1, keep, send, gb_u1, m_rows, de_rows = whole(
         routed_mlp_kernel,
         [((4 * chosen_rows, hidden), bf16)] * 2
@@ -944,21 +1122,27 @@
         + [((1, hidden), f32)]
         + [((4 * chosen_rows, D), bf16)] * 2,
         [core],
-        [*m_all, *de_all, w_m1, bias_up1],
+        [*m_all, *de_all, w_m1, bias_up1, pre_done],
     )
     plus = lambda *terms: sum(t.astype(f32) for t in terms).astype(bf16)
-    summed = plus(keep, swap(send, "section"))
-    (gw_m1,) = whole(
+    others = swap(send, "section")
+    gw_m1, grads_done = whole(
         routed_grads_kernel,
-        [((depth, mlp_rows, hidden), bf16)],
+        [((depth, mlp_rows, hidden), bf16), mark],
         [],
         [g1, de_rows, m_rows, du1],
     )
-    total = plus(summed[0], *[to_plane(summed[j], j) for j in (1, 2, 3)])
+    plus = lambda *terms: sum(t.astype(f32) for t in terms).astype(bf16)
+    r_m1 = reduce_z(gw_m1)
+    summed = whole(
+        add_parts_kernel, [((chosen_rows, D), bf16)] * 4, [], [keep, others, grads_done]
+    )
+    terms = [summed[0]] + [to_plane(summed[j], j) for j in (1, 2, 3)]
+    pre_d = down_grad(me, depth, (0, 1, 2, 3), g0, cot_other)
+    g_rows, slope_rows, rows_done = take_rows(picked, pre_d[0], g0, slope0)
+    (total,) = whole(add_kernel, [((chosen_rows, D), bf16)], [], [*terms, rows_done])
     crossed = swap(total, "section")
-    total, crossed, gw_m1 = fence(total, crossed, gw_m1)
-
-    r_m1 = reduce_z(gw_m1)
+
     delta, grad_logit, dh1, dz1, gg_mlp1, dqkv1, da_part = whole(
         functools.partial(routed_back_kernel, count),
         [
@@ -975,10 +1159,11 @@
             total,
             crossed,
             b_down1,
-            z1,
+            z_part,
+            z_recv,
+            chosen,
             grad_chosen,
             weight,
-            h1,
             gain_mlp1,
             w_o1,
             w_r1,
@@ -995,9 +1180,9 @@
         return jnp.concatenate([jnp.where(first, own, recv), jnp.where(first, recv, own)], axis=0)
 
     gw_o1 = out_by_columns(mm_rows(o1, dz1).astype(bf16))
-    gy0_b, gg_attn1, grad_router = whole(
+    gy0_b, gy_rows, gg_attn1, grad_router = whole(
         routed_out_kernel,
-        [((tokens, D), bf16), ((1, D), f32), ((1, D), f32)],
+        [((tokens, D), bf16), ((chosen_rows, D), bf16), ((1, D), f32), ((1, D), f32)],
         [],
         [
             da_part,
@@ -1011,26 +1196,48 @@
             cot_b,
         ],
     )
-    (attn1,) = attn_grad(me, False, depth, a1, dqkv1, gw_o1)
-    gw_d0 = down_grad(me, depth, g0, gy0_b)
-    gw_d0, attn1, gy0_b, r_m1 = fence(gw_d0, attn1, gy0_b, r_m1)
+    send_diagonal = lambda grads: [swap(grads[3][0], "x"), swap(grads[3][1], "y")]
+    send_far = lambda grads: [swap(grads[1][0], "x"), swap(grads[2][1], "y")]
+    near = lambda grads, diag: [plus(grads[2][0], diag[0]), plus(grads[1][1], diag[1])]
+    send_near = lambda sums: [swap(sums[0], "y"), swap(sums[1], "x")]
+    parts = lambda grads, near, far: [
+        v for h in range(2) for v in (grads[0][h], near[h], far[h])
+    ]
+
+    gw_d0 = down_rest(me, gy_rows, g_rows, pre_d)
+    gw_d0, gy_rows = fence(gw_d0, gy_rows)
+    diag_d, far_d = send_diagonal(gw_d0), send_far(gw_d0)
+    attn1 = attn_grad(me, False, depth, a1, dqkv1, gw_o1)
+    *gw_u0, dm_part, gb_u0 = up_rest(
+        me,
+        depth,
+        picked[:, None, :],
+        gy_rows,
+        w_d0,
+        slope_rows,
+        pre_du,
+        m0,
+        w_u0,
+        pre_dm,
+    )
+    diag_d, far_d, gw_u0, dm_part, gy0_b, attn1 = fence(
+        diag_d, far_d, pairs_of(gw_u0), dm_part, gy0_b, attn1
+    )
 
     r_a1 = reduce_z(attn1)
-    diag_d = swap(gw_d0[3], "x")
-    *gw_u0, dm_part, gb_u0 = mlp_back(me, depth, gy0_b, w_d0, slope0, m0, w_u0)
-    gw_u0, dm_part, gw_d0, diag_d = fence(gw_u0, dm_part, gw_d0, diag_d)
-
-    far_d, diag_u = swap(gw_d0[1], "x"), swap(gw_u0[3], "y")
-    sum_d = plus(gw_d0[2], diag_d)
+    diag_u = send_diagonal(gw_u0)
+    near_d = send_near(near(gw_d0, diag_d))
     dz0, gy_dh0, do0, gg_mlp0, g_down0 = norm_back_product(
         dm_part, swap(dm_part, "section"), h0, gain_mlp0, gy0_b, w_o0
     )
-    dqkv0, da_part = attention_call(attend_back_out_kernel, seg, [qkv0, do0], w_q0, 3 * HALF)
     gw_o0 = out_by_columns(mm_rows(o0, dz0).astype(bf16))
-    far_d, diag_u, sum_d, dqkv0, da_part, gw_o0 = fence(far_d, diag_u, sum_d, dqkv0, da_part, gw_o0)
-
-    near_u, near_d = swap(plus(gw_u0[1], diag_u), "x"), swap(sum_d, "y")
-    dx0_b, gg_attn0 = last_rows(da_part, swap(da_part, "section"), x_b, gain_attn0, gy_dh0)
+    dqkv0, da_part, gg_attn0 = attention_call(
+        attend_back_out_kernel, seg, [qkv0, do0, x_b], w_q0, 3 * HALF, sums=1
+    )
+    diag_u, near_d, dqkv0, da_part, gw_o0 = fence(diag_u, near_d, dqkv0, da_part, gw_o0)
+
+    far_u = send_far(gw_u0)
+    near_u = send_near(near(gw_u0, diag_u))
     here = lax.broadcasted_iota(jnp.int32, (depth, 4, bias_cols, rows), 1) == me
     gb_u1 = gb_u1.reshape(depth, 1, bias_cols, rows)
     gb_u1 = jnp.where(here, gb_u1, 0.0).transpose(2, 0, 1, 3).reshape(bias_cols, D)
@@ -1046,10 +1253,17 @@
     )
     strip = jnp.pad(strip, ((0, LANES - 16), (0, 0))).T.astype(bf16)
     attn0 = attn_grad(me, True, depth, a0, dqkv0, gw_o0, strip)
-    attn0, near_u, near_d, far_d, r_a1 = fence(attn0, near_u, near_d, far_d, r_a1)
-
-    diag_q, far_u = swap(attn0[3], "x"), swap(gw_u0[2], "y")
-    r_d0 = reduce_z(plus(gw_d0[0], near_d, far_d))
+    attn0, near_u, far_u, da_part = fence(attn0, near_u, far_u, da_part)
+
+    diag_q, far_q = send_diagonal(attn0), send_far(attn0)
+    (sum_du,) = whole(
+        sum_both_kernel,
+        [((depth, 2 * rows, 2 * D), bf16)],
+        [],
+        parts(gw_d0, near_d, far_d) + parts(gw_u0, near_u, far_u),
+    )
+    r_du = reduce_z(sum_du)
+    dx0_b = last_rows(da_part, swap(da_part, "section"), x_b, gain_attn0, gy_dh0)
     (y1_b,) = whole(
         routed_sum_kernel,
         [((tokens, D), bf16)],
@@ -1057,19 +1271,27 @@
         [y0_b, delta, weight, picked[:, None, :]],
     )
     boundary_out = jnp.where(first, dx0_b, y1_b).reshape(1, micro, 1, length, D)
-    boundary_out, diag_q, far_u, r_a1, r_m1 = fence(boundary_out, diag_q, far_u, r_a1, r_m1)
-
-    far_q, near_q = swap(attn0[1], "x"), swap(plus(attn0[2], diag_q), "y")
-    r_u0 = reduce_z(plus(gw_u0[0], near_u, far_u))
+    diag_q, r_a1, r_m1 = fence(diag_q, r_a1, r_m1)
+
+    near_q = send_near(near(attn0, diag_q))
+    far_q, boundary_out = fence(far_q, boundary_out)
     part = lambda v, j: lax.dynamic_index_in_dim(v, me ^ j, axis=0, keepdims=False)
+    (sum_q,) = whole(
+        halves_kernel,
+        [((depth, rows, width + LANES), bf16)],
+        [],
+        parts(attn0, near_q, far_q),
+    )
+    sum_q, r_a1, r_m1, r_du = fence(sum_q, r_a1, r_m1, r_du)
+    r_u0 = r_du[:rows]
+    r_d0 = jnp.concatenate([r_du[rows:, :D], r_du[rows:, D:]], axis=0)
+    r_a0 = reduce_z(sum_q)
     r_a1 = plus(part(r_a1, 0), *[to_plane(part(r_a1, j), j) for j in (1, 2, 3)])
     up = r_m1[: 4 * rows].reshape(4, rows, hidden)
     up = [part(up, 0)] + [to_plane(part(up, j), j) for j in (1, 2, 3)]
     (r_u1,) = whole(order_columns_kernel, [((rows, 2 * D), bf16)], [me], up)
     low = 4 * rows + half_units
     r_d1 = jnp.concatenate([r_m1[4 * rows : low], r_m1[low:]], axis=1)
-    far_q, near_q, r_a1, r_u1, r_d1, r_d0 = fence(far_q, near_q, r_a1, r_u1, r_d1, r_d0)
-    r_a0 = reduce_z(plus(attn0[0], near_q, far_q))
 
     def joined(grad0, grad1):
         keep = jnp.where(first, grad0, grad1)
@@ -1081,7 +1303,7 @@
     low, high = joined(r_u0, r_u1)
     cut = lambda v: v.reshape(rows, 4, depth, half_units).transpose(0, 2, 1, 3)
     out_up = jnp.stack([cut(low), cut(high)], axis=3).reshape(1, rows, FF)
-    r_a0, out_up, out_down, boundary_out = fence(r_a0, out_up, out_down, boundary_out)
+    r_a0, r_a1, out_up, out_down, boundary_out = fence(r_a0, r_a1, out_up, out_down, boundary_out)
     strip = r_a0[:, width:]
     strip_mine = jnp.where(first, strip[:, :8], strip[:, 8:16])
     strip_other = jnp.where(first, strip[:, 8:16], strip[:, :8])
@@ -1096,6 +1318,7 @@
         [keep, recv],
     )
     small = strip_mine.astype(f32).T
+    gain = small[0:1] + recv[:, width : width + 1].astype(f32).T
     bias_half = small[4 : 4 + bias_cols]
     bias_other = recv[:, width + 4 : width + 4 + bias_cols].astype(f32).T
     out_b_up = jnp.concatenate(
@@ -1103,7 +1326,7 @@
     ).reshape(1, units)
     return (
         boundary_out,
-        small[0:1],
+        gain,
         out_qkv[None],
         out_out[None],
         small[1:2],

time: 541 us -> 500 us (0.924)
  waiting for transfers between devices: 206 us -> 141 us
  local copies, waits for them, and re-layouts: 76.7 us -> 103 us
  starting transfers between devices: 56.4 us -> 64.8 us
  Pallas kernels: 138 us -> 131 us
    ppermute x21, waiting for transfers between devices: 72 us -> 22.8 us  [to_plane(): return lax.ppermute(v, ('y', 'x'), [(i, i ^ j) for i in range(4)])]
    unnamed x222 -> x311, local copies, waits for them, and re-layouts: 55.4 us -> 79.8 us
    reduce_scatter x5 -> x4, waiting for transfers between devices: 31.9 us -> 10.7 us  [reduce_z(): return lax.psum_scatter(part, 'z', scatter_dimension=0, tiled=False)]
    pallas_call x9 -> x11, Pallas kernels: 71.2 us -> 64.8 us  [tiled_call(): pl.pallas_call(kernel, grid=(steps,), out_shape=[jax.ShapeDtypeStruct(sha...]
    convert_element_type x9 -> x7, other arithmetic: 15.6 us -> 9.71 us  [shards(): plus = lambda *terms: sum((t.astype(f32) for t in terms)).astype(bf16)]
    pallas_call x2, Pallas kernels: 28.3 us -> 22.5 us  [attention_call(): pl.pallas_call(functools.partial(kernel, LANES, pairs, length), grid=(cou...]
    ppermute x38 -> x47, starting transfers between devices: 29.2 us -> 34.5 us  [swap(): return lax.ppermute(v, axis, [(0, 1), (1, 0)])]
    pallas_call x12 -> x16, Pallas kernels: 25.1 us -> 27.8 us  [whole(): pl.pallas_call(kernel, out_shape=[jax.ShapeDtypeStruct(shape, dtype) for...]
  transfers between devices with their start and end apart: 69 -> 77, of which waited for: 34 -> 35; matrix products, arithmetic and copies ran while one was open for 9% -> 10% of each run, Pallas kernels for 23% -> 25%
where the time goes in v3:
time: 500 us; the launch traced here: 492 us
  waiting for transfers between devices  141 us (28%)
  Pallas kernels  131 us (26%)
  local copies, waits for them, and re-layouts  103 us (21%)
  starting transfers between devices  64.8 us (13%)
  other arithmetic  34.1 us (7%)
  between operations  16.1 us (3%)
    ppermute x47, waiting for transfers between devices, swap(): return lax.ppermute(v, axis, [(0, 1), (1, 0)])  92.9 us
    unnamed x311, local copies, waits for them, and re-layouts  79.8 us
    pallas_call x11, Pallas kernels, tiled_call(): pl.pallas_call(kernel, grid=(steps,), out_shape=[jax.ShapeDtypeStruct(sha...  64.8 us
    ppermute x47, starting transfers between devices, swap(): return lax.ppermute(v, axis, [(0, 1), (1, 0)])  34.5 us
    ppermute x21, starting transfers between devices, to_plane(): return lax.ppermute(v, ('y', 'x'), [(i, i ^ j) for i in range(4)])  29.1 us
    pallas_call x16, Pallas kernels, whole(): pl.pallas_call(kernel, out_shape=[jax.ShapeDtypeStruct(shape, dtype) for...  27.8 us
    ppermute x21, waiting for transfers between devices, to_plane(): return lax.ppermute(v, ('y', 'x'), [(i, i ^ j) for i in range(4)])  22.8 us
    pallas_call x2, Pallas kernels, attention_call(): pl.pallas_call(functools.partial(kernel, LANES, pairs, length), grid=(cou...  22.5 us
  transfers between devices with their start and end apart: 77, of which 35 were waited for; matrix products, arithmetic and copies ran while one was open for 10% of the time, Pallas kernels for 25%

profile of v3, /device:TPU:0, one launch (start us, length us, event | category | flops | bytes accessed | tf_op | source)
XLA Modules:
  0.0 491.5 jit_solution(11153947053297750165)
XLA Ops:
  32.6 9.6 %collective-permute-done.7.u3 = bf16[64,512]{1,0:T(8,128)(2,1)S(1)} collective-permute-done((bf16[64,512]{1,0:T(8,128)(2,1)S(1)}, bf16[64,512]{1,0:T(8,128)(2,1)S(1)}, u32[]{:S(2)}, u32[]{:S(2)}) %collective-permute-start.7) | collective-permute-done | bytes 65568 | tf_op jit(solution)/shard_map/ppermute | solution.py:53
  44.2 5.1 %all-gather.11.cloned.1.call-done = bf16[256,2176]{1,0:T(8,128)(2,1)} async-done(((bf16[64,2176]{1,0:T(8,128)(2,1)}), bf16[256,2176]{1,0:T(8,128)(2,1)}) %all-gather.11.cloned.1.call-update) | async-done | bytes 1114128 | tf_op jit(solution)/shard_map/all_gather | solution.py:61
  53.2 4.0 broadcast_select_fusion
  57.2 18.6 %collective-permute-done.10.rest_2_ = bf16[4,64,2176]{2,1,0:T(8,128)(2,1)} collective-permute-done((bf16[4,64,2176]{2,1,0:T(8,128)(2,1)}, bf16[4,64,2176]{2,1,0:T(8,128)(2,1)}, u32[]{:S(2)}, u32[]{:S(2)}) %collective-permute-start.10) | collective-permute-done | bytes 1114144 | tf_op jit(solution)/shard_map/ppermute | solution.py:49
  81.9 23.2 %collective-permute-done.13.rest_1_ = bf16[4,64,2048]{2,1,0:T(8,128)(2,1)S(1)} collective-permute-done((bf16[4,64,2048]{2,1,0:T(8,128)(2,1)}, bf16[4,64,2048]{2,1,0:T(8,128)(2,1)S(1)}, u32[]{:S(2)}, u32[]{:S(2)}) %collective-permute-start.13) | collective-permute-done | bytes 1048608 | tf_op jit(solution)/shard_map/ppermute | solution.py:49
  119.1 5.1 %shard_map.198 = (bf16[4,4,64,1536]{3,2,1,0:T(8,128)(2,1)S(1)}, bf16[1024,1024]{1,0:T(8,128)(2,1)S(1)}, bf16[1024,1536]{1,0:T(8,128)(2,1)S(1)}) custom-call(s32[1]{0:T(128)} %bitcast.me_ref, bf16[1024,1024]{1,0:T(8,128)(2,1)S(1)} %get-tuple-element.200.x_ref, f32[1,1024]{1,0:T(1,128)S(1)} %get-tuple-element.505.gain_ref, bf16[4,64,2176]{2,1,0:T(8,128)(2,1)S(1)} %bitcast.149, ...), custom_call_target="tpu_custom_call" | custom-call | flops 1 | bytes 1 | tf_op jit(solution)/shard_map/pallas_call | solution.py:301
  129.1 6.6 %shard_map.199 = (bf16[1024,512]{1,0:T(8,128)(2,1)S(1)}, bf16[1024,1024]{1,0:T(8,128)(2,1)}) custom-call(bf16[1024,1536]{1,0:T(8,128)(2,1)S(1)} %get-tuple-element.213.qkv_ref, s32[2,512,1]{2,1,0:T(8,128)S(1)} %copy-done.29, s32[2,1,512]{2,1,0:T(1,128)S(1)} %copy-done.112, bf16[512,1024]{1,0:T(8,128)(2,1)S(1)} %pad_maximum_fusion.w_ref), custom_call_target="tpu_custom_call" | custom-call | flops 1 | bytes 1 | tf_op jit(solution)/shard_map/pallas_call | solution.py:229
  150.6 13.0 %collective-permute-done.19.rest_2_ = bf16[4,128,1024]{2,1,0:T(8,128)(2,1)} collective-permute-done((bf16[4,128,1024]{2,1,0:T(8,128)(2,1)}, bf16[4,128,1024]{2,1,0:T(8,128)(2,1)}, u32[]{:S(2)}, u32[]{:S(2)}) %collective-permute-start.19) | collective-permute-done | bytes 1048608 | tf_op jit(solution)/shard_map/ppermute | solution.py:49
  171.3 8.8 %shard_map.202 = (bf16[1024,2048]{1,0:T(8,128)(2,1)S(1)}, bf16[1024,2048]{1,0:T(8,128)(2,1)S(1)}) custom-call(bf16[1024,1024]{1,0:T(8,128)(2,1)S(1)} %copy-done.27, bf16[1024,2048]{1,0:T(8,128)(2,1)S(1)} %bitcast.137, f32[1,2048]{1,0:T(1,128)S(1)} %reshape.196.b_ref), custom_call_target="tpu_custom_call" | custom-call | flops 1 | bytes 1 | tf_op jit(solution)/shard_map/pallas_call | solution.py:319
  184.1 6.1 %all-gather.17.cloned.1.call-done = bf16[16,64,2048]{2,1,0:T(8,128)(2,1)} async-done(((bf16[4,64,2048]{2,1,0:T(8,128)(2,1)}), bf16[16,64,2048]{2,1,0:T(8,128)(2,1)}) %all-gather.17.cloned.1.call-update) | async-done | bytes 4194320 | tf_op jit(solution)/shard_map/all_gather | solution.py:61
  194.0 5.8 %shard_map.204.part_ref = bf16[1024,1024]{1,0:T(8,128)(2,1)} custom-call(bf16[1024,2048]{1,0:T(8,128)(2,1)S(1)} %copy-done.7, bf16[2048,1024]{1,0:T(8,128)(2,1)S(1)} %bitcast.140), custom_call_target="tpu_custom_call" | custom-call | flops 1 | bytes 1 | tf_op jit(solution)/shard_map/pallas_call | solution.py:319
  232.9 12.0 %shard_map.208 = (bf16[1024,2048]{1,0:T(8,128)(2,1)S(1)}, bf16[1024,1024]{1,0:T(8,128)(2,1)S(1)}, f32[8,128]{1,0:T(8,128)S(1)}) custom-call(bf16[1024,1024]{1,0:T(8,128)(2,1)S(1)} %copy-done.12, bf16[2048,1024]{1,0:T(8,128)(2,1)S(1)} %bitcast.141, bf16[1024,2048]{1,0:T(8,128)(2,1)S(1)} %copy-done.17, bf16[1024,2048]{1,0:T(8,128)(2,1)S(1)} %bitcast.138), custom_call_target="tpu_custom_call" | custom-call | flops 1 | bytes 1 | tf_op jit(solution)/shard_map/pallas_call | solution.py:319
  252.6 4.1 shard_map.209
  271.9 6.1 %shard_map.212 = (bf16[4,128,1024]{2,1,0:T(8,128)(2,1)S(1)}, bf16[4,128,1024]{2,1,0:T(8,128)(2,1)S(1)}, bf16[4,128,1024]{2,1,0:T(8,128)(2,1)S(1)}, bf16[4,128,1024]{2,1,0:T(8,128)(2,1)S(1)}) custom-call(s32[1]{0:T(128)} %bitcast.me_ref, bf16[1024,2048]{1,0:T(8,128)(2,1)S(1)} %copy-done.8, bf16[1024,1024]{1,0:T(8,128)(2,1)S(1)} %copy-done.13), custom_call_target="tpu_custom_call" | custom-call | flops 1 | bytes 1 | tf_op jit(solution)/shard_map/pallas_call | solution.py:491
  295.6 4.0 shard_map.217
  304.5 12.3 %shard_map.218 = (bf16[2,64,2048]{2,1,0:T(8,128)(2,1)S(1)}, bf16[2,64,2048]{2,1,0:T(8,128)(2,1)S(1)}, bf16[2,64,2048]{2,1,0:T(8,128)(2,1)}, bf16[2,64,2048]{2,1,...) custom-call(s32[1]{0:T(128)} %bitcast.me_ref, ...), custom_call_target="tpu_custom_call" | custom-call | flops 1 | bytes 1 | tf_op jit(solution)/shard_map/pallas_call | solution.py:319
  336.6 5.2 %shard_map.220 = (bf16[1024,1024]{1,0:T(8,128)(2,1)S(1)}, f32[1024,1024]{1,0:T(8,128)S(1)}, bf16[1024,512]{1,0:T(8,128)(2,1)S(1)}, f32[1,1024]{1,0:T(1,128)S(1)}, f32[1,1024]{1,0:T(1,128)S(1)}) custom-call(bf16[1024,1024]{1,0:T(8,128)(2,1)S(1)} %copy-done.56, bf16[1024,1024]{1,0:T(8,128)(2,1)} %collective-permute-done.46.recv_ref, ...), custom_call_target="tpu_custom_call" | custom-call | flops 1 | bytes 1 | tf_op jit(solution)/shard_map/pallas_call | solution.py:319
  351.8 15.9 %shard_map.221 = (bf16[1024,1536]{1,0:T(8,128)(2,1)S(1)}, bf16[1024,1024]{1,0:T(8,128)(2,1)S(1)}, f32[1,1024]{1,0:T(1,128)S(1)}) custom-call(bf16[1024,1536]{1,0:T(8,128)(2,1)S(1)} %copy-done.24, s32[2,512,1]{2,1,0:T(8,128)S(1)} %copy-done.30, s32[2,1,512]{2,1,0:T(1,128)S(1)} %copy-done.112, bf16[1024,512]{1,0:T(8,128)(2,1)S(1)} %get-tuple-element.311.g_ref, ...), custom_call_target="tpu_custom_call" | custom-call | flops 1 | bytes 1 | tf_op jit(solution)/shard_map/pallas_call | solution.py:229
  383.1 6.0 %shard_map.222 = (bf16[2,64,2176]{2,1,0:T(8,128)(2,1)S(1)}, bf16[2,64,2176]{2,1,0:T(8,128)(2,1)S(1)}, bf16[2,64,2176]{2,1,0:T(8,128)(2,1)}, bf16[2,64,2176]{2,1,...) custom-call(s32[1]{0:T(128)} %bitcast.me_ref, ...), custom_call_target="tpu_custom_call" | custom-call | flops 1 | bytes 1 | tf_op jit(solution)/shard_map/pallas_call | solution.py:319
  405.0 11.8 %collective-permute-done.52 = bf16[2,64,2176]{2,1,0:T(8,128)(2,1)} collective-permute-done((bf16[2,64,2176]{2,1,0:T(8,128)(2,1)}, bf16[2,64,2176]{2,1,0:T(8,128)(2,1)}, u32[]{:S(2)}, u32[]{:S(2)}) %collective-permute-start.52) | collective-permute-done | bytes 557088 | tf_op jit(solution)/shard_map/ppermute | solution.py:49
  441.6 5.7 %reduce-scatter.9.cloned.1.call-done = bf16[1,128,2048]{2,1,0:T(8,128)(2,1)} async-done(((bf16[4,128,2048]{2,1,0:T(8,128)(2,1)}), bf16[1,128,2048]{2,1,0:T(8,128)(2,1)}) %reduce-scatter.9.cloned.1.call-update) | async-done | bytes 524304 | tf_op jit(solution)/shard_map/reduce_scatter | solution.py:65
  457.6 4.6 collective-permute-done.59
  462.2 4.2 collective-permute-done.60
  472.3 4.9 %reduce-scatter.11.cloned.1.call-done = bf16[1,64,2176]{2,1,0:T(8,128)(2,1)} async-done(((bf16[4,64,2176]{2,1,0:T(8,128)(2,1)}), bf16[1,64,2176]{2,1,0:T(8,128)(2,1)}) %reduce-scatter.11.cloned.1.call-update) | async-done | bytes 278544 | tf_op jit(solution)/shard_map/reduce_scatter | solution.py:65
  (627 shorter events, 272.7 us)
Async XLA Ops:
  7.2 42.1 %all-gather.11.cloned.1.call-start = ((), (), s32[]{:S(2)}) async-start(), calls=%async_computation.8 | async-start | bytes 1392640 | tf_op jit(solution)/shard_map/all_gather | solution.py:61
  17.5 61.4 %all-gather.13.cloned.1.call-start = ((), (), s32[]{:S(2)}) async-start(), calls=%async_computation.9 | async-start | bytes 1310720 | tf_op jit(solution)/shard_map/all_gather | solution.py:61
  19.8 33.4 %collective-permute-start.11 = (bf16[1024,1024]{1,0:T(8,128)(2,1)}, bf16[1024,1024]{1,0:T(8,128)(2,1)}, u32[]{:S(2)}, u32[]{:S(2)}) collective-permute-start(bf16[1024,1024]{1,0:T(8,128)(2,1)} %bitcast.169), channel_id=1, source_target_pairs={{0,16},{16,0},{1,17},{17,1},{2,18},{18,2},{3,19},{19,3},{4,20},{20... | collective-permute-start | bytes 6291464 | tf_op jit(solution)/shard_map/ppermute | solution.py:49
  49.3 59.2 %all-gather.15.cloned.1.call-start = ((), (), s32[]{:S(2)}) async-start(), calls=%async_computation.10 | async-start | bytes 1310720 | tf_op jit(solution)/shard_map/all_gather | solution.py:61
  49.3 26.5 %collective-permute-start.10 = (bf16[4,64,2176]{2,1,0:T(8,128)(2,1)}, bf16[4,64,2176]{2,1,0:T(8,128)(2,1)}, u32[]{:S(2)}, u32[]{:S(2)}) collective-permute-start(bf16[4,64,2176]{2,1,0:T(8,128)(2,1)} %bitcast.146), channel_id=1, source_target_pairs={{0,2},{2,0},{1,3},{3,1},{4,6},{6,4},{5,7},{7,5},{8,10},{10,8},{9,1... | collective-permute-start | bytes 3342344 | tf_op jit(solution)/shard_map/ppermute | solution.py:49
  50.9 26.2 %collective-permute-start.9 = (bf16[4,64,2176]{2,1,0:T(8,128)(2,1)}, bf16[4,64,2176]{2,1,0:T(8,128)(2,1)}, u32[]{:S(2)}, u32[]{:S(2)}) collective-permute-start(bf16[4,64,2176]{2,1,0:T(8,128)(2,1)} %bitcast.147), channel_id=1, source_target_pairs={{0,1},{1,0},{2,3},{3,2},{4,5},{5,4},{6,7},{7,6},{8,9},{9,8},{10,11... | collective-permute-start | bytes 3342344 | tf_op jit(solution)/shard_map/ppermute | solution.py:49
  78.9 111.3 %all-gather.17.cloned.1.call-start = ((), (), s32[]{:S(2)}) async-start(), calls=%async_computation.11 | async-start | bytes 5242880 | tf_op jit(solution)/shard_map/all_gather | solution.py:61
  78.9 27.2 %collective-permute-start.12 = (bf16[4,64,2176]{2,1,0:T(8,128)(2,1)}, bf16[4,64,2176]{2,1,0:T(8,128)(2,1)S(1)}, u32[]{:S(2)}, u32[]{:S(2)}) collective-permute-start(bf16[4,64,2176]{2,1,0:T(8,128)(2,1)} %collective-permute-done.9.rest_1_), channel_id=1, source_target_pairs={{0,2},{2,0},{1,3},{3,1},{4,6},{6,4},{5,7},{7,5},{8,10},{10,8},{9,1... | collective-permute-start | bytes 3342344 | tf_op jit(solution)/shard_map/ppermute | solution.py:49
  108.5 140.2 %all-gather.19.cloned.1.call-start = ((), (), s32[]{:S(2)}) async-start(), calls=%async_computation.12 | async-start | bytes 2621440 | tf_op jit(solution)/shard_map/all_gather | solution.py:61
  108.7 28.0 %collective-permute-start.15 = (bf16[4,64,2048]{2,1,0:T(8,128)(2,1)}, bf16[4,64,2048]{2,1,0:T(8,128)(2,1)}, u32[]{:S(2)}, u32[]{:S(2)}) collective-permute-start(bf16[4,64,2048]{2,1,0:T(8,128)(2,1)} %bitcast.153), channel_id=1, source_target_pairs={{0,2},{2,0},{1,3},{3,1},{4,6},{6,4},{5,7},{7,5},{8,10},{10,8},{9,1... | collective-permute-start | bytes 3145736 | tf_op jit(solution)/shard_map/ppermute | solution.py:49
  110.3 26.4 %collective-permute-start.16 = (bf16[4,128,1024]{2,1,0:T(8,128)(2,1)}, bf16[4,128,1024]{2,1,0:T(8,128)(2,1)}, u32[]{:S(2)}, u32[]{:S(2)}) collective-permute-start(bf16[4,128,1024]{2,1,0:T(8,128)(2,1)} %bitcast.24.rest_0_), channel_id=1, source_target_pairs={{0,1},{1,0},{2,3},{3,2},{4,5},{5,4},{6,7},{7,6},{8,9},{9,8},{10,11... | collective-permute-start | bytes 3145736 | tf_op jit(solution)/shard_map/ppermute | solution.py:49
  137.2 26.3 %collective-permute-start.19 = (bf16[4,128,1024]{2,1,0:T(8,128)(2,1)}, bf16[4,128,1024]{2,1,0:T(8,128)(2,1)}, u32[]{:S(2)}, u32[]{:S(2)}) collective-permute-start(bf16[4,128,1024]{2,1,0:T(8,128)(2,1)} %bitcast.24.rest_0_), channel_id=1, source_target_pairs={{0,2},{2,0},{1,3},{3,1},{4,6},{6,4},{5,7},{7,5},{8,10},{10,8},{9,1... | collective-permute-start | bytes 3145736 | tf_op jit(solution)/shard_map/ppermute | solution.py:49
  142.2 41.9 %collective-permute-start.20 = (bf16[2,128,1024]{2,1,0:T(8,128)(2,1)}, bf16[2,128,1024]{2,1,0:T(8,128)(2,1)}, u32[]{:S(2)}, u32[]{:S(2)}) collective-permute-start(bf16[2,128,1024]{2,1,0:T(8,128)(2,1)} %slice.133), channel_id=1, source_target_pairs={{0,2},{2,0},{1,3},{3,1},{4,6},{6,4},{5,7},{7,5},{8,10},{10,8},{9,1... | collective-permute-start | bytes 1572872 | tf_op jit(solution)/shard_map/ppermute | solution.py:49
  166.2 238.8 %reduce-scatter.7.cloned.1.call-start = ((), (), s32[]{:S(2)}) async-start(), calls=%async_computation.5 | async-start | bytes 2621440 | tf_op jit(solution)/shard_map/reduce_scatter | solution.py:65
  219.7 28.9 %collective-permute-start.29 = (bf16[128,1024]{1,0:T(8,128)(2,1)}, bf16[128,1024]{1,0:T(8,128)(2,1)}, u32[]{:S(2)}, u32[]{:S(2)}) collective-permute-start(bf16[128,1024]{1,0:T(8,128)(2,1)} %get-tuple-element.245.d0), channel_id=1, source_target_pairs={{0,2},{1,3},{2,0},{3,1},{4,6},{5,7},{6,4},{7,5},{8,10},{9,11},{10,... | collective-permute-start | bytes 786440 | tf_op jit(solution)/shard_map/ppermute | solution.py:53
  221.2 27.5 %collective-permute-start.30 = (bf16[128,1024]{1,0:T(8,128)(2,1)}, bf16[128,1024]{1,0:T(8,128)(2,1)}, u32[]{:S(2)}, u32[]{:S(2)}) collective-permute-start(bf16[128,1024]{1,0:T(8,128)(2,1)} %get-tuple-element.245.d0), channel_id=1, source_target_pairs={{0,3},{1,2},{2,1},{3,0},{4,7},{5,6},{6,5},{7,4},{8,11},{9,10},{10,... | collective-permute-start | bytes 786440 | tf_op jit(solution)/shard_map/ppermute | solution.py:53
  222.6 26.0 %collective-permute-start.25 = (bf16[128,1024]{1,0:T(8,128)(2,1)}, bf16[128,1024]{1,0:T(8,128)(2,1)}, u32[]{:S(2)}, u32[]{:S(2)}) collective-permute-start(bf16[128,1024]{1,0:T(8,128)(2,1)} %shard_map.207.m0), channel_id=1, source_target_pairs={{0,1},{1,0},{2,3},{3,2},{4,5},{5,4},{6,7},{7,6},{8,9},{9,8},{10,11... | collective-permute-start | bytes 786440 | tf_op jit(solution)/shard_map/ppermute | solution.py:53
  260.9 156.5 %reduce-scatter.5.cloned.1.call-start = ((), (), s32[]{:S(2)}) async-start(), calls=%async_computation.4 | async-start | bytes 5242880 | tf_op jit(solution)/shard_map/reduce_scatter | solution.py:65
  289.9 28.6 %collective-permute-start.41 = (bf16[512,512]{1,0:T(8,128)(2,1)S(1)}, bf16[512,512]{1,0:T(8,128)(2,1)S(1)}, u32[]{:S(2)}, u32[]{:S(2)}) collective-permute-start(bf16[512,512]{1,0:T(8,128)(2,1)S(1)} %constant_dynamic-slice_fusion.1), channel_id=1, source_target_pairs={{0,16},{16,0},{1,17},{17,1},{2,18},{18,2},{3,19},{19,3},{4,20},{20... | collective-permute-start | bytes 1572872 | tf_op jit(solution)/shard_map/ppermute | solution.py:49
  326.4 120.9 %reduce-scatter.9.cloned.1.call-start = ((), (), s32[]{:S(2)}) async-start(), calls=%async_computation.6 | async-start | bytes 2621440 | tf_op jit(solution)/shard_map/reduce_scatter | solution.py:65
  400.8 76.5 %reduce-scatter.11.cloned.1.call-start = ((), (), s32[]{:S(2)}) async-start(), calls=%async_computation.7 | async-start | bytes 1392640 | tf_op jit(solution)/shard_map/reduce_scatter | solution.py:65
  402.3 25.7 %collective-permute-start.57 = (bf16[1024,1024]{1,0:T(8,128)(2,1)}, bf16[1024,1024]{1,0:T(8,128)(2,1)}, u32[]{:S(2)}, u32[]{:S(2)}) collective-permute-start(bf16[1024,1024]{1,0:T(8,128)(2,1)} %copy-done.51), channel_id=1, source_target_pairs={{0,16},{16,0},{1,17},{17,1},{2,18},{18,2},{3,19},{19,3},{4,20},{20... | collective-permute-start | bytes 6291464 | tf_op jit(solution)/shard_map/ppermute | solution.py:49
  402.3 33.6 %collective-permute-start.55 = (bf16[2,64,2176]{2,1,0:T(8,128)(2,1)}, bf16[2,64,2176]{2,1,0:T(8,128)(2,1)S(1)}, u32[]{:S(2)}, u32[]{:S(2)}) collective-permute-start(bf16[2,64,2176]{2,1,0:T(8,128)(2,1)} %get-tuple-element.349), channel_id=1, source_target_pairs={{0,1},{1,0},{2,3},{3,2},{4,5},{5,4},{6,7},{7,6},{8,9},{9,8},{10,11... | collective-permute-start | bytes 1671176 | tf_op jit(solution)/shard_map/ppermute | solution.py:49
  403.8 32.0 %collective-permute-start.56 = (bf16[2,64,2176]{2,1,0:T(8,128)(2,1)}, bf16[2,64,2176]{2,1,0:T(8,128)(2,1)S(1)}, u32[]{:S(2)}, u32[]{:S(2)}) collective-permute-start(bf16[2,64,2176]{2,1,0:T(8,128)(2,1)} %copy-done.135), channel_id=1, source_target_pairs={{0,2},{2,0},{1,3},{3,1},{4,6},{6,4},{5,7},{7,5},{8,10},{10,8},{9,1... | collective-permute-start | bytes 1671176 | tf_op jit(solution)/shard_map/ppermute | solution.py:49
  (204 other events, 1541.6 us)
Sparse Core Ops, SparseCore 0:
  17.6 31.6 all-gather.10
  51.4 27.3 all-gather.12
  81.0 27.4 all-gather.14
  109.9 80.2 all-gather.16
  191.6 44.4 all-gather.18
  261.1 40.4 reduce-scatter.6
  326.5 74.0 reduce-scatter.4
  402.9 44.3 reduce-scatter.8
  449.7 27.4 reduce-scatter.10

commit v4 on v3

--- a/solution.py
+++ b/solution.py
@@ -247,8 +247,8 @@
     )(arrays[0], seg[:, :, None], seg[:, None, :], *arrays[1:], weights)
 
 
-def attn_grad_kernel(relative, count, me_ref, a_ref, d_ref, *refs):
-    beside, refs = refs[:count], refs[count:]
+def attn_grad_kernel(relative, count, earlier, me_ref, a_ref, d_ref, *refs):
+    beside, refs = refs[:count], refs[count + earlier :]
     out = refs[-1] if relative else refs[0]
     product = mm_rows(a_ref[...], d_ref[...]).astype(bf16)
     out[:, :, :, : 3 * HALF] = product.reshape(*out.shape[:3], 3 * HALF)
@@ -264,7 +264,7 @@
                 refs[2 * j + h][...] = out[:, me_ref[0] ^ j]
 
 
-def attn_grad(me, relative, depth, a, dqkv, *beside):
+def attn_grad(me, relative, depth, a, dqkv, *beside, earlier=()):
     tokens, step = a.shape[0], D // 4
     rows = D // (4 * depth)
     deep = step // (4 * rows)
@@ -278,7 +278,7 @@
         block = pl.BlockSpec((deep, 4, rows, width), lambda i: (i, 0, 0, 0))
         outs = [((depth, 4, rows, width), bf16, block)]
     found = tiled_call(
-        functools.partial(attn_grad_kernel, relative, len(beside)),
+        functools.partial(attn_grad_kernel, relative, len(beside), len(earlier)),
         D // step,
         outs,
         [
@@ -286,7 +286,8 @@
             (a, pl.BlockSpec((tokens, step), lambda i: (0, i))),
             (dqkv, resident(dqkv.shape)),
         ]
-        + [(v, pl.BlockSpec((step, v.shape[1]), lambda i: (i, 0))) for v in beside],
+        + [(v, pl.BlockSpec((step, v.shape[1]), lambda i: (i, 0))) for v in beside]
+        + [(v, pl.BlockSpec((1, *v.shape[1:]), lambda i: (0, 0, 0))) for v in earlier],
         [pltpu.VMEM((deep, 4, rows, width), bf16)] if relative else [],
     )
     return pairs_of(found) if relative else found[0]
@@ -315,7 +316,7 @@
     return pl.BlockSpec(shape, lambda i: (0, 0), pipeline_mode=pl.Buffered(1))
 
 
-def tiled_call(kernel, steps, outs, ins, scratch=()):
+def tiled_call(kernel, steps, outs, ins, scratch=(), room=56):
     return pl.pallas_call(
         kernel,
         grid=(steps,),
@@ -323,9 +324,25 @@
         in_specs=[spec for _, spec in ins],
         out_specs=[spec for _, _, spec in outs],
         scratch_shapes=list(scratch),
-        compiler_params=pltpu.CompilerParams(vmem_limit_bytes=20 << 20),
+        compiler_params=pltpu.CompilerParams(vmem_limit_bytes=room << 20),
         cost_estimate=light,
     )(*[v for v, _ in ins])
+
+
+def shard_kernel(core_ref, qkv_ref, wo_ref, keep_strip, send_strip, keep_ref, send_ref):
+    for h, (first_half, second_half) in enumerate(((keep_ref, send_ref), (send_ref, keep_ref))):
+
+        @pl.when(core_ref[0] == h)
+        def _(outs=(first_half, second_half)):
+            for k, out in enumerate(outs):
+                for t in range(3):
+                    low = t * D + k * HALF
+                    cut = qkv_ref[:, low : low + HALF]
+                    out[:, t * HALF : (t + 1) * HALF] = cut.astype(bf16)
+                out[:, 3 * HALF : 4 * HALF] = wo_ref[:, k * HALF : (k + 1) * HALF].astype(bf16)
+
+    keep_ref[:, 4 * HALF :] = keep_strip[...]
+    send_ref[:, 4 * HALF :] = send_strip[...]
 
 
 def copy_weights(spans, low, high, me, pieces, w_ref, sems):
@@ -370,8 +387,9 @@
     )
 
 
-def down_kernel(g_ref, w_ref, out_ref):
+def down_kernel(g_ref, w_ref, out_ref, done_ref):
     out_ref[...] = mm(g_ref[...], w_ref[...]).astype(bf16)
+    done_ref[...] = jnp.zeros_like(done_ref)
 
 
 def down_product(g, w, step=256):
@@ -379,9 +397,13 @@
     return tiled_call(
         down_kernel,
         tokens // step,
-        [((tokens, D), bf16, pl.BlockSpec((step, D), lambda i: (i, 0)))],
+        [
+            ((tokens, D), bf16, pl.BlockSpec((step, D), lambda i: (i, 0))),
+            (*mark, pl.BlockSpec(mark[0], lambda i: (0, 0))),
+        ],
         [(g, pl.BlockSpec((step, width), lambda i: (i, 0))), (w, resident(w.shape))],
-    )[0]
+        room=20,
+    )
 
 
 def choose_kernel(
@@ -500,7 +522,7 @@
             out_specs=[pl.BlockSpec((depth, units, D), lambda i, me: (0, 0, 0))] * len(chips),
         ),
         out_shape=[jax.ShapeDtypeStruct((depth, units, D), bf16)] * len(chips),
-        compiler_params=pltpu.CompilerParams(vmem_limit_bytes=20 << 20),
+        compiler_params=pltpu.CompilerParams(vmem_limit_bytes=56 << 20),
         cost_estimate=light,
     )(jnp.reshape(me, (1,)), g, d)
 
@@ -622,6 +644,7 @@
             (w_up, pl.BlockSpec((D, step), lambda i: (0, i))),
         ],
         [pltpu.VMEM((tokens, D), f32)],
+        room=36,
     )
 
 
@@ -664,7 +687,7 @@
 
 
 def up_rest_kernel(
-    me_ref, picked_ref, gy_ref, wd_ref, slope_ref, du_ref, m_ref, wu_ref, dm_in, *refs
+    me_ref, picked_ref, gy_ref, wd_ref, slope_ref, du_ref, m_ref, wu_ref, dm_in, _, *refs
 ):
     outs, (dm_ref, gb_ref, du, acc, gw) = refs[:8], refs[8:]
     half = gw.shape[0] // 2
@@ -699,7 +722,7 @@
             dm_ref[at] = put_rows(dm_in[at], cut, picked_ref[s], length).astype(bf16)
 
 
-def up_rest(me, depth, picked, gy, w_down, slope, du, m, w_up, dm, step=512):
+def up_rest(me, depth, picked, gy, w_down, slope, du, m, w_up, dm, earlier, step=512):
     tokens, width = du.shape
     rows = D // (4 * depth)
     tall = lambda height: pl.BlockSpec((height, step), lambda i: (0, i))
@@ -723,6 +746,7 @@
             (m, once(m)),
             (w_up, tall(D)),
             (dm, once(dm)),
+            (earlier, pl.BlockSpec((1, 1, *earlier.shape[2:]), lambda i: (0, 0, 0, 0))),
         ],
         [
             pltpu.VMEM((tokens, step), bf16),
@@ -730,19 +754,6 @@
             pltpu.VMEM((depth, 4, rows, step), bf16),
         ],
     )
-
-
-def sum_both_kernel(*refs):
-    out_ref = refs[-1]
-    for h in range(2):
-        down, up = refs[3 * h : 3 * h + 3], refs[6 + 3 * h : 9 + 3 * h]
-        depth, rows = up[0].shape[:2]
-        at = slice(h * depth, (h + 1) * depth)
-        add = lambda these: sum(ref[...].astype(f32) for ref in these).astype(bf16)
-        out_ref[at, :rows] = add(up)
-        total = add(down)
-        out_ref[at, rows:, :D] = total[:, :rows]
-        out_ref[at, rows:, D:] = total[:, rows:]
 
 
 def order_rows_kernel(me_ref, *refs):
@@ -777,7 +788,7 @@
         out_ref[:, pl.ds(start, width)] = ref[...]
 
 
-def routed_attn_kernel(count, a_ref, seg_col_ref, seg_row_ref, w_ref, qkv_ref, o_ref):
+def routed_attn_kernel(count, a_ref, seg_col_ref, seg_row_ref, w_ref, _, qkv_ref, o_ref):
     weights = w_ref[:, :, :, : 3 * HALF].reshape(D, 3 * HALF)
     qkv_ref[...] = mm(a_ref[...], weights).astype(bf16)
     attend_kernel(count, HALF // LANES, count, qkv_ref, seg_col_ref, seg_row_ref, o_ref)
@@ -955,8 +966,6 @@
     micro, length = boundary_in.shape[1], boundary_in.shape[3]
     tokens = micro * length
 
-    qkv_halves = w_qkv[0].astype(bf16).reshape(rows, 3, 2, HALF)
-    out_halves = w_out[0].astype(bf16).reshape(rows, 2, HALF)
     up_halves = w_up[0].astype(bf16).reshape(rows, depth, 4, 2, half_units)
     down_halves = w_down[0].astype(bf16).reshape(2, half_units, D)
     bias_cols = half_units // rows
@@ -975,13 +984,16 @@
             [jnp.where(first, strip, none), jnp.where(first, none, strip)], axis=1
         )
         strip = jnp.pad(strip, ((0, 0), (0, LANES - 16)))
-        attn = jnp.concatenate(
-            [pick(qkv_halves, 2).reshape(rows, 3 * HALF), pick(out_halves, 1), strip], axis=1
-        )
         up = pick(up_halves, 3).transpose(0, 2, 1, 3).reshape(rows, D * 2)
-        return attn, up, pick(down_halves, 0)
-
-    kept, sent = half(core), half(1 - core)
+        return strip, up, pick(down_halves, 0)
+
+    kept, sent = list(half(core)), list(half(1 - core))
+    kept[0], sent[0] = whole(
+        shard_kernel,
+        [((rows, 4 * HALF + LANES), bf16)] * 2,
+        [core],
+        [w_qkv[0], w_out[0], kept[0], sent[0]],
+    )
     came = tuple(swap(v, "section") for v in sent)
     width = 4 * HALF
     shard0 = [jnp.where(first, k, r) for k, r in zip(kept, came)]
@@ -1085,14 +1097,15 @@
     (w_u0,) = place(me, [own_u, px_u, py_u, pd_u], spans_all, ((0, D * 2),))
     w_u0 = w_u0.reshape(D, D * 2)
     g0, slope0 = up_product(m0, w_u0, bias_up0)
-    g0, pd_d0, pd_d1, w_r1 = fence(g0, pd_d0, pd_d1, w_r1)
+    g0, pd_d0, pd_d1 = fence(g0, pd_d0, pd_d1)
 
     spans_cut = spans_all[:3] + [(3, 0, halfway), (3, halfway, depth)]
     (w_d0,) = place(
         me, [own_d, px_d, py_d, pd_d0, pd_d1], spans_cut, ((0, D),), plane_first=True
     )
     w_d0 = w_d0.reshape(D * 2, D)
-    e_part = down_product(g0, w_d0)
+    e_part, down_done = down_product(g0, w_d0)
+    w_r1, down_done = fence(w_r1, down_done)
     w_o1 = whole_out(w_r1[..., 3 * HALF :])
 
     y0_b, chosen, grad_chosen, weight, de1, a1 = choose_rows(
@@ -1103,7 +1116,7 @@
         functools.partial(routed_attn_kernel, count),
         [((chosen_rows, 3 * HALF), bf16), ((chosen_rows, HALF), bf16)],
         [],
-        [a1, seg1_col, seg1_row, w_r1],
+        [a1, seg1_col, seg1_row, w_r1, down_done],
     )
     z_part = mm(o1, w_o1).astype(bf16)
     z_recv = swap(z_part, "section")
@@ -1207,7 +1220,7 @@
     gw_d0 = down_rest(me, gy_rows, g_rows, pre_d)
     gw_d0, gy_rows = fence(gw_d0, gy_rows)
     diag_d, far_d = send_diagonal(gw_d0), send_far(gw_d0)
-    attn1 = attn_grad(me, False, depth, a1, dqkv1, gw_o1)
+    attn1 = attn_grad(me, False, depth, a1, dqkv1, gw_o1, earlier=[gw_d0[0][0]])
     *gw_u0, dm_part, gb_u0 = up_rest(
         me,
         depth,
@@ -1219,22 +1232,30 @@
         m0,
         w_u0,
         pre_dm,
-    )
-    diag_d, far_d, gw_u0, dm_part, gy0_b, attn1 = fence(
-        diag_d, far_d, pairs_of(gw_u0), dm_part, gy0_b, attn1
-    )
-
+        attn1,
+    )
     r_a1 = reduce_z(attn1)
+    diag_d, far_d, gw_u0, dm_part, gy0_b = fence(
+        diag_d, far_d, pairs_of(gw_u0), dm_part, gy0_b
+    )
+
     diag_u = send_diagonal(gw_u0)
     near_d = send_near(near(gw_d0, diag_d))
     dz0, gy_dh0, do0, gg_mlp0, g_down0 = norm_back_product(
         dm_part, swap(dm_part, "section"), h0, gain_mlp0, gy0_b, w_o0
     )
-    gw_o0 = out_by_columns(mm_rows(o0, dz0).astype(bf16))
     dqkv0, da_part, gg_attn0 = attention_call(
         attend_back_out_kernel, seg, [qkv0, do0, x_b], w_q0, 3 * HALF, sums=1
     )
-    diag_u, near_d, dqkv0, da_part, gw_o0 = fence(diag_u, near_d, dqkv0, da_part, gw_o0)
+    diag_u, near_d, dqkv0, da_part, dz0 = fence(diag_u, near_d, dqkv0, da_part, dz0)
+    gw_o0 = out_by_columns(mm_rows(o0, dz0).astype(bf16))
+    (sum_d,) = whole(
+        halves_kernel,
+        [((depth, half_units, D), bf16)],
+        [],
+        parts(gw_d0, near_d, far_d),
+    )
+    r_d0 = reduce_z(sum_d)
 
     far_u = send_far(gw_u0)
     near_u = send_near(near(gw_u0, diag_u))
@@ -1256,13 +1277,13 @@
     attn0, near_u, far_u, da_part = fence(attn0, near_u, far_u, da_part)
 
     diag_q, far_q = send_diagonal(attn0), send_far(attn0)
-    (sum_du,) = whole(
-        sum_both_kernel,
-        [((depth, 2 * rows, 2 * D), bf16)],
+    (sum_u,) = whole(
+        halves_kernel,
+        [((depth, rows, 2 * D), bf16)],
         [],
-        parts(gw_d0, near_d, far_d) + parts(gw_u0, near_u, far_u),
-    )
-    r_du = reduce_z(sum_du)
+        parts(gw_u0, near_u, far_u),
+    )
+    r_u0 = reduce_z(sum_u)
     dx0_b = last_rows(da_part, swap(da_part, "section"), x_b, gain_attn0, gy_dh0)
     (y1_b,) = whole(
         routed_sum_kernel,
@@ -1282,9 +1303,7 @@
         [],
         parts(attn0, near_q, far_q),
     )
-    sum_q, r_a1, r_m1, r_du = fence(sum_q, r_a1, r_m1, r_du)
-    r_u0 = r_du[:rows]
-    r_d0 = jnp.concatenate([r_du[rows:, :D], r_du[rows:, D:]], axis=0)
+    sum_q, r_a1, r_m1, r_d0 = fence(sum_q, r_a1, r_m1, r_d0)
     r_a0 = reduce_z(sum_q)
     r_a1 = plus(part(r_a1, 0), *[to_plane(part(r_a1, j), j) for j in (1, 2, 3)])
     up = r_m1[: 4 * rows].reshape(4, rows, hidden)

time: 500 us -> 480 us (0.960)
  local copies, waits for them, and re-layouts: 103 us -> 63.5 us
  Pallas kernels: 131 us -> 166 us
  waiting for transfers between devices: 141 us -> 120 us
  other arithmetic: 34.1 us -> 42.4 us
    unnamed x311 -> x201, local copies, waits for them, and re-layouts: 79.8 us -> 43.5 us
    pallas_call x11, Pallas kernels: 64.8 us -> 93.5 us  [tiled_call(): pl.pallas_call(kernel, grid=(steps,), out_shape=[jax.ShapeDtypeStruct(sha...]
    ppermute x47, waiting for transfers between devices: 92.9 us -> 84.2 us  [swap(): return lax.ppermute(v, axis, [(0, 1), (1, 0)])]
    reduce_scatter x4 -> x5, waiting for transfers between devices: 10.7 us -> 2.07 us  [reduce_z(): return lax.psum_scatter(part, 'z', scatter_dimension=0, tiled=False)]
    pallas_call x16 -> x18, Pallas kernels: 27.8 us -> 31.5 us  [whole(): pl.pallas_call(kernel, out_shape=[jax.ShapeDtypeStruct(shape, dtype) for...]
  transfers between devices with their start and end apart: 77 -> 78, of which waited for: 35 -> 29; matrix products, arithmetic and copies ran while one was open for 10% -> 12% of each run, Pallas kernels for 25% -> 34%
where the time goes in v4:
time: 480 us; the launch traced here: 474 us
  Pallas kernels  166 us (35%)
  waiting for transfers between devices  120 us (25%)
  local copies, waits for them, and re-layouts  63.5 us (13%)
  starting transfers between devices  62.7 us (13%)
  other arithmetic  42.4 us (9%)
  between operations  15.8 us (3%)
    pallas_call x11, Pallas kernels, tiled_call(): pl.pallas_call(kernel, grid=(steps,), out_shape=[jax.ShapeDtypeStruct(sha...  93.5 us
    ppermute x47, waiting for transfers between devices, swap(): return lax.ppermute(v, axis, [(0, 1), (1, 0)])  84.2 us
    unnamed x201, local copies, waits for them, and re-layouts  43.5 us
    ppermute x47, starting transfers between devices, swap(): return lax.ppermute(v, axis, [(0, 1), (1, 0)])  34.3 us
    pallas_call x18, Pallas kernels, whole(): pl.pallas_call(kernel, out_shape=[jax.ShapeDtypeStruct(shape, dtype) for...  31.5 us
    ppermute x21, starting transfers between devices, to_plane(): return lax.ppermute(v, ('y', 'x'), [(i, i ^ j) for i in range(4)])  27.7 us
    ppermute x21, waiting for transfers between devices, to_plane(): return lax.ppermute(v, ('y', 'x'), [(i, i ^ j) for i in range(4)])  23.3 us
    pallas_call x2, Pallas kernels, attention_call(): pl.pallas_call(functools.partial(kernel, LANES, pairs, length), grid=(cou...  22.4 us
  transfers between devices with their start and end apart: 78, of which 29 were waited for; matrix products, arithmetic and copies ran while one was open for 12% of the time, Pallas kernels for 34%

profile of v4, /device:TPU:0, one launch (start us, length us, event | category | flops | bytes accessed | tf_op | source)
XLA Modules:
  0.0 473.5 jit_solution(1675684427793040339)
XLA Ops:
  31.0 9.6 %collective-permute-done.7.u3 = bf16[64,512]{1,0:T(8,128)(2,1)S(1)} collective-permute-done((bf16[64,512]{1,0:T(8,128)(2,1)S(1)}, bf16[64,512]{1,0:T(8,128)(2,1)S(1)}, u32[]{:S(2)}, u32[]{:S(2)}) %collective-permute-start.7) | collective-permute-done | bytes 65568 | tf_op jit(solution)/shard_map/ppermute | solution.py:53
  42.5 5.1 %all-gather.11.cloned.1.call-done = bf16[256,2176]{1,0:T(8,128)(2,1)} async-done(((bf16[64,2176]{1,0:T(8,128)(2,1)}), bf16[256,2176]{1,0:T(8,128)(2,1)}) %all-gather.11.cloned.1.call-update) | async-done | bytes 1114128 | tf_op jit(solution)/shard_map/all_gather | solution.py:61
  55.1 19.1 %collective-permute-done.10.rest_2_ = bf16[4,64,2176]{2,1,0:T(8,128)(2,1)} collective-permute-done((bf16[4,64,2176]{2,1,0:T(8,128)(2,1)}, bf16[4,64,2176]{2,1,0:T(8,128)(2,1)}, u32[]{:S(2)}, u32[]{:S(2)}) %collective-permute-start.10) | collective-permute-done | bytes 1114144 | tf_op jit(solution)/shard_map/ppermute | solution.py:49
  80.3 23.2 %collective-permute-done.13.rest_1_ = bf16[4,64,2048]{2,1,0:T(8,128)(2,1)S(1)} collective-permute-done((bf16[4,64,2048]{2,1,0:T(8,128)(2,1)}, bf16[4,64,2048]{2,1,0:T(8,128)(2,1)S(1)}, u32[]{:S(2)}, u32[]{:S(2)}) %collective-permute-start.13) | collective-permute-done | bytes 1048608 | tf_op jit(solution)/shard_map/ppermute | solution.py:49
  117.4 5.1 %shard_map.199 = (bf16[4,4,64,1536]{3,2,1,0:T(8,128)(2,1)S(1)}, bf16[1024,1024]{1,0:T(8,128)(2,1)S(1)}, bf16[1024,1536]{1,0:T(8,128)(2,1)S(1)}) custom-call(s32[1]{0:T(128)} %bitcast.me_ref, bf16[1024,1024]{1,0:T(8,128)(2,1)S(1)} %get-tuple-element.206.x_ref, f32[1,1024]{1,0:T(1,128)S(1)} %get-tuple-element.505.gain_ref, bf16[4,64,2176]{2,1,0:T(8,128)(2,1)S(1)} %bitcast.148, ...), custom_call_target="tpu_custom_call" | custom-call | flops 1 | bytes 1 | tf_op jit(solution)/shard_map/pallas_call | solution.py:302
  127.5 5.7 %shard_map.200 = (bf16[1024,512]{1,0:T(8,128)(2,1)S(1)}, bf16[1024,1024]{1,0:T(8,128)(2,1)S(1)}) custom-call(bf16[1024,1536]{1,0:T(8,128)(2,1)S(1)} %get-tuple-element.219.qkv_ref, s32[2,512,1]{2,1,0:T(8,128)S(1)} %copy-done.14, s32[2,1,512]{2,1,0:T(1,128)S(1)} %copy-done.70, bf16[512,1024]{1,0:T(8,128)(2,1)S(1)} %pad_maximum_fusion.w_ref), custom_call_target="tpu_custom_call" | custom-call | flops 1 | bytes 1 | tf_op jit(solution)/shard_map/pallas_call | solution.py:229
  142.1 6.3 %shard_map.201 = (f32[1024,1024]{1,0:T(8,128)}, bf16[1024,1024]{1,0:T(8,128)(2,1)}) custom-call(bf16[1024,1024]{1,0:T(8,128)(2,1)} %copy-done.3, bf16[1024,1024]{1,0:T(8,128)(2,1)} %copy-done.32, bf16[1024,1024]{1,0:T(8,128)(2,1)} %collective-permute-done.17.recv_ref, f32[1,1024]{1,0:T(1,128)} %get-tuple-element.504.gain_ref), custom_call_target="tpu_custom_call" | custom-call | flops 1 | bytes 1 | tf_op jit(solution)/shard_map/pallas_call | solution.py:320
  148.4 12.6 %collective-permute-done.19.rest_2_ = bf16[4,128,1024]{2,1,0:T(8,128)(2,1)S(1)} collective-permute-done((bf16[4,128,1024]{2,1,0:T(8,128)(2,1)}, bf16[4,128,1024]{2,1,0:T(8,128)(2,1)S(1)}, u32[]{:S(2)}, u32[]{:S(2)}) %collective-permute-start.19) | collective-permute-done | bytes 1048608 | tf_op jit(solution)/shard_map/ppermute | solution.py:49
  167.2 11.2 %shard_map.203 = (bf16[1024,2048]{1,0:T(8,128)(2,1)}, bf16[1024,2048]{1,0:T(8,128)(2,1)}) custom-call(bf16[1024,1024]{1,0:T(8,128)(2,1)} %get-tuple-element.231.m_ref, bf16[1024,2048]{1,0:T(8,128)(2,1)} %bitcast.136, f32[1,2048]{1,0:T(1,128)} %reshape.181.b_ref), custom_call_target="tpu_custom_call" | custom-call | flops 1 | bytes 1 | tf_op jit(solution)/shard_map/pallas_call | solution.py:320
  181.7 5.0 %shard_map.205 = (bf16[1024,1024]{1,0:T(8,128)(2,1)S(1)}, f32[8,128]{1,0:T(8,128)S(1)}) custom-call(bf16[1024,2048]{1,0:T(8,128)(2,1)S(1)} %copy-done.5, bf16[2048,1024]{1,0:T(8,128)(2,1)S(1)} %bitcast.139), custom_call_target="tpu_custom_call" | custom-call | flops 1 | bytes 1 | tf_op jit(solution)/shard_map/pallas_call | solution.py:320
  191.8 6.2 %shard_map.206 = (bf16[1024,1024]{1,0:T(8,128)(2,1)}, bf16[128,1024]{1,0:T(8,128)(2,1)}, bf16[128,1024]{1,0:T(8,128)(2,1)}, f32[128,1]{1,0:T(8,128)}, bf16[128,1...) custom-call(f32[1024,1024]{1,0:T(8,128)} %get-tuple-element.228.h_ref, bf16[1024,1024]{1,0:T(8,128)(2,1)} %copy-done.33, ...), custom_call_target="tpu_custom_call" | custom-call | flops 1 | bytes 1 | tf_op jit(solution)/shard_map/pallas_call | solution.py:320
  218.5 12.8 %shard_map.209 = (bf16[1024,2048]{1,0:T(8,128)(2,1)S(1)}, bf16[1024,1024]{1,0:T(8,128)(2,1)S(1)}, f32[8,128]{1,0:T(8,128)S(1)}) custom-call(bf16[1024,1024]{1,0:T(8,128)(2,1)S(1)} %copy-done.8, bf16[2048,1024]{1,0:T(8,128)(2,1)S(1)} %bitcast.141, bf16[1024,2048]{1,0:T(8,128)(2,1)S(1)} %copy-done.10, bf16[1024,2048]{1,0:T(8,128)(2,1)} %bitcast.137), custom_call_target="tpu_custom_call" | custom-call | flops 1 | bytes 1 | tf_op jit(solution)/shard_map/pallas_call | solution.py:320
  256.0 9.6 %shard_map.213 = (bf16[4,128,1024]{2,1,0:T(8,128)(2,1)}, bf16[4,128,1024]{2,1,0:T(8,128)(2,1)}, bf16[4,128,1024]{2,1,0:T(8,128)(2,1)}, bf16[4,128,1024]{2,1,0:T(8,128)(2,1)}) custom-call(s32[1]{0:T(128)} %bitcast.me_ref, bf16[1024,2048]{1,0:T(8,128)(2,1)} %get-tuple-element.239.g_ref.refs_1_, bf16[1024,1024]{1,0:T(8,128)(2,1)} %get-tuple-element.257.d_ref), custom_call_target="tpu_custom_call" | custom-call | flops 1 | bytes 1 | tf_op jit(solution)/shard_map/pallas_call | solution.py:513
  265.6 5.3 %shard_map.214 = (bf16[128,2048]{1,0:T(8,128)(2,1)}, bf16[128,2048]{1,0:T(8,128)(2,1)}, f32[8,128]{1,0:T(8,128)}) custom-call(s32[2,64,1]{2,1,0:T(8,128)} %copy.183.picked_ref, bf16[4,128,1024]{2,1,0:T(8,128)(2,1)} %get-tuple-element.271.refs_0_, bf16[1024,2048]{1,0:T(8,128)(2,1)} %get-tuple-element.239.g_ref.refs_1_, ...), custom_call_target="tpu_custom_call" | custom-call | flops 1 | bytes 1 | tf_op jit(solution)/shard_map/pallas_call | solution.py:320
  289.1 5.0 %shard_map.219._ = bf16[4,4,64,2048]{3,2,1,0:T(8,128)(2,1)} custom-call(s32[1]{0:T(128)} %bitcast.me_ref, bf16[128,1024]{1,0:T(8,128)(2,1)} %get-tuple-element.245.a_ref, bf16[128,1536]{1,0:T(8,128)(2,1)} %copy-done.58, bf16[1024,512]{1,0:T(8,128)(2,1)} %pad_maximum_fusion.2.refs_0_, bf16[2,128,1024]{2,1,0:T(8,128)(2,1)} %copy-done.34), custom_call_target="tpu_custom_call" | custom-call | flops 1 | bytes 1 | tf_op jit(solution)/shard_map/pallas_call | solution.py:320
  298.3 16.6 %shard_map.220 = (bf16[2,64,2048]{2,1,0:T(8,128)(2,1)}, bf16[2,64,2048]{2,1,0:T(8,128)(2,1)}, bf16[2,64,2048]{2,1,0:T(8,128)(2,1)}, bf16[2,64,2048]{2,1,0:T(8,12...) custom-call(s32[1]{0:T(128)} %bitcast.me_ref, ...), custom_call_target="tpu_custom_call" | custom-call | flops 1 | bytes 1 | tf_op jit(solution)/shard_map/pallas_call | solution.py:320
  314.9 4.8 %collective-permute-done.39.refs_2_ = bf16[2,128,1024]{2,1,0:T(8,128)(2,1)S(1)} collective-permute-done((bf16[2,128,1024]{2,1,0:T(8,128)(2,1)}, bf16[2,128,1024]{2,1,0:T(8,128)(2,1)S(1)}, u32[]{:S(2)}, u32[]{:S(2)}) %collective-permute-start.39) | collective-permute-done | bytes 524320 | tf_op jit(solution)/shard_map/ppermute | solution.py:49
  332.2 9.8 %shard_map.221 = (bf16[1024,1024]{1,0:T(8,128)(2,1)}, f32[1024,1024]{1,0:T(8,128)}, bf16[1024,512]{1,0:T(8,128)(2,1)}, f32[1,1024]{1,0:T(1,128)}, f32[1,1024]{1,0:T(1,128)}) custom-call(bf16[1024,1024]{1,0:T(8,128)(2,1)} %get-tuple-element.319.part_ref, bf16[1024,1024]{1,0:T(8,128)(2,1)} %collective-permute-done.46.recv_ref, ...), custom_call_target="tpu_custom_call" | custom-call | flops 1 | bytes 1 | tf_op jit(solution)/shard_map/pallas_call | solution.py:320
  345.1 16.8 %shard_map.222 = (bf16[1024,1536]{1,0:T(8,128)(2,1)S(1)}, bf16[1024,1024]{1,0:T(8,128)(2,1)}, f32[1,1024]{1,0:T(1,128)S(1)}) custom-call(bf16[1024,1536]{1,0:T(8,128)(2,1)S(1)} %copy-done.12, s32[2,512,1]{2,1,0:T(8,128)S(1)} %copy-done.15, s32[2,1,512]{2,1,0:T(1,128)S(1)} %copy-done.70, bf16[1024,512]{1,0:T(8,128)(2,1)S(1)} %copy-done.43, ...), custom_call_target="tpu_custom_call" | custom-call | flops 1 | bytes 1 | tf_op jit(solution)/shard_map/pallas_call | solution.py:229
  380.2 8.7 %shard_map.223 = (bf16[2,64,2176]{2,1,0:T(8,128)(2,1)}, bf16[2,64,2176]{2,1,0:T(8,128)(2,1)}, bf16[2,64,2176]{2,1,0:T(8,128)(2,1)}, bf16[2,64,2176]{2,1,0:T(8,12...) custom-call(s32[1]{0:T(128)} %bitcast.me_ref, ...), custom_call_target="tpu_custom_call" | custom-call | flops 1 | bytes 1 | tf_op jit(solution)/shard_map/pallas_call | solution.py:320
  397.0 9.1 %collective-permute-done.52 = bf16[2,64,2176]{2,1,0:T(8,128)(2,1)} collective-permute-done((bf16[2,64,2176]{2,1,0:T(8,128)(2,1)}, bf16[2,64,2176]{2,1,0:T(8,128)(2,1)}, u32[]{:S(2)}, u32[]{:S(2)}) %collective-permute-start.52) | collective-permute-done | bytes 557088 | tf_op jit(solution)/shard_map/ppermute | solution.py:49
  415.6 6.7 %shard_map.224 = bf16[1024,1024]{1,0:T(8,128)(2,1)} custom-call(bf16[1024,1024]{1,0:T(8,128)(2,1)} %get-tuple-element.360.part_ref, bf16[1024,1024]{1,0:T(8,128)(2,1)} %collective-permute-done.57.recv_ref, bf16[1024,1024]{1,0:T(8,128)(2,1)} %copy-done.3, f32[1,1024]{1,0:T(1,128)} %copy-done.71, f32[1024,1024]{1,0:T(8,128)} %get-tuple-element.361.sum_ref), custom_call_target="tpu_custom_call" | custom-call | flops 1 | bytes 1 | tf_op jit(solution)/shard_map/pallas_call | solution.py:320
  441.8 4.4 collective-permute-done.59
  446.3 5.2 %collective-permute-done.60 = bf16[64,2048]{1,0:T(8,128)(2,1)S(1)} collective-permute-done((bf16[64,2048]{1,0:T(8,128)(2,1)S(1)}, bf16[64,2048]{1,0:T(8,128)(2,1)S(1)}, u32[]{:S(2)}, u32[]{:S(2)}) %collective-permute-start.60) | collective-permute-done | bytes 262176 | tf_op jit(solution)/shard_map/ppermute | solution.py:53
  (514 shorter events, 234.0 us)
Async XLA Ops:
  7.2 40.4 %all-gather.11.cloned.1.call-start = ((), (), s32[]{:S(2)}) async-start(), calls=%async_computation.10 | async-start | bytes 1392640 | tf_op jit(solution)/shard_map/all_gather | solution.py:61
  15.8 61.4 %all-gather.13.cloned.1.call-start = ((), (), s32[]{:S(2)}) async-start(), calls=%async_computation.11 | async-start | bytes 1310720 | tf_op jit(solution)/shard_map/all_gather | solution.py:61
  18.2 32.9 %collective-permute-start.11 = (bf16[1024,1024]{1,0:T(8,128)(2,1)}, bf16[1024,1024]{1,0:T(8,128)(2,1)}, u32[]{:S(2)}, u32[]{:S(2)}) collective-permute-start(bf16[1024,1024]{1,0:T(8,128)(2,1)} %bitcast.170), channel_id=1, source_target_pairs={{0,16},{16,0},{1,17},{17,1},{2,18},{18,2},{3,19},{19,3},{4,20},{20... | collective-permute-start | bytes 6291464 | tf_op jit(solution)/shard_map/ppermute | solution.py:49
  47.6 59.2 %all-gather.15.cloned.1.call-start = ((), (), s32[]{:S(2)}) async-start(), calls=%async_computation.12 | async-start | bytes 1310720 | tf_op jit(solution)/shard_map/all_gather | solution.py:61
  77.2 111.3 %all-gather.17.cloned.1.call-start = ((), (), s32[]{:S(2)}) async-start(), calls=%async_computation.13 | async-start | bytes 5242880 | tf_op jit(solution)/shard_map/all_gather | solution.py:61
  77.3 27.2 %collective-permute-start.12 = (bf16[4,64,2176]{2,1,0:T(8,128)(2,1)}, bf16[4,64,2176]{2,1,0:T(8,128)(2,1)S(1)}, u32[]{:S(2)}, u32[]{:S(2)}) collective-permute-start(bf16[4,64,2176]{2,1,0:T(8,128)(2,1)} %collective-permute-done.9.rest_1_), channel_id=1, source_target_pairs={{0,2},{2,0},{1,3},{3,1},{4,6},{6,4},{5,7},{7,5},{8,10},{10,8},{9,1... | collective-permute-start | bytes 3342344 | tf_op jit(solution)/shard_map/ppermute | solution.py:49
  106.8 127.7 %all-gather.19.cloned.1.call-start = ((), (), s32[]{:S(2)}) async-start(), calls=%async_computation.14 | async-start | bytes 2621440 | tf_op jit(solution)/shard_map/all_gather | solution.py:61
  107.0 27.2 %collective-permute-start.15 = (bf16[4,64,2048]{2,1,0:T(8,128)(2,1)}, bf16[4,64,2048]{2,1,0:T(8,128)(2,1)}, u32[]{:S(2)}, u32[]{:S(2)}) collective-permute-start(bf16[4,64,2048]{2,1,0:T(8,128)(2,1)} %bitcast.152), channel_id=1, source_target_pairs={{0,2},{2,0},{1,3},{3,1},{4,6},{6,4},{5,7},{7,5},{8,10},{10,8},{9,1... | collective-permute-start | bytes 3145736 | tf_op jit(solution)/shard_map/ppermute | solution.py:49
  140.5 37.9 %collective-permute-start.20 = (bf16[2,128,1024]{2,1,0:T(8,128)(2,1)}, bf16[2,128,1024]{2,1,0:T(8,128)(2,1)}, u32[]{:S(2)}, u32[]{:S(2)}) collective-permute-start(bf16[2,128,1024]{2,1,0:T(8,128)(2,1)} %slice.128), channel_id=1, source_target_pairs={{0,2},{2,0},{1,3},{3,1},{4,6},{6,4},{5,7},{7,5},{8,10},{10,8},{9,1... | collective-permute-start | bytes 1572872 | tf_op jit(solution)/shard_map/ppermute | solution.py:49
  161.9 235.1 %reduce-scatter.8.cloned.1.call-start = ((), (), s32[]{:S(2)}) async-start(), calls=%async_computation.6 | async-start | bytes 2621440 | tf_op jit(solution)/shard_map/reduce_scatter | solution.py:65
  206.2 28.3 %collective-permute-start.29 = (bf16[128,1024]{1,0:T(8,128)(2,1)S(1)}, bf16[128,1024]{1,0:T(8,128)(2,1)S(1)}, u32[]{:S(2)}, u32[]{:S(2)}) collective-permute-start(bf16[128,1024]{1,0:T(8,128)(2,1)S(1)} %copy-done.45), channel_id=1, source_target_pairs={{0,2},{1,3},{2,0},{3,1},{4,6},{5,7},{6,4},{7,5},{8,10},{9,11},{10,... | collective-permute-start | bytes 786440 | tf_op jit(solution)/shard_map/ppermute | solution.py:53
  207.7 26.8 %collective-permute-start.30 = (bf16[128,1024]{1,0:T(8,128)(2,1)S(1)}, bf16[128,1024]{1,0:T(8,128)(2,1)S(1)}, u32[]{:S(2)}, u32[]{:S(2)}) collective-permute-start(bf16[128,1024]{1,0:T(8,128)(2,1)S(1)} %copy-done.45), channel_id=1, source_target_pairs={{0,3},{1,2},{2,1},{3,0},{4,7},{5,6},{6,5},{7,4},{8,11},{9,10},{10,... | collective-permute-start | bytes 786440 | tf_op jit(solution)/shard_map/ppermute | solution.py:53
  208.6 26.7 %collective-permute-start.25 = (bf16[128,1024]{1,0:T(8,128)(2,1)S(1)}, bf16[128,1024]{1,0:T(8,128)(2,1)S(1)}, u32[]{:S(2)}, u32[]{:S(2)}) collective-permute-start(bf16[128,1024]{1,0:T(8,128)(2,1)S(1)} %shard_map.208.m0), channel_id=1, source_target_pairs={{0,1},{1,0},{2,3},{3,2},{4,5},{5,4},{6,7},{7,6},{8,9},{9,8},{10,11... | collective-permute-start | bytes 786440 | tf_op jit(solution)/shard_map/ppermute | solution.py:53
  248.6 158.2 %reduce-scatter.6.cloned.1.call-start = ((), (), s32[]{:S(2)}) async-start(), calls=%async_computation.5 | async-start | bytes 5242880 | tf_op jit(solution)/shard_map/reduce_scatter | solution.py:65
  294.1 137.8 %reduce-scatter.10.cloned.1.call-start = ((), (), s32[]{:S(2)}) async-start(), calls=%async_computation.7 | async-start | bytes 1310720 | tf_op jit(solution)/shard_map/reduce_scatter | solution.py:65
  324.4 39.2 %collective-permute-start.45 = (bf16[2,128,1024]{2,1,0:T(8,128)(2,1)}, bf16[2,128,1024]{2,1,0:T(8,128)(2,1)}, u32[]{:S(2)}, u32[]{:S(2)}) collective-permute-start(bf16[2,128,1024]{2,1,0:T(8,128)(2,1)} %add_convert_fusion.4), channel_id=1, source_target_pairs={{0,1},{1,0},{2,3},{3,2},{4,5},{5,4},{6,7},{7,6},{8,9},{9,8},{10,11... | collective-permute-start | bytes 1572872 | tf_op jit(solution)/shard_map/ppermute | solution.py:49
  327.1 37.8 %collective-permute-start.44 = (bf16[2,128,1024]{2,1,0:T(8,128)(2,1)}, bf16[2,128,1024]{2,1,0:T(8,128)(2,1)}, u32[]{:S(2)}, u32[]{:S(2)}) collective-permute-start(bf16[2,128,1024]{2,1,0:T(8,128)(2,1)} %add_convert_fusion.5), channel_id=1, source_target_pairs={{0,2},{2,0},{1,3},{3,1},{4,6},{6,4},{5,7},{7,5},{8,10},{10,8},{9,1... | collective-permute-start | bytes 1572872 | tf_op jit(solution)/shard_map/ppermute | solution.py:49
  328.4 36.5 %collective-permute-start.42 = (bf16[2,64,2048]{2,1,0:T(8,128)(2,1)}, bf16[2,64,2048]{2,1,0:T(8,128)(2,1)}, u32[]{:S(2)}, u32[]{:S(2)}) collective-permute-start(bf16[2,64,2048]{2,1,0:T(8,128)(2,1)} %get-tuple-element.313), channel_id=1, source_target_pairs={{0,1},{1,0},{2,3},{3,2},{4,5},{5,4},{6,7},{7,6},{8,9},{9,8},{10,11... | collective-permute-start | bytes 1572872 | tf_op jit(solution)/shard_map/ppermute | solution.py:49
  329.9 35.0 %collective-permute-start.43 = (bf16[2,64,2048]{2,1,0:T(8,128)(2,1)}, bf16[2,64,2048]{2,1,0:T(8,128)(2,1)}, u32[]{:S(2)}, u32[]{:S(2)}) collective-permute-start(bf16[2,64,2048]{2,1,0:T(8,128)(2,1)} %get-tuple-element.314), channel_id=1, source_target_pairs={{0,2},{2,0},{1,3},{3,1},{4,6},{6,4},{5,7},{7,5},{8,10},{10,8},{9,1... | collective-permute-start | bytes 1572872 | tf_op jit(solution)/shard_map/ppermute | solution.py:49
  331.5 57.5 %collective-permute-start.50 = (bf16[2,64,2048]{2,1,0:T(8,128)(2,1)}, bf16[2,64,2048]{2,1,0:T(8,128)(2,1)S(1)}, u32[]{:S(2)}, u32[]{:S(2)}) collective-permute-start(bf16[2,64,2048]{2,1,0:T(8,128)(2,1)} %get-tuple-element.349), channel_id=1, source_target_pairs={{0,1},{1,0},{2,3},{3,2},{4,5},{5,4},{6,7},{7,6},{8,9},{9,8},{10,11... | collective-permute-start | bytes 1572872 | tf_op jit(solution)/shard_map/ppermute | solution.py:49
  370.9 69.8 %reduce-scatter.14.cloned.1.call-start = ((), (), s32[]{:S(2)}) async-start(), calls=%async_computation.9 | async-start | bytes 1310720 | tf_op jit(solution)/shard_map/reduce_scatter | solution.py:65
  391.7 33.9 %collective-permute-start.55 = (bf16[2,64,2176]{2,1,0:T(8,128)(2,1)}, bf16[2,64,2176]{2,1,0:T(8,128)(2,1)S(1)}, u32[]{:S(2)}, u32[]{:S(2)}) collective-permute-start(bf16[2,64,2176]{2,1,0:T(8,128)(2,1)} %get-tuple-element.358), channel_id=1, source_target_pairs={{0,1},{1,0},{2,3},{3,2},{4,5},{5,4},{6,7},{7,6},{8,9},{9,8},{10,11... | collective-permute-start | bytes 1671176 | tf_op jit(solution)/shard_map/ppermute | solution.py:49
  393.0 32.6 %collective-permute-start.56 = (bf16[2,64,2176]{2,1,0:T(8,128)(2,1)}, bf16[2,64,2176]{2,1,0:T(8,128)(2,1)S(1)}, u32[]{:S(2)}, u32[]{:S(2)}) collective-permute-start(bf16[2,64,2176]{2,1,0:T(8,128)(2,1)} %get-tuple-element.359), channel_id=1, source_target_pairs={{0,2},{2,0},{1,3},{3,1},{4,6},{6,4},{5,7},{7,5},{8,10},{10,8},{9,1... | collective-permute-start | bytes 1671176 | tf_op jit(solution)/shard_map/ppermute | solution.py:49
  397.0 62.2 %reduce-scatter.12.cloned.1.call-start = ((), (), s32[]{:S(2)}) async-start(), calls=%async_computation.8 | async-start | bytes 1392640 | tf_op jit(solution)/shard_map/reduce_scatter | solution.py:65
  (152 other events, 1370.2 us)
Sparse Core Ops, SparseCore 0:
  15.9 31.6 all-gather.10
  49.7 27.3 all-gather.12
  79.3 27.4 all-gather.14
  108.2 80.2 all-gather.16
  189.9 44.4 all-gather.18
  248.7 42.4 reduce-scatter.7
  294.2 75.4 reduce-scatter.5
  372.6 27.6 reduce-scatter.9
  403.2 25.8 reduce-scatter.13
  432.8 26.2 reduce-scatter.11

commit v5 on v4

--- a/solution.py
+++ b/solution.py
@@ -837,7 +837,7 @@
         send_ref[...] = e
 
 
-def routed_grads_kernel(g_ref, d_ref, m_ref, du_ref, out_ref, done_ref):
+def routed_grads_kernel(g_ref, d_ref, m_ref, du_ref, _, out_ref, done_ref):
     depth, all_rows, hidden = out_ref.shape
     rows = D // depth
     units = (all_rows - rows) // 2
@@ -850,13 +850,14 @@
     done_ref[...] = jnp.zeros_like(done_ref)
 
 
-def add_parts_kernel(a_ref, b_ref, _, *outs):
-    for j, out in enumerate(outs):
+def add_parts_kernel(a_ref, b_ref, *outs):
+    outs[-1][...] = jnp.zeros_like(outs[-1])
+    for j, out in enumerate(outs[:-1]):
         out[...] = (a_ref[j].astype(f32) + b_ref[j].astype(f32)).astype(bf16)
 
 
 def add_kernel(*refs):
-    refs[-1][...] = sum(ref[...].astype(f32) for ref in refs[:-2]).astype(bf16)
+    refs[-1][...] = sum(ref[...].astype(f32) for ref in refs[:4]).astype(bf16)
 
 
 def routed_back_kernel(count, core_ref, *refs):
@@ -1139,21 +1140,21 @@
     )
     plus = lambda *terms: sum(t.astype(f32) for t in terms).astype(bf16)
     others = swap(send, "section")
+    *summed, added = whole(
+        add_parts_kernel, [((chosen_rows, D), bf16)] * 4 + [mark], [], [keep, others]
+    )
     gw_m1, grads_done = whole(
         routed_grads_kernel,
         [((depth, mlp_rows, hidden), bf16), mark],
         [],
-        [g1, de_rows, m_rows, du1],
+        [g1, de_rows, m_rows, du1, added],
     )
     plus = lambda *terms: sum(t.astype(f32) for t in terms).astype(bf16)
     r_m1 = reduce_z(gw_m1)
-    summed = whole(
-        add_parts_kernel, [((chosen_rows, D), bf16)] * 4, [], [keep, others, grads_done]
-    )
     terms = [summed[0]] + [to_plane(summed[j], j) for j in (1, 2, 3)]
     pre_d = down_grad(me, depth, (0, 1, 2, 3), g0, cot_other)
     g_rows, slope_rows, rows_done = take_rows(picked, pre_d[0], g0, slope0)
-    (total,) = whole(add_kernel, [((chosen_rows, D), bf16)], [], [*terms, rows_done])
+    (total,) = whole(add_kernel, [((chosen_rows, D), bf16)], [], [*terms, rows_done, grads_done])
     crossed = swap(total, "section")
 
     delta, grad_logit, dh1, dz1, gg_mlp1, dqkv1, da_part = whole(
@@ -1297,28 +1298,27 @@
     near_q = send_near(near(attn0, diag_q))
     far_q, boundary_out = fence(far_q, boundary_out)
     part = lambda v, j: lax.dynamic_index_in_dim(v, me ^ j, axis=0, keepdims=False)
+    def joined(grad0, grad1):
+        keep = jnp.where(first, grad0, grad1)
+        recv = swap(jnp.where(first, grad1, grad0), "section")
+        return jnp.where(first, keep, recv).astype(f32), jnp.where(first, recv, keep).astype(f32)
+
+    low = 4 * rows + half_units
+    r_d1 = jnp.concatenate([r_m1[4 * rows : low], r_m1[low:]], axis=1)
+    low, high = joined(r_d0, r_d1)
+    out_down = jnp.concatenate([low, high], axis=0)[None]
     (sum_q,) = whole(
         halves_kernel,
         [((depth, rows, width + LANES), bf16)],
         [],
         parts(attn0, near_q, far_q),
     )
-    sum_q, r_a1, r_m1, r_d0 = fence(sum_q, r_a1, r_m1, r_d0)
+    sum_q, r_a1, r_m1, out_down = fence(sum_q, r_a1, r_m1, out_down)
     r_a0 = reduce_z(sum_q)
     r_a1 = plus(part(r_a1, 0), *[to_plane(part(r_a1, j), j) for j in (1, 2, 3)])
     up = r_m1[: 4 * rows].reshape(4, rows, hidden)
     up = [part(up, 0)] + [to_plane(part(up, j), j) for j in (1, 2, 3)]
     (r_u1,) = whole(order_columns_kernel, [((rows, 2 * D), bf16)], [me], up)
-    low = 4 * rows + half_units
-    r_d1 = jnp.concatenate([r_m1[4 * rows : low], r_m1[low:]], axis=1)
-
-    def joined(grad0, grad1):
-        keep = jnp.where(first, grad0, grad1)
-        recv = swap(jnp.where(first, grad1, grad0), "section")
-        return jnp.where(first, keep, recv).astype(f32), jnp.where(first, recv, keep).astype(f32)
-
-    low, high = joined(r_d0, r_d1)
-    out_down = jnp.concatenate([low, high], axis=0)[None]
     low, high = joined(r_u0, r_u1)
     cut = lambda v: v.reshape(rows, 4, depth, half_units).transpose(0, 2, 1, 3)
     out_up = jnp.stack([cut(low), cut(high)], axis=3).reshape(1, rows, FF)

time: 480 us -> 478 us (level)
  waiting for transfers between devices: 120 us -> 127 us
    reduce_scatter x5, waiting for transfers between devices: 2.07 us -> 10.1 us  [reduce_z(): return lax.psum_scatter(part, 'z', scatter_dimension=0, tiled=False)]
    unnamed x201 -> x207, local copies, waits for them, and re-layouts: 43.5 us -> 39.2 us
  transfers between devices with their start and end apart: 78 -> 78, of which waited for: 29 -> 32; matrix products, arithmetic and copies ran while one was open for 12% -> 12% of each run, Pallas kernels for 34% -> 33%
where the time goes in v5:
time: 478 us; the launch traced here: 472 us
  Pallas kernels  163 us (34%)
  waiting for transfers between devices  127 us (27%)
  starting transfers between devices  64.4 us (13%)
  local copies, waits for them, and re-layouts  59.3 us (12%)
  other arithmetic  39.9 us (8%)
  between operations  15.9 us (3%)
    pallas_call x11, Pallas kernels, tiled_call(): pl.pallas_call(kernel, grid=(steps,), out_shape=[jax.ShapeDtypeStruct(sha...  93 us
    ppermute x47, waiting for transfers between devices, swap(): return lax.ppermute(v, axis, [(0, 1), (1, 0)])  83.5 us
    unnamed x207, local copies, waits for them, and re-layouts  39.2 us
    ppermute x47, starting transfers between devices, swap(): return lax.ppermute(v, axis, [(0, 1), (1, 0)])  35.8 us
    pallas_call x18, Pallas kernels, whole(): pl.pallas_call(kernel, out_shape=[jax.ShapeDtypeStruct(shape, dtype) for...  29.7 us
    ppermute x21, starting transfers between devices, to_plane(): return lax.ppermute(v, ('y', 'x'), [(i, i ^ j) for i in range(4)])  27.8 us
    ppermute x21, waiting for transfers between devices, to_plane(): return lax.ppermute(v, ('y', 'x'), [(i, i ^ j) for i in range(4)])  23.7 us
    pallas_call x2, Pallas kernels, attention_call(): pl.pallas_call(functools.partial(kernel, LANES, pairs, length), grid=(cou...  22.6 us
  transfers between devices with their start and end apart: 78, of which 32 were waited for; matrix products, arithmetic and copies ran while one was open for 12% of the time, Pallas kernels for 33%

profile of v5, /device:TPU:0, one launch (start us, length us, event | category | flops | bytes accessed | tf_op | source)
XLA Modules:
  0.0 471.5 jit_solution(5315195581372517028)
XLA Ops:
  29.6 5.7 %collective-permute-done.6.u2 = bf16[64,512]{1,0:T(8,128)(2,1)S(1)} collective-permute-done((bf16[64,512]{1,0:T(8,128)(2,1)S(1)}, bf16[64,512]{1,0:T(8,128)(2,1)S(1)}, u32[]{:S(2)}, u32[]{:S(2)}) %collective-permute-start.6) | collective-permute-done | bytes 65568 | tf_op jit(solution)/shard_map/ppermute | solution.py:53
  55.0 19.1 %collective-permute-done.10.rest_2_ = bf16[4,64,2176]{2,1,0:T(8,128)(2,1)} collective-permute-done((bf16[4,64,2176]{2,1,0:T(8,128)(2,1)}, bf16[4,64,2176]{2,1,0:T(8,128)(2,1)}, u32[]{:S(2)}, u32[]{:S(2)}) %collective-permute-start.10) | collective-permute-done | bytes 1114144 | tf_op jit(solution)/shard_map/ppermute | solution.py:49
  80.3 23.2 %collective-permute-done.13.rest_1_ = bf16[4,64,2048]{2,1,0:T(8,128)(2,1)S(1)} collective-permute-done((bf16[4,64,2048]{2,1,0:T(8,128)(2,1)}, bf16[4,64,2048]{2,1,0:T(8,128)(2,1)S(1)}, u32[]{:S(2)}, u32[]{:S(2)}) %collective-permute-start.13) | collective-permute-done | bytes 1048608 | tf_op jit(solution)/shard_map/ppermute | solution.py:49
  117.4 5.1 %shard_map.199 = (bf16[4,4,64,1536]{3,2,1,0:T(8,128)(2,1)S(1)}, bf16[1024,1024]{1,0:T(8,128)(2,1)S(1)}, bf16[1024,1536]{1,0:T(8,128)(2,1)S(1)}) custom-call(s32[1]{0:T(128)} %bitcast.me_ref, bf16[1024,1024]{1,0:T(8,128)(2,1)S(1)} %get-tuple-element.207.x_ref, f32[1,1024]{1,0:T(1,128)S(1)} %get-tuple-element.507.gain_ref, bf16[4,64,2176]{2,1,0:T(8,128)(2,1)S(1)} %bitcast.154, ...), custom_call_target="tpu_custom_call" | custom-call | flops 1 | bytes 1 | tf_op jit(solution)/shard_map/pallas_call | solution.py:302
  127.5 5.7 %shard_map.200 = (bf16[1024,512]{1,0:T(8,128)(2,1)S(1)}, bf16[1024,1024]{1,0:T(8,128)(2,1)S(1)}) custom-call(bf16[1024,1536]{1,0:T(8,128)(2,1)S(1)} %get-tuple-element.220.qkv_ref, s32[2,512,1]{2,1,0:T(8,128)S(1)} %copy-done.14, s32[2,1,512]{2,1,0:T(1,128)S(1)} %copy-done.68, bf16[512,1024]{1,0:T(8,128)(2,1)S(1)} %pad_maximum_fusion.w_ref), custom_call_target="tpu_custom_call" | custom-call | flops 1 | bytes 1 | tf_op jit(solution)/shard_map/pallas_call | solution.py:229
  142.1 6.3 %shard_map.201 = (f32[1024,1024]{1,0:T(8,128)}, bf16[1024,1024]{1,0:T(8,128)(2,1)}) custom-call(bf16[1024,1024]{1,0:T(8,128)(2,1)} %copy-done.3, bf16[1024,1024]{1,0:T(8,128)(2,1)} %copy-done.32, bf16[1024,1024]{1,0:T(8,128)(2,1)} %collective-permute-done.17.recv_ref, f32[1,1024]{1,0:T(1,128)} %get-tuple-element.506.gain_ref), custom_call_target="tpu_custom_call" | custom-call | flops 1 | bytes 1 | tf_op jit(solution)/shard_map/pallas_call | solution.py:320
  148.3 12.7 %collective-permute-done.19.rest_2_ = bf16[4,128,1024]{2,1,0:T(8,128)(2,1)S(1)} collective-permute-done((bf16[4,128,1024]{2,1,0:T(8,128)(2,1)}, bf16[4,128,1024]{2,1,0:T(8,128)(2,1)S(1)}, u32[]{:S(2)}, u32[]{:S(2)}) %collective-permute-start.19) | collective-permute-done | bytes 1048608 | tf_op jit(solution)/shard_map/ppermute | solution.py:49
  167.1 11.2 %shard_map.203 = (bf16[1024,2048]{1,0:T(8,128)(2,1)}, bf16[1024,2048]{1,0:T(8,128)(2,1)}) custom-call(bf16[1024,1024]{1,0:T(8,128)(2,1)} %get-tuple-element.232.m_ref, bf16[1024,2048]{1,0:T(8,128)(2,1)} %bitcast.142, f32[1,2048]{1,0:T(1,128)} %reshape.181.b_ref), custom_call_target="tpu_custom_call" | custom-call | flops 1 | bytes 1 | tf_op jit(solution)/shard_map/pallas_call | solution.py:320
  181.7 5.0 %shard_map.205 = (bf16[1024,1024]{1,0:T(8,128)(2,1)S(1)}, f32[8,128]{1,0:T(8,128)S(1)}) custom-call(bf16[1024,2048]{1,0:T(8,128)(2,1)S(1)} %copy-done.5, bf16[2048,1024]{1,0:T(8,128)(2,1)S(1)} %bitcast.145), custom_call_target="tpu_custom_call" | custom-call | flops 1 | bytes 1 | tf_op jit(solution)/shard_map/pallas_call | solution.py:320
  191.8 6.2 %shard_map.206 = (bf16[1024,1024]{1,0:T(8,128)(2,1)}, bf16[128,1024]{1,0:T(8,128)(2,1)}, bf16[128,1024]{1,0:T(8,128)(2,1)}, f32[128,1]{1,0:T(8,128)}, bf16[128,1...) custom-call(f32[1024,1024]{1,0:T(8,128)} %get-tuple-element.229.h_ref, bf16[1024,1024]{1,0:T(8,128)(2,1)} %copy-done.33, ...), custom_call_target="tpu_custom_call" | custom-call | flops 1 | bytes 1 | tf_op jit(solution)/shard_map/pallas_call | solution.py:320
  218.1 12.8 %shard_map.209 = (bf16[1024,2048]{1,0:T(8,128)(2,1)S(1)}, bf16[1024,1024]{1,0:T(8,128)(2,1)S(1)}, f32[8,128]{1,0:T(8,128)S(1)}) custom-call(bf16[1024,1024]{1,0:T(8,128)(2,1)S(1)} %copy-done.8, bf16[2048,1024]{1,0:T(8,128)(2,1)S(1)} %bitcast.147, bf16[1024,2048]{1,0:T(8,128)(2,1)S(1)} %copy-done.10, bf16[1024,2048]{1,0:T(8,128)(2,1)} %bitcast.143), custom_call_target="tpu_custom_call" | custom-call | flops 1 | bytes 1 | tf_op jit(solution)/shard_map/pallas_call | solution.py:320
  251.7 9.9 %shard_map.212 = (bf16[4,128,1024]{2,1,0:T(8,128)(2,1)}, bf16[4,128,1024]{2,1,0:T(8,128)(2,1)}, bf16[4,128,1024]{2,1,0:T(8,128)(2,1)}, bf16[4,128,1024]{2,1,0:T(8,128)(2,1)}) custom-call(s32[1]{0:T(128)} %bitcast.me_ref, bf16[1024,2048]{1,0:T(8,128)(2,1)} %get-tuple-element.240.g_ref.refs_1_, bf16[1024,1024]{1,0:T(8,128)(2,1)} %get-tuple-element.258.d_ref), custom_call_target="tpu_custom_call" | custom-call | flops 1 | bytes 1 | tf_op jit(solution)/shard_map/pallas_call | solution.py:513
  261.7 5.3 %shard_map.213 = (bf16[128,2048]{1,0:T(8,128)(2,1)}, bf16[128,2048]{1,0:T(8,128)(2,1)}, f32[8,128]{1,0:T(8,128)}) custom-call(s32[2,64,1]{2,1,0:T(8,128)} %copy.183.picked_ref, bf16[4,128,1024]{2,1,0:T(8,128)(2,1)} %get-tuple-element.267.refs_0_, bf16[1024,2048]{1,0:T(8,128)(2,1)} %get-tuple-element.240.g_ref.refs_1_, ...), custom_call_target="tpu_custom_call" | custom-call | flops 1 | bytes 1 | tf_op jit(solution)/shard_map/pallas_call | solution.py:320
  284.4 5.0 %shard_map.219._ = bf16[4,4,64,2048]{3,2,1,0:T(8,128)(2,1)} custom-call(s32[1]{0:T(128)} %bitcast.me_ref, bf16[128,1024]{1,0:T(8,128)(2,1)} %get-tuple-element.246.a_ref, bf16[128,1536]{1,0:T(8,128)(2,1)} %copy-done.60, bf16[1024,512]{1,0:T(8,128)(2,1)} %pad_maximum_fusion.2.refs_0_, bf16[2,128,1024]{2,1,0:T(8,128)(2,1)} %copy-done.34), custom_call_target="tpu_custom_call" | custom-call | flops 1 | bytes 1 | tf_op jit(solution)/shard_map/pallas_call | solution.py:320
  293.6 16.1 %shard_map.220 = (bf16[2,64,2048]{2,1,0:T(8,128)(2,1)}, bf16[2,64,2048]{2,1,0:T(8,128)(2,1)}, bf16[2,64,2048]{2,1,0:T(8,128)(2,1)}, bf16[2,64,2048]{2,1,0:T(8,12...) custom-call(s32[1]{0:T(128)} %bitcast.me_ref, ...), custom_call_target="tpu_custom_call" | custom-call | flops 1 | bytes 1 | tf_op jit(solution)/shard_map/pallas_call | solution.py:320
  309.7 5.4 %collective-permute-done.39.refs_2_ = bf16[2,128,1024]{2,1,0:T(8,128)(2,1)S(1)} collective-permute-done((bf16[2,128,1024]{2,1,0:T(8,128)(2,1)}, bf16[2,128,1024]{2,1,0:T(8,128)(2,1)S(1)}, u32[]{:S(2)}, u32[]{:S(2)}) %collective-permute-start.39) | collective-permute-done | bytes 524320 | tf_op jit(solution)/shard_map/ppermute | solution.py:49
  328.5 9.7 %shard_map.221 = (bf16[1024,1024]{1,0:T(8,128)(2,1)}, f32[1024,1024]{1,0:T(8,128)}, bf16[1024,512]{1,0:T(8,128)(2,1)}, f32[1,1024]{1,0:T(1,128)}, f32[1,1024]{1,0:T(1,128)}) custom-call(bf16[1024,1024]{1,0:T(8,128)(2,1)} %get-tuple-element.321.part_ref, bf16[1024,1024]{1,0:T(8,128)(2,1)} %collective-permute-done.46.recv_ref, ...), custom_call_target="tpu_custom_call" | custom-call | flops 1 | bytes 1 | tf_op jit(solution)/shard_map/pallas_call | solution.py:320
  341.4 16.9 %shard_map.222 = (bf16[1024,1536]{1,0:T(8,128)(2,1)S(1)}, bf16[1024,1024]{1,0:T(8,128)(2,1)}, f32[1,1024]{1,0:T(1,128)S(1)}) custom-call(bf16[1024,1536]{1,0:T(8,128)(2,1)S(1)} %copy-done.12, s32[2,512,1]{2,1,0:T(8,128)S(1)} %copy-done.15, s32[2,1,512]{2,1,0:T(1,128)S(1)} %copy-done.68, bf16[1024,512]{1,0:T(8,128)(2,1)S(1)} %copy-done.43, ...), custom_call_target="tpu_custom_call" | custom-call | flops 1 | bytes 1 | tf_op jit(solution)/shard_map/pallas_call | solution.py:229
  374.4 8.7 %shard_map.223 = (bf16[2,64,2176]{2,1,0:T(8,128)(2,1)}, bf16[2,64,2176]{2,1,0:T(8,128)(2,1)}, bf16[2,64,2176]{2,1,0:T(8,128)(2,1)}, bf16[2,64,2176]{2,1,0:T(8,12...) custom-call(s32[1]{0:T(128)} %bitcast.me_ref, ...), custom_call_target="tpu_custom_call" | custom-call | flops 1 | bytes 1 | tf_op jit(solution)/shard_map/pallas_call | solution.py:320
  392.4 6.7 %shard_map.224 = bf16[1024,1024]{1,0:T(8,128)(2,1)} custom-call(bf16[1024,1024]{1,0:T(8,128)(2,1)} %get-tuple-element.362.part_ref, bf16[1024,1024]{1,0:T(8,128)(2,1)} %collective-permute-done.57.recv_ref, bf16[1024,1024]{1,0:T(8,128)(2,1)} %copy-done.3, f32[1,1024]{1,0:T(1,128)} %copy-done.69, f32[1024,1024]{1,0:T(8,128)} %get-tuple-element.363.sum_ref), custom_call_target="tpu_custom_call" | custom-call | flops 1 | bytes 1 | tf_op jit(solution)/shard_map/pallas_call | solution.py:320
  413.7 9.5 %collective-permute-done.58.refs_4_ = bf16[2,64,2176]{2,1,0:T(8,128)(2,1)S(1)} collective-permute-done((bf16[2,64,2176]{2,1,0:T(8,128)(2,1)S(1)}, bf16[2,64,2176]{2,1,0:T(8,128)(2,1)S(1)}, u32[]{:S(2)}, u32[]{:S(2)}) %collective-permute-start.58) | collective-permute-done | bytes 557088 | tf_op jit(solution)/shard_map/ppermute | solution.py:49
  434.2 4.4 collective-permute-done.60
  438.7 4.5 collective-permute-done.62
  447.1 10.0 %reduce-scatter.12.cloned.1.call-done = bf16[1,64,2176]{2,1,0:T(8,128)(2,1)} async-done(((bf16[4,64,2176]{2,1,0:T(8,128)(2,1)}), bf16[1,64,2176]{2,1,0:T(8,128)(2,1)}) %reduce-scatter.12.cloned.1.call-update) | async-done | bytes 278544 | tf_op jit(solution)/shard_map/reduce_scatter | solution.py:65
  (520 shorter events, 230.4 us)
Async XLA Ops:
  7.2 40.4 %all-gather.11.cloned.1.call-start = ((), (), s32[]{:S(2)}) async-start(), calls=%async_computation.10 | async-start | bytes 1392640 | tf_op jit(solution)/shard_map/all_gather | solution.py:61
  15.8 61.4 %all-gather.13.cloned.1.call-start = ((), (), s32[]{:S(2)}) async-start(), calls=%async_computation.11 | async-start | bytes 1310720 | tf_op jit(solution)/shard_map/all_gather | solution.py:61
  18.2 32.9 %collective-permute-start.11 = (bf16[1024,1024]{1,0:T(8,128)(2,1)}, bf16[1024,1024]{1,0:T(8,128)(2,1)}, u32[]{:S(2)}, u32[]{:S(2)}) collective-permute-start(bf16[1024,1024]{1,0:T(8,128)(2,1)} %bitcast.176), channel_id=1, source_target_pairs={{0,16},{16,0},{1,17},{17,1},{2,18},{18,2},{3,19},{19,3},{4,20},{20... | collective-permute-start | bytes 6291464 | tf_op jit(solution)/shard_map/ppermute | solution.py:49
  47.6 59.2 %all-gather.15.cloned.1.call-start = ((), (), s32[]{:S(2)}) async-start(), calls=%async_computation.12 | async-start | bytes 1310720 | tf_op jit(solution)/shard_map/all_gather | solution.py:61
  47.7 26.5 %collective-permute-start.10 = (bf16[4,64,2176]{2,1,0:T(8,128)(2,1)}, bf16[4,64,2176]{2,1,0:T(8,128)(2,1)}, u32[]{:S(2)}, u32[]{:S(2)}) collective-permute-start(bf16[4,64,2176]{2,1,0:T(8,128)(2,1)} %bitcast.151), channel_id=1, source_target_pairs={{0,2},{2,0},{1,3},{3,1},{4,6},{6,4},{5,7},{7,5},{8,10},{10,8},{9,1... | collective-permute-start | bytes 3342344 | tf_op jit(solution)/shard_map/ppermute | solution.py:49
  77.2 111.3 %all-gather.17.cloned.1.call-start = ((), (), s32[]{:S(2)}) async-start(), calls=%async_computation.13 | async-start | bytes 5242880 | tf_op jit(solution)/shard_map/all_gather | solution.py:61
  77.2 27.2 %collective-permute-start.12 = (bf16[4,64,2176]{2,1,0:T(8,128)(2,1)}, bf16[4,64,2176]{2,1,0:T(8,128)(2,1)S(1)}, u32[]{:S(2)}, u32[]{:S(2)}) collective-permute-start(bf16[4,64,2176]{2,1,0:T(8,128)(2,1)} %collective-permute-done.9.rest_1_), channel_id=1, source_target_pairs={{0,2},{2,0},{1,3},{3,1},{4,6},{6,4},{5,7},{7,5},{8,10},{10,8},{9,1... | collective-permute-start | bytes 3342344 | tf_op jit(solution)/shard_map/ppermute | solution.py:49
  106.8 127.6 %all-gather.19.cloned.1.call-start = ((), (), s32[]{:S(2)}) async-start(), calls=%async_computation.14 | async-start | bytes 2621440 | tf_op jit(solution)/shard_map/all_gather | solution.py:61
  107.0 27.1 %collective-permute-start.15 = (bf16[4,64,2048]{2,1,0:T(8,128)(2,1)}, bf16[4,64,2048]{2,1,0:T(8,128)(2,1)}, u32[]{:S(2)}, u32[]{:S(2)}) collective-permute-start(bf16[4,64,2048]{2,1,0:T(8,128)(2,1)} %bitcast.158), channel_id=1, source_target_pairs={{0,2},{2,0},{1,3},{3,1},{4,6},{6,4},{5,7},{7,5},{8,10},{10,8},{9,1... | collective-permute-start | bytes 3145736 | tf_op jit(solution)/shard_map/ppermute | solution.py:49
  134.8 26.2 %collective-permute-start.19 = (bf16[4,128,1024]{2,1,0:T(8,128)(2,1)}, bf16[4,128,1024]{2,1,0:T(8,128)(2,1)S(1)}, u32[]{:S(2)}, u32[]{:S(2)}) collective-permute-start(bf16[4,128,1024]{2,1,0:T(8,128)(2,1)} %bitcast.25.rest_0_), channel_id=1, source_target_pairs={{0,2},{2,0},{1,3},{3,1},{4,6},{6,4},{5,7},{7,5},{8,10},{10,8},{9,1... | collective-permute-start | bytes 3145736 | tf_op jit(solution)/shard_map/ppermute | solution.py:49
  140.5 37.8 %collective-permute-start.20 = (bf16[2,128,1024]{2,1,0:T(8,128)(2,1)}, bf16[2,128,1024]{2,1,0:T(8,128)(2,1)}, u32[]{:S(2)}, u32[]{:S(2)}) collective-permute-start(bf16[2,128,1024]{2,1,0:T(8,128)(2,1)} %slice.128), channel_id=1, source_target_pairs={{0,2},{2,0},{1,3},{3,1},{4,6},{6,4},{5,7},{7,5},{8,10},{10,8},{9,1... | collective-permute-start | bytes 1572872 | tf_op jit(solution)/shard_map/ppermute | solution.py:49
  161.9 237.2 %reduce-scatter.8.cloned.1.call-start = ((), (), s32[]{:S(2)}) async-start(), calls=%async_computation.6 | async-start | bytes 2621440 | tf_op jit(solution)/shard_map/reduce_scatter | solution.py:65
  206.8 27.6 %collective-permute-start.29 = (bf16[128,1024]{1,0:T(8,128)(2,1)S(1)}, bf16[128,1024]{1,0:T(8,128)(2,1)S(1)}, u32[]{:S(2)}, u32[]{:S(2)}) collective-permute-start(bf16[128,1024]{1,0:T(8,128)(2,1)S(1)} %copy-done.45), channel_id=1, source_target_pairs={{0,2},{1,3},{2,0},{3,1},{4,6},{5,7},{6,4},{7,5},{8,10},{9,11},{10,... | collective-permute-start | bytes 786440 | tf_op jit(solution)/shard_map/ppermute | solution.py:53
  207.3 27.1 %collective-permute-start.28 = (bf16[128,1024]{1,0:T(8,128)(2,1)S(1)}, bf16[128,1024]{1,0:T(8,128)(2,1)S(1)}, u32[]{:S(2)}, u32[]{:S(2)}) collective-permute-start(bf16[128,1024]{1,0:T(8,128)(2,1)S(1)} %copy-done.45), channel_id=1, source_target_pairs={{0,1},{1,0},{2,3},{3,2},{4,5},{5,4},{6,7},{7,6},{8,9},{9,8},{10,11... | collective-permute-start | bytes 786440 | tf_op jit(solution)/shard_map/ppermute | solution.py:53
  208.1 26.3 %collective-permute-start.27 = (bf16[128,1024]{1,0:T(8,128)(2,1)S(1)}, bf16[128,1024]{1,0:T(8,128)(2,1)S(1)}, u32[]{:S(2)}, u32[]{:S(2)}) collective-permute-start(bf16[128,1024]{1,0:T(8,128)(2,1)S(1)} %shard_map.208.m0), channel_id=1, source_target_pairs={{0,3},{1,2},{2,1},{3,0},{4,7},{5,6},{6,5},{7,4},{8,11},{9,10},{10,... | collective-permute-start | bytes 786440 | tf_op jit(solution)/shard_map/ppermute | solution.py:53
  248.1 152.6 %reduce-scatter.6.cloned.1.call-start = ((), (), s32[]{:S(2)}) async-start(), calls=%async_computation.5 | async-start | bytes 5242880 | tf_op jit(solution)/shard_map/reduce_scatter | solution.py:65
  289.4 112.2 %reduce-scatter.10.cloned.1.call-start = ((), (), s32[]{:S(2)}) async-start(), calls=%async_computation.7 | async-start | bytes 1310720 | tf_op jit(solution)/shard_map/reduce_scatter | solution.py:65
  318.6 39.8 %collective-permute-start.42 = (bf16[2,64,2048]{2,1,0:T(8,128)(2,1)}, bf16[2,64,2048]{2,1,0:T(8,128)(2,1)}, u32[]{:S(2)}, u32[]{:S(2)}) collective-permute-start(bf16[2,64,2048]{2,1,0:T(8,128)(2,1)} %get-tuple-element.315), channel_id=1, source_target_pairs={{0,1},{1,0},{2,3},{3,2},{4,5},{5,4},{6,7},{7,6},{8,9},{9,8},{10,11... | collective-permute-start | bytes 1572872 | tf_op jit(solution)/shard_map/ppermute | solution.py:49
  319.3 40.5 %collective-permute-start.43 = (bf16[2,64,2048]{2,1,0:T(8,128)(2,1)}, bf16[2,64,2048]{2,1,0:T(8,128)(2,1)}, u32[]{:S(2)}, u32[]{:S(2)}) collective-permute-start(bf16[2,64,2048]{2,1,0:T(8,128)(2,1)} %get-tuple-element.316), channel_id=1, source_target_pairs={{0,2},{2,0},{1,3},{3,1},{4,6},{6,4},{5,7},{7,5},{8,10},{10,8},{9,1... | collective-permute-start | bytes 1572872 | tf_op jit(solution)/shard_map/ppermute | solution.py:49
  322.6 37.1 %collective-permute-start.44 = (bf16[2,128,1024]{2,1,0:T(8,128)(2,1)}, bf16[2,128,1024]{2,1,0:T(8,128)(2,1)}, u32[]{:S(2)}, u32[]{:S(2)}) collective-permute-start(bf16[2,128,1024]{2,1,0:T(8,128)(2,1)} %add_convert_fusion.5), channel_id=1, source_target_pairs={{0,2},{2,0},{1,3},{3,1},{4,6},{6,4},{5,7},{7,5},{8,10},{10,8},{9,1... | collective-permute-start | bytes 1572872 | tf_op jit(solution)/shard_map/ppermute | solution.py:49
  325.4 34.4 %collective-permute-start.45 = (bf16[2,128,1024]{2,1,0:T(8,128)(2,1)}, bf16[2,128,1024]{2,1,0:T(8,128)(2,1)}, u32[]{:S(2)}, u32[]{:S(2)}) collective-permute-start(bf16[2,128,1024]{2,1,0:T(8,128)(2,1)} %add_convert_fusion.4), channel_id=1, source_target_pairs={{0,1},{1,0},{2,3},{3,2},{4,5},{5,4},{6,7},{7,6},{8,9},{9,8},{10,11... | collective-permute-start | bytes 1572872 | tf_op jit(solution)/shard_map/ppermute | solution.py:49
  327.7 55.5 %collective-permute-start.50 = (bf16[2,64,2048]{2,1,0:T(8,128)(2,1)}, bf16[2,64,2048]{2,1,0:T(8,128)(2,1)S(1)}, u32[]{:S(2)}, u32[]{:S(2)}) collective-permute-start(bf16[2,64,2048]{2,1,0:T(8,128)(2,1)} %get-tuple-element.351), channel_id=1, source_target_pairs={{0,1},{1,0},{2,3},{3,2},{4,5},{5,4},{6,7},{7,6},{8,9},{9,8},{10,11... | collective-permute-start | bytes 1572872 | tf_op jit(solution)/shard_map/ppermute | solution.py:49
  371.3 61.8 %reduce-scatter.14.cloned.1.call-start = ((), (), s32[]{:S(2)}) async-start(), calls=%async_computation.9 | async-start | bytes 1310720 | tf_op jit(solution)/shard_map/reduce_scatter | solution.py:65
  392.3 64.8 %reduce-scatter.12.cloned.1.call-start = ((), (), s32[]{:S(2)}) async-start(), calls=%async_computation.8 | async-start | bytes 1392640 | tf_op jit(solution)/shard_map/reduce_scatter | solution.py:65
  (155 other events, 1324.7 us)
Sparse Core Ops, SparseCore 0:
  15.9 31.6 all-gather.10
  49.7 27.3 all-gather.12
  79.3 27.4 all-gather.14
  108.2 80.2 all-gather.16
  189.9 44.4 all-gather.18
  248.2 42.5 reduce-scatter.7
  293.2 76.0 reduce-scatter.5
  371.7 27.6 reduce-scatter.9
  402.3 25.7 reduce-scatter.13
  430.3 26.8 reduce-scatter.11
